TPU v7x, 32 devices: a whole 2x2x4 slice. The times are simulated.
32 devices in a mesh: wide: 8 (over y, x, core), tp: 4 (over z).
Axes of the slice: x: 2, y: 2, z: 4, core: 2. Of those that a mesh axis runs over, the one named last changes fastest.
Arguments:
- hidden_in: bfloat16 [8, 1024, 1024], P('tp', 'wide'), may hold values from -6 to 6
- lengths: int32 [8], replicated, may hold values from 256 to 1024, as said below
- pre_gain: bfloat16 [1024], P('wide'), may hold values from 0.5 to 1.5
- pre_shift: bfloat16 [1024], P('wide'), may hold values from -1.796875 to 1.796875
- w_query: bfloat16 [1024, 1024], P('wide', 'tp'), may hold values from -0.1875 to 0.1875
- w_key: bfloat16 [1024, 1024], P('wide', 'tp'), may hold values from -0.1875 to 0.1875
- w_value: bfloat16 [1024, 1024], P('wide', 'tp'), may hold values from -0.1875 to 0.1875
- b_query: bfloat16 [16, 64], P('tp', 'wide'), may hold values from -1.796875 to 1.796875
- b_value: bfloat16 [16, 64], P('tp', 'wide'), may hold values from -1.796875 to 1.796875
- w_dense: bfloat16 [1024, 1024], P('tp', 'wide'), may hold values from -0.75 to 0.75
- b_dense: bfloat16 [1024], P('wide'), may hold values from -1.796875 to 1.796875
- mid_gain: bfloat16 [1024], P('wide'), may hold values from 0.5 to 1.5
- mid_shift: bfloat16 [1024], P('wide'), may hold values from -1.796875 to 1.796875
- w_up: bfloat16 [1024, 4096], P('wide', 'tp'), may hold values from -0.1875 to 0.1875
- b_up: bfloat16 [16, 256], P('tp', 'wide'), may hold values from -1.796875 to 1.796875
- w_down: bfloat16 [4096, 1024], P('tp', 'wide'), may hold values from -0.09375 to 0.09375
- b_down: bfloat16 [1024], P('wide'), may hold values from -1.796875 to 1.796875
- cotangent: bfloat16 [8, 1024, 1024], P('tp', 'wide'), may hold values from -6 to 6
Outputs:
- output: bfloat16 [8, 1024, 1024], P('tp', 'wide')
- grad_in: bfloat16 [8, 1024, 1024], P('tp', 'wide')
- grad_pre_gain: float32 [1024], P('wide')
- grad_pre_shift: float32 [1024], P('wide')
- grad_w_query: float32 [1024, 1024], P('wide', 'tp')
- grad_w_key: float32 [1024, 1024], P('wide', 'tp')
- grad_w_value: float32 [1024, 1024], P('wide', 'tp')
- grad_b_query: float32 [16, 64], P('tp', 'wide')
- grad_b_value: float32 [16, 64], P('tp', 'wide')
- grad_w_dense: float32 [1024, 1024], P('tp', 'wide')
- grad_b_dense: float32 [1024], P('wide')
- grad_mid_gain: float32 [1024], P('wide')
- grad_mid_shift: float32 [1024], P('wide')
- grad_w_up: float32 [1024, 4096], P('wide', 'tp')
- grad_b_up: float32 [16, 256], P('tp', 'wide')
- grad_w_down: float32 [4096, 1024], P('tp', 'wide')
- grad_b_down: float32 [1024], P('wide')
Inputs may be any that keep to these rules, and one draw needn't show every extreme that they name: lengths[s] tokens fill the leading positions of slot s; some slot is full and some holds exactly 256 tokens.
All inputs are finite; a program needn't handle non-finite values.
Results may differ from a plain program's by a relative error of at most 0.02.
Values may be sent and summed in bfloat16 or wider, within the bound.
A program may use at most 192 MiB of HBM per device.

v0:
```python
import math

import jax
import jax.numpy as jnp
from jax import lax
from jax.sharding import PartitionSpec as P

HEAD = 64


def norm_rows(values, gain_vec, shift_vec):
    middle = jnp.mean(values, axis=-1, keepdims=True)
    centred = values - middle
    spread = jnp.mean(centred * centred, axis=-1, keepdims=True)
    return centred * lax.rsqrt(spread + 1e-05) * gain_vec + shift_vec


def flatten_rows(tensor):
    return tensor.reshape(-1, tensor.shape[-1])


def row_product(first_op, second_op):
    return jnp.dot(first_op, second_op, preferred_element_type=jnp.float32)


def inner_rows(first_op, second_op):
    return lax.dot_general(
        flatten_rows(first_op),
        flatten_rows(second_op),
        (((0,), (0,)), ((), ())),
        preferred_element_type=jnp.float32,
    )


def times_transposed(first_op, second_op):
    return lax.dot_general(
        first_op,
        second_op,
        (((first_op.ndim - 1,), (1,)), ((), ())),
        preferred_element_type=jnp.float32,
    )


def activate(values):
    return jax.nn.gelu(values, approximate=True)


def masked_scores(query_blk, key_blk, lengths_blk, slopes, distance, causal_mask, key_places):
    raw_scores = (
        jnp.einsum("gihd,gjhd->ghij", query_blk, key_blk, preferred_element_type=jnp.float32)
        * 0.125
    )
    raw_scores = raw_scores - slopes[None, :, None, None] * distance[None, None]
    allowed = causal_mask[None] & (key_places[None, None, :] < lengths_blk[:, None, None])
    return jnp.where(allowed[:, None], raw_scores, -jnp.inf)


def per_device(
    hidden_in,
    lengths,
    pre_gain,
    pre_shift,
    w_query,
    w_key,
    w_value,
    b_query,
    b_value,
    w_dense,
    b_dense,
    mid_gain,
    mid_shift,
    w_up,
    b_up,
    w_down,
    b_down,
    cotangent,
):
    local_slots, block_len, _unused = hidden_in.shape
    heads_dev = b_query.shape[0]
    head_width = heads_dev * HEAD
    slot_total = local_slots * lax.axis_size("tp")
    slot_len = block_len * lax.axis_size("wide")
    wide_at = lax.axis_index("wide")
    tp_at = lax.axis_index("tp")
    vec_part = pre_gain.shape[0]
    (
        gain_one,
        shift_one,
        query_w,
        key_w,
        value_w,
        query_b,
        value_b,
        dense_w,
        dense_b,
        gain_two,
        shift_two,
        up_w,
        up_b,
        down_w,
        down_b,
    ) = (
        lax.all_gather(pre_gain, "wide", axis=0, tiled=True),
        lax.all_gather(pre_shift, "wide", axis=0, tiled=True),
        lax.all_gather(w_query, "wide", axis=0, tiled=True),
        lax.all_gather(w_key, "wide", axis=0, tiled=True),
        lax.all_gather(w_value, "wide", axis=0, tiled=True),
        lax.all_gather(b_query, "wide", axis=1, tiled=True),
        lax.all_gather(b_value, "wide", axis=1, tiled=True),
        lax.all_gather(w_dense, "wide", axis=1, tiled=True),
        lax.all_gather(b_dense, "wide", axis=0, tiled=True),
        lax.all_gather(mid_gain, "wide", axis=0, tiled=True),
        lax.all_gather(mid_shift, "wide", axis=0, tiled=True),
        lax.all_gather(w_up, "wide", axis=0, tiled=True),
        lax.all_gather(b_up, "wide", axis=1, tiled=True),
        lax.all_gather(w_down, "wide", axis=1, tiled=True),
        lax.all_gather(b_down, "wide", axis=0, tiled=True),
    )
    gain_one = gain_one.astype(jnp.float32)
    shift_one = shift_one.astype(jnp.float32)
    gain_two = gain_two.astype(jnp.float32)
    shift_two = shift_two.astype(jnp.float32)
    query_places = wide_at * block_len + jnp.arange(block_len, dtype=jnp.int32)
    key_places = jnp.arange(slot_len, dtype=jnp.int32)
    distance = (query_places[:, None] - key_places[None, :]).astype(jnp.float32)
    causal_mask = key_places[None, :] <= query_places[:, None]
    head_index = tp_at * heads_dev + jnp.arange(heads_dev, dtype=jnp.int32)
    slopes = jnp.exp2(-0.5 * (head_index.astype(jnp.float32) + 1.0))
    own_lengths = lax.dynamic_slice_in_dim(lengths, tp_at * local_slots, local_slots, 0)
    validity = (query_places[None, :] < own_lengths[:, None]).astype(jnp.float32)
    group_size = math.gcd(slot_total, max(1, 512 // block_len))
    group_count = slot_total // group_size
    grouped_lengths = lengths.reshape(group_count, group_size)
    hidden = hidden_in.astype(jnp.float32)

    def query_view(tensor):
        return tensor.reshape(group_count, group_size, block_len, heads_dev, HEAD)

    def pair_view(tensor):
        return tensor.reshape(group_count, group_size, slot_len, 2, heads_dev, HEAD)

    def forward_group(inputs):
        query_blk, pair_blk, lengths_blk = inputs
        masked = masked_scores(
            query_blk, pair_blk[:, :, 0], lengths_blk, slopes, distance, causal_mask, key_places
        )
        highest = jnp.max(masked, axis=-1, keepdims=True)
        totals = highest + jnp.log(jnp.sum(jnp.exp(masked - highest), axis=-1, keepdims=True))
        probabilities = jnp.exp(masked - totals).astype(jnp.bfloat16)
        summed = jnp.einsum(
            "ghij,gjhd->gihd", probabilities, pair_blk[:, :, 1], preferred_element_type=jnp.float32
        )
        return (totals[..., 0], summed)

    def attention_forward(hidden_rows):
        normed_f, norm_back = jax.vjp(norm_rows, hidden_rows, gain_one, shift_one)
        normed = normed_f.astype(jnp.bfloat16)
        normed_all = lax.all_gather(normed, "tp", axis=0, tiled=True)
        queries = (
            row_product(normed_all, query_w) + query_b.reshape(head_width).astype(jnp.float32)
        ).astype(jnp.bfloat16)
        keys_now = row_product(normed_all, key_w).astype(jnp.bfloat16)
        values_now = (
            row_product(normed_all, value_w) + value_b.reshape(head_width).astype(jnp.float32)
        ).astype(jnp.bfloat16)
        pairs = jnp.concatenate([keys_now, values_now], axis=-1)
        pairs_all = lax.all_gather(pairs, "wide", axis=1, tiled=True)
        totals, summed = lax.map(
            forward_group, (query_view(queries), pair_view(pairs_all), grouped_lengths)
        )
        return (
            normed_all,
            queries,
            pairs_all,
            totals,
            summed.reshape(slot_total, block_len, head_width),
            norm_back,
        )

    forward_parts = attention_forward(hidden)
    attention = forward_parts[4].astype(jnp.bfloat16)
    branch = lax.psum_scatter(
        row_product(attention, dense_w).astype(jnp.bfloat16), "tp", scatter_dimension=0, tiled=True
    ).astype(jnp.float32)
    residual = hidden + branch + dense_b.astype(jnp.float32)
    second_f, second_back = jax.vjp(norm_rows, residual, gain_two, shift_two)
    second = second_f.astype(jnp.bfloat16)
    grad_output = validity[:, :, None] * cotangent.astype(jnp.float32)
    grad_down = grad_output.astype(jnp.bfloat16)
    second_all, grad_down_all = (
        lax.all_gather(second, "tp", axis=0, tiled=True),
        lax.all_gather(grad_down, "tp", axis=0, tiled=True),
    )
    pre_act = row_product(second_all, up_w) + up_b.reshape(-1).astype(jnp.float32)
    act_value, act_back = jax.vjp(activate, pre_act)
    activated = act_value.astype(jnp.bfloat16)
    down_out = lax.psum_scatter(
        row_product(activated, down_w).astype(jnp.bfloat16), "tp", scatter_dimension=0, tiled=True
    ).astype(jnp.float32)
    grad_act = times_transposed(grad_down_all, down_w)
    grad_pre = act_back(grad_act)[0].astype(jnp.bfloat16)
    grad_up = inner_rows(second_all, grad_pre)
    grad_up_b = jnp.sum(flatten_rows(grad_pre), axis=0, dtype=jnp.float32).reshape(up_b.shape)
    grad_down_w = inner_rows(activated, grad_down_all)
    grad_second = lax.psum_scatter(
        times_transposed(grad_pre, up_w), "tp", scatter_dimension=0, tiled=True
    )
    output = (validity[:, :, None] * (residual + down_out + down_b.astype(jnp.float32))).astype(
        jnp.bfloat16
    )
    grad_resid_norm, grad_gain_two, grad_shift_two = second_back(grad_second)
    grad_resid = grad_output + grad_resid_norm
    grad_branch = grad_resid.astype(jnp.bfloat16)
    hidden_again, grad_branch = lax.optimization_barrier((hidden, grad_branch))
    forward_parts = attention_forward(hidden_again)
    normed_all, queries, pairs_all, totals, summed, norm_back = forward_parts
    attention_back = summed.astype(jnp.bfloat16)
    branch_all = lax.all_gather(grad_branch, "tp", axis=0, tiled=True)
    grad_dense_w = inner_rows(attention_back, branch_all)
    grad_attention = times_transposed(branch_all, dense_w).astype(jnp.bfloat16)

    def backward_group(inputs):
        query_blk, pair_blk, lengths_blk, totals_blk, grad_blk = inputs
        masked = masked_scores(
            query_blk, pair_blk[:, :, 0], lengths_blk, slopes, distance, causal_mask, key_places
        )
        probabilities = jnp.exp(masked - totals_blk[..., None])
        grad_probs = jnp.einsum(
            "gihd,gjhd->ghij", grad_blk, pair_blk[:, :, 1], preferred_element_type=jnp.float32
        )
        row_delta = jnp.sum(probabilities * grad_probs, axis=-1, keepdims=True)
        grad_scores = (probabilities * (grad_probs - row_delta)).astype(jnp.bfloat16)
        grad_query = (
            jnp.einsum(
                "ghij,gjhd->gihd",
                grad_scores,
                pair_blk[:, :, 0],
                preferred_element_type=jnp.float32,
            )
            * 0.125
        )
        grad_key = (
            jnp.einsum(
                "ghij,gihd->gjhd", grad_scores, query_blk, preferred_element_type=jnp.float32
            )
            * 0.125
        )
        grad_value = jnp.einsum(
            "ghij,gihd->gjhd",
            probabilities.astype(jnp.bfloat16),
            grad_blk,
            preferred_element_type=jnp.float32,
        )
        return (grad_query, jnp.stack([grad_key, grad_value], axis=2))

    grad_query_all, grad_pairs = lax.map(
        backward_group,
        (
            query_view(queries),
            pair_view(pairs_all),
            grouped_lengths,
            totals,
            query_view(grad_attention),
        ),
    )
    grad_pairs_local = lax.psum_scatter(
        grad_pairs.reshape(slot_total, slot_len, 2 * head_width).astype(jnp.bfloat16),
        "wide",
        scatter_dimension=1,
        tiled=True,
    ).astype(jnp.float32)
    grad_queries = grad_query_all.reshape(slot_total, block_len, head_width).astype(jnp.bfloat16)
    grad_keys = grad_pairs_local[:, :, :head_width].astype(jnp.bfloat16)
    grad_values = grad_pairs_local[:, :, head_width:].astype(jnp.bfloat16)
    grad_query_w = inner_rows(normed_all, grad_queries)
    grad_key_w = inner_rows(normed_all, grad_keys)
    grad_value_w = inner_rows(normed_all, grad_values)
    grad_query_b = jnp.sum(flatten_rows(grad_queries), axis=0, dtype=jnp.float32).reshape(
        heads_dev, HEAD
    )
    grad_value_b = jnp.sum(flatten_rows(grad_values), axis=0, dtype=jnp.float32).reshape(
        heads_dev, HEAD
    )
    grad_normed = lax.psum_scatter(
        (
            times_transposed(grad_queries, query_w)
            + times_transposed(grad_keys, key_w)
            + times_transposed(grad_values, value_w)
        ).astype(jnp.bfloat16),
        "tp",
        scatter_dimension=0,
        tiled=True,
    ).astype(jnp.float32)
    grad_hidden_norm, grad_gain_one, grad_shift_one = norm_back(grad_normed)
    grad_in = (grad_resid + grad_hidden_norm).astype(jnp.bfloat16)
    (
        sum_query_w,
        sum_key_w,
        sum_value_w,
        sum_query_b,
        sum_value_b,
        sum_dense_w,
        sum_up_w,
        sum_up_b,
        sum_down_w,
    ) = (
        lax.psum_scatter(
            grad_query_w.astype(jnp.bfloat16), "wide", scatter_dimension=0, tiled=True
        ).astype(jnp.float32),
        lax.psum_scatter(
            grad_key_w.astype(jnp.bfloat16), "wide", scatter_dimension=0, tiled=True
        ).astype(jnp.float32),
        lax.psum_scatter(
            grad_value_w.astype(jnp.bfloat16), "wide", scatter_dimension=0, tiled=True
        ).astype(jnp.float32),
        lax.psum_scatter(
            grad_query_b.astype(jnp.bfloat16), "wide", scatter_dimension=1, tiled=True
        ).astype(jnp.float32),
        lax.psum_scatter(
            grad_value_b.astype(jnp.bfloat16), "wide", scatter_dimension=1, tiled=True
        ).astype(jnp.float32),
        lax.psum_scatter(
            grad_dense_w.astype(jnp.bfloat16), "wide", scatter_dimension=1, tiled=True
        ).astype(jnp.float32),
        lax.psum_scatter(
            grad_up.astype(jnp.bfloat16), "wide", scatter_dimension=0, tiled=True
        ).astype(jnp.float32),
        lax.psum_scatter(
            grad_up_b.astype(jnp.bfloat16), "wide", scatter_dimension=1, tiled=True
        ).astype(jnp.float32),
        lax.psum_scatter(
            grad_down_w.astype(jnp.bfloat16), "wide", scatter_dimension=1, tiled=True
        ).astype(jnp.float32),
    )
    grad_dense_b = jnp.sum(grad_resid, axis=(0, 1))
    grad_down_b = jnp.sum(grad_output, axis=(0, 1))
    sum_gain_one, sum_shift_one, sum_dense_b, sum_gain_two, sum_shift_two, sum_down_b = lax.psum(
        (grad_gain_one, grad_shift_one, grad_dense_b, grad_gain_two, grad_shift_two, grad_down_b),
        ("wide", "tp"),
    )

    def own_part(tensor):
        return lax.dynamic_slice_in_dim(tensor, wide_at * vec_part, vec_part, 0)

    return (
        output,
        grad_in,
        own_part(sum_gain_one),
        own_part(sum_shift_one),
        sum_query_w,
        sum_key_w,
        sum_value_w,
        sum_query_b,
        sum_value_b,
        sum_dense_w,
        own_part(sum_dense_b),
        own_part(sum_gain_two),
        own_part(sum_shift_two),
        sum_up_w,
        sum_up_b,
        sum_down_w,
        own_part(sum_down_b),
    )


def solution(mesh):
    return jax.shard_map(
        per_device,
        mesh=mesh,
        in_specs=(
            P("tp", "wide", None),
            P(),
            P("wide"),
            P("wide"),
            P("wide", "tp"),
            P("wide", "tp"),
            P("wide", "tp"),
            P("tp", "wide"),
            P("tp", "wide"),
            P("tp", "wide"),
            P("wide"),
            P("wide"),
            P("wide"),
            P("wide", "tp"),
            P("tp", "wide"),
            P("tp", "wide"),
            P("wide"),
            P("tp", "wide", None),
        ),
        out_specs=(
            P("tp", "wide", None),
            P("tp", "wide", None),
            P("wide"),
            P("wide"),
            P("wide", "tp"),
            P("wide", "tp"),
            P("wide", "tp"),
            P("tp", "wide"),
            P("tp", "wide"),
            P("tp", "wide"),
            P("wide"),
            P("wide"),
            P("wide"),
            P("wide", "tp"),
            P("tp", "wide"),
            P("tp", "wide"),
            P("wide"),
        ),
        check_vma=False,
    )
```

profile of v0, /device:TPU:0, one launch (start us, length us, event | category | flops | bytes accessed | tf_op | source)
XLA Modules:
  0.0 1197.6 jit_solution(1751168843750282210)
XLA Ops:
  9.8 10.4 all-gather
  20.2 8.6 all-gather.1
  31.0 8.1 all-gather.2
  39.3 9.7 all_gather.69
  48.9 9.2 all_gather.70
  58.1 19.0 %all-gather.19.cloned.1.call-done = bf16[8,128,1024]{2,1,0:T(8,128)(2,1)} async-done(((bf16[2,128,1024]{2,1,0:T(8,128)(2,1)}), bf16[8,128,1024]{2,1,0:T(8,128)(2,1)}) %all-gather.19.cloned.1.call-update) | async-done | bytes 2097168 | tf_op jit(solution)/shard_map/all_gather | solution.py:158
  83.0 8.8 all-gather.3
  92.0 12.5 %all_gather.73 = bf16[1024,256]{1,0:T(8,128)(2,1)S(1)} all-gather(bf16[128,256]{1,0:T(8,128)(2,1)S(1)} %copy-done.28), channel_id=1, replica_groups=mesh['wide'=8,'tp'=4] {'wide'}, dimensions={0}, use_global_device_ids=true | all-gather | bytes 589824 | tf_op jit(solution)/shard_map/all_gather | solution.py:105
  104.5 9.7 all_gather.75
  117.0 21.2 %all-gather.21.cloned.1.call-done = bf16[8,1024,512]{2,1,0:T(8,128)(2,1)} async-done(((bf16[8,128,512]{2,1,0:T(8,128)(2,1)}), bf16[8,1024,512]{2,1,0:T(8,128)(2,1)}) %all-gather.21.cloned.1.call-update) | async-done | bytes 8388624 | tf_op jit(solution)/shard_map/all_gather | solution.py:167
  138.2 11.5 copy.94
  149.8 21.8 %while.40 = (s32[]{:T(128)}, bf16[2,4,128,4,64]{2,4,3,1,0:T(8,128)(2,1)S(1)}, bf16[2,4,1024,2,4,64]{2,5,4,3,1,0:T(8,128)(2,1)}, s32[2,4]{1,0:T(2,128)S(1)}, bf16...) while((s32[]{:T(128)}, ...), condition=%wide.region_5.6_spmd.clone.clone, body=%wide.region_2.5_spmd.clone.clone.sunk | while | flops 567674880 | bytes 50398400 | solution.py:168
  150.7 2.8 copy_bitcast_fusion.2
  161.6 2.8 copy_bitcast_fusion.2
  174.4 8.7 all-gather.4
  183.1 7.8 all-gather.5
  191.0 8.7 all-gather.6
  199.7 17.8 %reduce-scatter.21.cloned.1.call-done = bf16[2,128,1024]{2,1,0:T(8,128)(2,1)} async-done(((bf16[8,128,1024]{2,1,0:T(8,128)(2,1)}), bf16[2,128,1024]{2,1,0:T(8,128)(2,1)}) %reduce-scatter.21.cloned.1.call-update) | async-done | bytes 524304 | tf_op jit(solution)/shard_map/reduce_scatter | solution.py:182
  224.4 9.1 all-gather.7
  233.5 12.8 %all-gather.25.cloned.1.call-done = bf16[1024,1024]{1,0:T(8,128)(2,1)} async-done(((bf16[128,1024]{1,0:T(8,128)(2,1)}), bf16[1024,1024]{1,0:T(8,128)(2,1)}) %all-gather.25.cloned.1.call-update) | async-done | bytes 2097168 | tf_op jit(solution)/shard_map/all_gather | solution.py:114
  246.3 47.7 %all-gather.23.cloned.1.call-done = bf16[8,128,1024]{2,1,0:T(8,128)(2,1)} async-done(((bf16[2,128,1024]{2,1,0:T(8,128)(2,1)}), bf16[8,128,1024]{2,1,0:T(8,128)(2,1)}) %all-gather.23.cloned.1.call-update) | async-done | bytes 2097168 | tf_op jit(solution)/shard_map/all_gather | solution.py:191
  294.0 6.5 fusion.83
  300.6 40.0 %all-gather.29.cloned.1.call-done = bf16[8,128,1024]{2,1,0:T(8,128)(2,1)} async-done(((bf16[2,128,1024]{2,1,0:T(8,128)(2,1)}), bf16[8,128,1024]{2,1,0:T(8,128)(2,1)}) %all-gather.29.cloned.1.call-update) | async-done | bytes 2097168 | tf_op jit(solution)/shard_map/all_gather | solution.py:192
  340.5 28.8 %all-gather.27.cloned.1.call-done = bf16[1024,1024]{1,0:T(8,128)(2,1)} async-done(((bf16[1024,128]{1,0:T(8,128)(2,1)}), bf16[1024,1024]{1,0:T(8,128)(2,1)}) %all-gather.27.cloned.1.call-update) | async-done | bytes 2097168 | tf_op jit(solution)/shard_map/all_gather | solution.py:116
  369.3 8.9 fusion.127
  379.6 4.3 fusion.81
  384.0 7.1 fusion.85
  391.3 9.0 all-gather.8
  400.3 60.6 %reduce-scatter.25.cloned.1.call-done = f32[2,128,1024]{2,1,0:T(8,128)} async-done(((f32[8,128,1024]{2,1,0:T(8,128)}), f32[2,128,1024]{2,1,0:T(8,128)}) %reduce-scatter.25.cloned.1.call-update) | async-done | bytes 1048592 | tf_op jit(solution)/shard_map/reduce_scatter | solution.py:205
  463.2 44.1 %reduce-scatter.23.cloned.1.call-done = bf16[2,128,1024]{2,1,0:T(8,128)(2,1)} async-done(((bf16[8,128,1024]{2,1,0:T(8,128)(2,1)}), bf16[2,128,1024]{2,1,0:T(8,128)(2,1)}) %reduce-scatter.23.cloned.1.call-update) | async-done | bytes 524304 | tf_op jit(solution)/shard_map/reduce_scatter | solution.py:197
  507.3 2.8 fusion.126
  514.5 44.2 %all-gather.31.cloned.1.call-done = bf16[8,128,1024]{2,1,0:T(8,128)(2,1)} async-done(((bf16[2,128,1024]{2,1,0:T(8,128)(2,1)}), bf16[8,128,1024]{2,1,0:T(8,128)(2,1)}) %all-gather.31.cloned.1.call-update) | async-done | bytes 2097168 | tf_op jit(solution)/shard_map/all_gather | solution.py:158
  564.6 40.7 %all-gather.35.cloned.1.call-done = bf16[8,128,1024]{2,1,0:T(8,128)(2,1)} async-done(((bf16[2,128,1024]{2,1,0:T(8,128)(2,1)}), bf16[8,128,1024]{2,1,0:T(8,128)(2,1)}) %all-gather.35.cloned.1.call-update) | async-done | bytes 2097168 | tf_op jit(solution)/shard_map/all_gather | solution.py:218
  610.6 49.6 %all-gather.33.cloned.1.call-done = bf16[8,1024,512]{2,1,0:T(8,128)(2,1)} async-done(((bf16[8,128,512]{2,1,0:T(8,128)(2,1)}), bf16[8,1024,512]{2,1,0:T(8,128)(2,1)}) %all-gather.33.cloned.1.call-update) | async-done | bytes 8388624 | tf_op jit(solution)/shard_map/all_gather | solution.py:167
  660.2 11.5 copy.100
  671.7 8.4 copy.104
  680.3 21.9 %while.41 = (s32[]{:T(128)}, f32[2,4,4,128]{3,2,1,0:T(4,128)S(1)}, bf16[2,4,128,4,64]{2,4,3,1,0:T(8,128)(2,1)S(1)}, s32[2,4]{1,0:T(2,128)S(1)}, bf16[2,4,128,4,6...) while((s32[]{:T(128)}, f32[2,4,4,128]{3,2,1,0:T(4,128)S(1)}, ...), condition=%wide.region_18.19_spmd.clone.clone, body=%wide.region_15.18_spmd.clone.clone.sunk | while | flops 567674880 | bytes 50406604 | solution.py:168
  681.2 2.8 dynamic-slice_bitcast_fusion.6
  692.2 2.8 dynamic-slice_bitcast_fusion.6
  703.1 35.1 %while.42 = (s32[]{:T(128)}, bf16[2,4,128,4,64]{2,4,3,1,0:T(8,128)(2,1)}, bf16[2,4,1024,2,4,64]{2,5,4,3,1,0:T(8,128)(2,1)}, bf16[2,4,1024,2,4,64]{2,5,4,1,3,0:T(...) while((s32[]{:T(128)}, ...), condition=%wide.region_21.22_spmd.clone.clone, body=%wide.region_19.21_spmd.clone.clone.sunk | while | flops 1368918016 | bytes 161269104 | solution.py:256
  704.5 2.8 dynamic-slice_bitcast_fusion.7
  708.6 3.6 multiply_reduce_fusion.7
  717.7 3.2 copy-done.7
  721.8 2.8 dynamic-slice_bitcast_fusion.7
  725.9 3.6 multiply_reduce_fusion.7
  735.0 3.2 copy-done.7
  738.2 11.4 copy.107
  751.2 5.9 bitcast_convert_fusion
  757.1 2.8 copy.130
  760.0 6.8 bitcast_convert_fusion.1
  770.4 3.1 fusion.88
  773.6 47.6 %reduce-scatter.27.cloned.1.call-done = bf16[8,128,512]{2,1,0:T(8,128)(2,1)} async-done(((bf16[8,1024,512]{2,1,0:T(8,128)(2,1)}), bf16[8,128,512]{2,1,0:T(8,128)(2,1)}) %reduce-scatter.27.cloned.1.call-update) | async-done | bytes 1048592 | tf_op jit(solution)/shard_map/reduce_scatter | solution.py:266
  821.2 3.2 fusion.90
  824.5 2.7 fusion.106
  834.8 23.4 %reduce-scatter.41.cloned.1.call-done = bf16[32,4]{1,0:T(8,128)(2,1)} async-done(((bf16[256,4]{1,0:T(8,128)(2,1)}), bf16[32,4]{1,0:T(8,128)(2,1)}) %reduce-scatter.41.cloned.1.call-update) | async-done | bytes 272
  859.5 42.9 %reduce-scatter.43.cloned.1.call-done = bf16[128,1024]{1,0:T(8,128)(2,1)} async-done(((bf16[1024,1024]{1,0:T(8,128)(2,1)}), bf16[128,1024]{1,0:T(8,128)(2,1)}) %reduce-scatter.43.cloned.1.call-update) | async-done | bytes 262160
  904.4 42.3 %reduce-scatter.37.cloned.1.call-done = bf16[128,1024]{1,0:T(8,128)(2,1)} async-done(((bf16[1024,1024]{1,0:T(8,128)(2,1)}), bf16[128,1024]{1,0:T(8,128)(2,1)}) %reduce-scatter.37.cloned.1.call-update) | async-done | bytes 262160 | tf_op jit(solution)/shard_map/reduce_scatter | solution.py:325
  948.6 35.2 %reduce-scatter.39.cloned.1.call-done = bf16[128,256]{1,0:T(8,128)(2,1)} async-done(((bf16[1024,256]{1,0:T(8,128)(2,1)}), bf16[128,256]{1,0:T(8,128)(2,1)}) %reduce-scatter.39.cloned.1.call-update) | async-done | bytes 65552
  985.4 35.5 %reduce-scatter.31.cloned.1.call-done = bf16[128,256]{1,0:T(8,128)(2,1)} async-done(((bf16[1024,256]{1,0:T(8,128)(2,1)}), bf16[128,256]{1,0:T(8,128)(2,1)}) %reduce-scatter.31.cloned.1.call-update) | async-done | bytes 65552 | tf_op jit(solution)/shard_map/reduce_scatter | solution.py:307
  1023.7 12.1 %all-reduce.3 = (bf16[4,64]{1,0:T(4,128)(2,1)S(1)}, bf16[4,64]{1,0:T(4,128)(2,1)S(1)}) all-reduce(bf16[4,64]{1,0:T(4,128)(2,1)S(1)} %reduce_sum.251, bf16[4,64]{1,0:T(4,128)(2,1)S(1)} %convert_element_type.288), channel_id=10, replica_groups=mesh['wide'=8,'tp'=4] {'wide'}, use_global_device_ids=true, to_apply=%region_34.35.clone | all-reduce | flops 512 | bytes 2048
  1036.5 21.7 %reduce-scatter.35.cloned.1.call-done = bf16[128,256]{1,0:T(8,128)(2,1)} async-done(((bf16[1024,256]{1,0:T(8,128)(2,1)}), bf16[128,256]{1,0:T(8,128)(2,1)}) %reduce-scatter.35.cloned.1.call-update) | async-done | bytes 65552 | tf_op jit(solution)/shard_map/reduce_scatter | solution.py:313
  1059.7 36.2 %reduce-scatter.33.cloned.1.call-done = bf16[128,256]{1,0:T(8,128)(2,1)} async-done(((bf16[1024,256]{1,0:T(8,128)(2,1)}), bf16[128,256]{1,0:T(8,128)(2,1)}) %reduce-scatter.33.cloned.1.call-update) | async-done | bytes 65552 | tf_op jit(solution)/shard_map/reduce_scatter | solution.py:310
  1097.4 44.5 %reduce-scatter.29.cloned.1.call-done = bf16[2,128,1024]{2,1,0:T(8,128)(2,1)} async-done(((bf16[8,128,1024]{2,1,0:T(8,128)(2,1)}), bf16[2,128,1024]{2,1,0:T(8,128)(2,1)}) %reduce-scatter.29.cloned.1.call-update) | async-done | bytes 524304 | tf_op jit(solution)/shard_map/reduce_scatter | solution.py:284
  1147.3 39.7 %all-reduce.2 = (f32[1024]{0:T(1024)S(1)}, f32[1024]{0:T(1024)S(1)}, f32[1024]{0:T(1024)S(1)}, f32[1024]{0:T(1024)S(1)}, f32[1024]{0:T(1024)S(1)}, /*index=5*/f32[1024]{0:T(1024)S(1)}) all-reduce(f32[1024]{0:T(1024)S(1)} %get-tuple-element.442, f32[1024]{0:T(1024)S(1)} %get-tuple-element.447, ...), channel_id=1, replica_groups=mesh['wide'=8,'tp'=4] {'wide','tp'}, use_global_device_ids=true, to_apply=%region_27.28 | all-reduce | flops 6144 | bytes 49152 | tf_op jit(solution)/shard_map/psum | solution.py:337
  (331 shorter events, 125.3 us)
Async XLA Ops:
  7.2 69.9 %all-gather.19.cloned.1.call-start = ((), (), s32[]{:S(2)}) async-start(), calls=%async_computation.12 | async-start | bytes 2621440 | tf_op jit(solution)/shard_map/all_gather | solution.py:158
  20.2 492.4 %copy-start.26 = (f32[8,1,128]{2,1,0:T(1,128)}, f32[8,1,128]{2,1,0:T(1,128)S(1)}, u32[]{:S(2)}) copy-start(f32[8,1,128]{2,1,0:T(1,128)S(1)} %convert_element_type.303) | copy-start | bytes 12292
  30.9 107.2 %all-gather.21.cloned.1.call-start = ((), (), s32[]{:S(2)}) async-start(), calls=%async_computation.13 | async-start | bytes 9437184 | tf_op jit(solution)/shard_map/all_gather | solution.py:167
  48.9 33.9 %copy-start.16 = (bf16[1024,256]{1,0:T(8,128)(2,1)}, bf16[1024,256]{1,0:T(8,128)(2,1)S(1)}, u32[]{:S(2)}) copy-start(bf16[1024,256]{1,0:T(8,128)(2,1)S(1)} %all_gather.69) | copy-start | bytes 1572868
  58.1 502.9 %copy-start.14 = (bf16[1024,256]{1,0:T(8,128)(2,1)}, bf16[1024,256]{1,0:T(8,128)(2,1)S(1)}, u32[]{:S(2)}) copy-start(bf16[1024,256]{1,0:T(8,128)(2,1)S(1)} %all_gather.70) | copy-start | bytes 1572868
  79.4 3.6 copy-start.53
  79.4 3.6 copy-start.45
  79.4 12.6 %copy-start.28 = (bf16[128,256]{1,0:T(8,128)(2,1)S(1)}, bf16[128,256]{1,0:T(8,128)(2,1)}, u32[]{:S(2)}) copy-start(bf16[128,256]{1,0:T(8,128)(2,1)} %param.28) | copy-start | bytes 196612
  79.4 25.1 %copy-start.29 = (bf16[256,128]{1,0:T(8,128)(2,1)S(1)}, bf16[256,128]{1,0:T(8,128)(2,1)}, u32[]{:S(2)}) copy-start(bf16[256,128]{1,0:T(8,128)(2,1)} %param.33) | copy-start | bytes 196612
  82.9 134.6 %reduce-scatter.21.cloned.1.call-start = ((), (), s32[]{:S(2)}) async-start(), calls=%async_computation.14 | async-start | bytes 2621440 | tf_op jit(solution)/shard_map/reduce_scatter | solution.py:182
  104.5 9.7 copy-start.19
  114.2 57.5 %copy-start.22 = (bf16[256,1024]{1,0:T(8,128)(2,1)}, bf16[256,1024]{1,0:T(8,128)(2,1)S(1)}, u32[]{:S(2)}) copy-start(bf16[256,1024]{1,0:T(8,128)(2,1)S(1)} %all_gather.75) | copy-start | bytes 1572868
  171.6 11.5 copy-start.48
  171.6 19.3 %copy-start.49 = (bf16[128]{0:T(256)(128)(2,1)S(1)}, bf16[128]{0:T(256)(128)(2,1)}, u32[]{:S(2)}) copy-start(bf16[128]{0:T(256)(128)(2,1)} %param.36) | copy-start | bytes 772
  171.6 45.9 %copy-start.2 = (bf16[2,128,1024]{2,1,0:T(8,128)(2,1)S(1)}, bf16[2,128,1024]{2,1,0:T(8,128)(2,1)}, u32[]{:S(2)}) copy-start(bf16[2,128,1024]{2,1,0:T(8,128)(2,1)} %param.24) | copy-start | bytes 1572868
  171.7 50.9 %copy-start.8 = (bf16[2,128,1024]{2,1,0:T(8,128)(2,1)S(1)}, bf16[2,128,1024]{2,1,0:T(8,128)(2,1)}, u32[]{:S(2)}) copy-start(bf16[2,128,1024]{2,1,0:T(8,128)(2,1)} %param.41) | copy-start | bytes 1572868
  173.7 50.7 %copy-start.46 = (bf16[4,32]{1,0:T(4,128)(2,1)S(1)}, bf16[4,32]{1,0:T(4,128)(2,1)}, u32[]{:S(2)}) copy-start(bf16[4,32]{1,0:T(4,128)(2,1)} %param.38) | copy-start | bytes 772
  173.7 72.6 %all-gather.25.cloned.1.call-start = ((), (), s32[]{:S(2)}) async-start(), calls=%async_computation.16 | async-start | bytes 2359296 | tf_op jit(solution)/shard_map/all_gather | solution.py:114
  174.3 119.7 %all-gather.23.cloned.1.call-start = ((), (), s32[]{:S(2)}) async-start(), calls=%async_computation.15 | async-start | bytes 2621440 | tf_op jit(solution)/shard_map/all_gather | solution.py:191
  222.4 118.1 %all-gather.29.cloned.1.call-start = ((), (), s32[]{:S(2)}) async-start(), calls=%async_computation.19 | async-start | bytes 2621440 | tf_op jit(solution)/shard_map/all_gather | solution.py:192
  222.6 287.5 %copy-start.32 = (f32[2,128]{1,0:T(2,128)}, f32[2,128]{1,0:T(2,128)S(1)}, u32[]{:S(2)}) copy-start(f32[2,128]{1,0:T(2,128)S(1)} %compare_convert_fusion) | copy-start | bytes 3076
  223.6 145.8 %all-gather.27.cloned.1.call-start = ((), (), s32[]{:S(2)}) async-start(), calls=%async_computation.17 | async-start | bytes 2359296 | tf_op jit(solution)/shard_map/all_gather | solution.py:116
  224.3 236.6 %reduce-scatter.25.cloned.1.call-start = ((), (), s32[]{:S(2)}) async-start(), calls=%async_computation.20 | async-start | bytes 5242880 | tf_op jit(solution)/shard_map/reduce_scatter | solution.py:205
  233.5 150.5 %copy-start.42 = (f32[1,2,4,128]{3,1,2,0:T(2,128)}, f32[1,2,4,128]{3,1,2,0:T(2,128)S(1)}, u32[]{:S(2)}) copy-start(f32[1,2,4,128]{3,1,2,0:T(2,128)S(1)} %copy.151) | copy-start | bytes 12292
  369.3 10.3 copy-start.52
  383.9 7.3 copy-start.50
  384.0 76.9 %copy-start.4 = (bf16[2,128,1024]{2,1,0:T(8,128)(2,1)S(1)}, bf16[2,128,1024]{2,1,0:T(8,128)(2,1)}, u32[]{:S(2)}) copy-start(bf16[2,128,1024]{2,1,0:T(8,128)(2,1)} %reduce-scatter.21.cloned.1.call-done) | copy-start | bytes 1572868
  384.0 123.4 %reduce-scatter.23.cloned.1.call-start = ((), (), s32[]{:S(2)}) async-start(), calls=%async_computation.18 | async-start | bytes 2621440 | tf_op jit(solution)/shard_map/reduce_scatter | solution.py:197
  391.1 167.6 %all-gather.31.cloned.1.call-start = ((), (), s32[]{:S(2)}) async-start(), calls=%async_computation.21 | async-start | bytes 2621440 | tf_op jit(solution)/shard_map/all_gather | solution.py:158
  391.3 121.3 %copy-start = (f32[2,128,1024]{2,1,0:T(8,128)}, f32[2,128,1024]{2,1,0:T(8,128)S(1)}, u32[]{:S(2)}) copy-start(f32[2,128,1024]{2,1,0:T(8,128)S(1)} %convert_element_type.237) | copy-start | bytes 3145732
  510.1 48.6 %copy-start.17 = (bf16[1024,256]{1,0:T(8,128)(2,1)S(1)}, bf16[1024,256]{1,0:T(8,128)(2,1)}, u32[]{:S(2)}) copy-start(bf16[1024,256]{1,0:T(8,128)(2,1)} %copy-done.16) | copy-start | bytes 1572868
  512.3 51.1 %copy-start.30 = (f32[2,128]{1,0:T(2,128)}, f32[2,128]{1,0:T(2,128)S(1)}, u32[]{:S(2)}) copy-start(f32[2,128]{1,0:T(2,128)S(1)} %broadcast_multiply_fusion.3) | copy-start | bytes 3076
  512.6 48.5 %copy-start.40 = (f32[2,128]{1,0:T(2,128)}, f32[2,128]{1,0:T(2,128)S(1)}, u32[]{:S(2)}) copy-start(f32[2,128]{1,0:T(2,128)S(1)} %multiply_reduce_fusion.2) | copy-start | bytes 3076
  512.6 50.8 %copy-start.34 = (f32[2,128]{1,0:T(2,128)}, f32[2,128]{1,0:T(2,128)S(1)}, u32[]{:S(2)}) copy-start(f32[2,128]{1,0:T(2,128)S(1)} %fusion.125) | copy-start | bytes 3076
  513.7 91.7 %all-gather.35.cloned.1.call-start = ((), (), s32[]{:S(2)}) async-start(), calls=%async_computation.23 | async-start | bytes 2621440 | tf_op jit(solution)/shard_map/all_gather | solution.py:218
  514.4 145.8 %all-gather.33.cloned.1.call-start = ((), (), s32[]{:S(2)}) async-start(), calls=%async_computation.22 | async-start | bytes 9437184 | tf_op jit(solution)/shard_map/all_gather | solution.py:167
  561.0 44.3 %copy-start.23 = (bf16[256,1024]{1,0:T(8,128)(2,1)S(1)}, bf16[256,1024]{1,0:T(8,128)(2,1)}, u32[]{:S(2)}) copy-start(bf16[256,1024]{1,0:T(8,128)(2,1)} %copy-done.22) | copy-start | bytes 1572868
  563.4 44.5 %copy-start.20 = (bf16[1024,256]{1,0:T(8,128)(2,1)S(1)}, bf16[1024,256]{1,0:T(8,128)(2,1)}, u32[]{:S(2)}) copy-start(bf16[1024,256]{1,0:T(8,128)(2,1)} %copy-done.19) | copy-start | bytes 1572868
  564.6 256.6 %reduce-scatter.27.cloned.1.call-start = ((), (), s32[]{:S(2)}) async-start(), calls=%async_computation.24 | async-start | bytes 9437184 | tf_op jit(solution)/shard_map/reduce_scatter | solution.py:266
  713.1 3.4 slice-start
  730.4 3.4 slice-start
  735.0 3.2 copy-start.7
  749.6 108.5 %reduce-scatter.41.cloned.1.call-start = ((), (), s32[]{:S(2)}) async-start(), calls=%async_computation.31 | async-start | bytes 73728
  751.1 151.3 %reduce-scatter.43.cloned.1.call-start = ((), (), s32[]{:S(2)}) async-start(), calls=%async_computation.32 | async-start | bytes 2359296
  759.9 6.9 copy-start.25
  759.9 186.7 %reduce-scatter.37.cloned.1.call-start = ((), (), s32[]{:S(2)}) async-start(), calls=%async_computation.29 | async-start | bytes 2359296 | tf_op jit(solution)/shard_map/reduce_scatter | solution.py:325
  766.8 3.6 copy-start.12
  766.8 217.0 %reduce-scatter.39.cloned.1.call-start = ((), (), s32[]{:S(2)}) async-start(), calls=%async_computation.30 | async-start | bytes 589824
  770.3 250.6 %reduce-scatter.31.cloned.1.call-start = ((), (), s32[]{:S(2)}) async-start(), calls=%async_computation.26 | async-start | bytes 589824 | tf_op jit(solution)/shard_map/reduce_scatter | solution.py:307
  773.5 51.0 %copy-start.21 = (bf16[1024,256]{1,0:T(8,128)(2,1)S(1)}, bf16[1024,256]{1,0:T(8,128)(2,1)}, u32[]{:S(2)}) copy-start(bf16[1024,256]{1,0:T(8,128)(2,1)} %copy-done.19) | copy-start | bytes 1572868
  773.5 284.6 %reduce-scatter.35.cloned.1.call-start = ((), (), s32[]{:S(2)}) async-start(), calls=%async_computation.28 | async-start | bytes 589824 | tf_op jit(solution)/shard_map/reduce_scatter | solution.py:313
  824.4 271.4 %reduce-scatter.33.cloned.1.call-start = ((), (), s32[]{:S(2)}) async-start(), calls=%async_computation.27 | async-start | bytes 589824 | tf_op jit(solution)/shard_map/reduce_scatter | solution.py:310
  828.8 313.0 %reduce-scatter.29.cloned.1.call-start = ((), (), s32[]{:S(2)}) async-start(), calls=%async_computation.25 | async-start | bytes 2621440 | tf_op jit(solution)/shard_map/reduce_scatter | solution.py:284
  833.3 308.6 %copy-start.1 = (f32[2,128,1024]{2,1,0:T(8,128)S(1)}, f32[2,128,1024]{2,1,0:T(8,128)}, u32[]{:S(2)}) copy-start(f32[2,128,1024]{2,1,0:T(8,128)} %copy-done) | copy-start | bytes 3145732
  833.3 308.6 %copy-start.27 = (f32[8,1,128]{2,1,0:T(1,128)S(1)}, f32[8,1,128]{2,1,0:T(1,128)}, u32[]{:S(2)}) copy-start(f32[8,1,128]{2,1,0:T(1,128)} %copy-done.26) | copy-start | bytes 12292
  833.3 308.6 %copy-start.31 = (f32[2,128]{1,0:T(2,128)S(1)}, f32[2,128]{1,0:T(2,128)}, u32[]{:S(2)}) copy-start(f32[2,128]{1,0:T(2,128)} %copy-done.30) | copy-start | bytes 3076
  833.3 309.9 %copy-start.41 = (f32[2,128]{1,0:T(2,128)S(1)}, f32[2,128]{1,0:T(2,128)}, u32[]{:S(2)}) copy-start(f32[2,128]{1,0:T(2,128)} %copy-done.40) | copy-start | bytes 3076
  833.3 309.9 %copy-start.35 = (f32[2,128]{1,0:T(2,128)S(1)}, f32[2,128]{1,0:T(2,128)}, u32[]{:S(2)}) copy-start(f32[2,128]{1,0:T(2,128)} %copy-done.34) | copy-start | bytes 3076
  833.3 311.5 %copy-start.6 = (f32[2,128,1024]{2,1,0:T(8,128)S(1)}, f32[2,128,1024]{2,1,0:T(8,128)}, u32[]{:S(2)}) copy-start(f32[2,128,1024]{2,1,0:T(8,128)} %copy-done.5) | copy-start | bytes 3145732
  833.3 311.5 %copy-start.9 = (bf16[2,128,1024]{2,1,0:T(8,128)(2,1)S(1)}, bf16[2,128,1024]{2,1,0:T(8,128)(2,1)}, u32[]{:S(2)}) copy-start(bf16[2,128,1024]{2,1,0:T(8,128)(2,1)} %param.41) | copy-start | bytes 1572868
  833.3 311.5 %copy-start.33 = (f32[2,128]{1,0:T(2,128)S(1)}, f32[2,128]{1,0:T(2,128)}, u32[]{:S(2)}) copy-start(f32[2,128]{1,0:T(2,128)} %copy-done.32) | copy-start | bytes 3076
  833.3 311.5 %copy-start.39 = (f32[2,128]{1,0:T(2,128)S(1)}, f32[2,128]{1,0:T(2,128)}, u32[]{:S(2)}) copy-start(f32[2,128]{1,0:T(2,128)} %copy-done.38) | copy-start | bytes 3076
  948.6 198.7 %copy-start.36 = (f32[1024]{0:T(1024)S(1)}, f32[1024]{0:T(1024)}, u32[]{:S(2)}) copy-start(f32[1024]{0:T(1024)} %get-tuple-element.440) | copy-start | bytes 12292
  948.6 198.7 %copy-start.37 = (f32[1024]{0:T(1024)S(1)}, f32[1024]{0:T(1024)}, u32[]{:S(2)}) copy-start(f32[1024]{0:T(1024)} %get-tuple-element.444) | copy-start | bytes 12292
  (20 other events, 37.8 us)
Sparse Core Ops, SparseCore 0:
  31.1 45.9 all-gather.18
  83.0 55.0 all-gather.20
  173.9 43.6 reduce-scatter.20
  219.3 27.0 all-gather.24
  248.3 45.6 all-gather.22
  296.0 44.4 all-gather.28
  342.4 26.8 all-gather.26
  384.1 76.7 reduce-scatter.24
  463.2 44.0 reduce-scatter.22
  513.8 44.8 all-gather.30
  560.9 44.4 all-gather.34
  607.1 53.0 all-gather.32
  749.8 71.3 reduce-scatter.26
  824.6 33.5 reduce-scatter.40
  861.3 41.0 reduce-scatter.42
  905.6 41.0 reduce-scatter.36
  949.6 34.1 reduce-scatter.38
  986.7 34.1 reduce-scatter.30
  1024.0 34.1 reduce-scatter.34
  1061.7 34.1 reduce-scatter.32
  1098.2 43.6 reduce-scatter.28
where the time goes:
time: 1200 us
  waiting for transfers between devices  758 us (63%)
  blocking collectives  172 us (14%)
  matrix products  108 us (9%)
  local copies, waits for them, and re-layouts  86.3 us (7%)
  other arithmetic  54.7 us (5%)
  between operations  16.1 us (1%)
    unnamed x24, waiting for transfers between devices  104 us
    all_gather x2, waiting for transfers between devices, attention_forward(): pairs_all = lax.all_gather(pairs, 'wide', axis=1, tiled=True)  70.8 us
    all_gather x2, waiting for transfers between devices, attention_forward(): normed_all = lax.all_gather(normed, 'tp', axis=0, tiled=True)  63.2 us
    reduce_scatter x1, waiting for transfers between devices, per_device(): lax.psum_scatter(times_transposed(grad_pre, up_w), 'tp', scatter_dimensio...  60.6 us
    all_gather x1, waiting for transfers between devices, per_device(): lax.all_gather(second, 'tp', axis=0, tiled=True)  47.7 us
    reduce_scatter x1, waiting for transfers between devices, per_device(): lax.psum_scatter(grad_pairs.reshape(slot_total, slot_len, 2 * head_width)...  47.6 us
    reduce_scatter x1, waiting for transfers between devices, per_device(): lax.psum_scatter((times_transposed(grad_queries, query_w) + times_transpo...  44.5 us
    reduce_scatter x1, waiting for transfers between devices, per_device(): lax.psum_scatter(row_product(activated, down_w).astype(jnp.bfloat16), 'tp...  44.1 us
  transfers between devices with their start and end apart: 21, of which 21 were waited for; matrix products, arithmetic and copies ran while one was open for 7% of the time, Pallas kernels for 0%

commit v1 on v0

--- a/solution.py
+++ b/solution.py
@@ -1,11 +1,15 @@
+import functools
 import math
 
 import jax
 import jax.numpy as jnp
 from jax import lax
+from jax.experimental import pallas as pl
+from jax.experimental.pallas import tpu as pltpu
 from jax.sharding import PartitionSpec as P
 
 HEAD = 64
+MESH = pl.DeviceIdType.MESH
 
 
 def norm_rows(values, gain_vec, shift_vec):
@@ -363,9 +367,1030 @@
     )
 
 
+BF = jnp.bfloat16
+F32 = jnp.float32
+LOG2E = 1.4426950408889634
+NEG = -1e30
+BLK = 128
+
+
+def hbm():
+    return pl.BlockSpec(memory_space=pl.ANY)
+
+
+def vmem():
+    return pl.BlockSpec(memory_space=pltpu.VMEM)
+
+
+def square_places():
+    own = lax.axis_index("wide")
+    core = own % 2
+    col = (own // 2) % 2
+    row = own // 4
+    pair = own + 1 - 2 * core
+    along_x = own + 2 - 4 * col
+    along_y = own + 4 - 8 * row
+    return own, pair, along_x, along_y, along_x + along_y - own
+
+
+def greet(targets):
+    barrier = pltpu.get_barrier_semaphore()
+    for target in targets:
+        pl.semaphore_signal(barrier, inc=1, device_id=target, device_id_type=MESH)
+    pl.semaphore_wait(barrier, len(targets))
+
+
+def remote(src, dst, send_sem, recv_sem, target):
+    return pltpu.make_async_remote_copy(
+        src_ref=src,
+        dst_ref=dst,
+        send_sem=send_sem,
+        recv_sem=recv_sem,
+        device_id=target,
+        device_id_type=MESH,
+    )
+
+
+class SquareGather:
+    SENDS = 13
+
+    def __init__(self, src, dst, send, recv, local):
+        own, pair, ax, ay, dg = square_places()
+
+        def place(slot, dev):
+            return dst.at[slot, pl.ds(pl.multiple_of(dev * BLK, BLK), BLK)]
+
+        def both(dev):
+            return dst.at[:, pl.ds(pl.multiple_of(dev * BLK, BLK), BLK)]
+
+        to_x, to_y, to_p = {"wide": ax}, {"wide": ay}, {"wide": pair}
+        self.local = pltpu.make_async_copy(src, both(own), local)
+        copies = {}
+        copies["x0"] = remote(src.at[0], place(0, own), send.at[0], recv.at[0], to_x)
+        copies["x1"] = remote(src.at[1], place(1, own), send.at[1], recv.at[1], to_x)
+        copies["y0"] = remote(src.at[0], place(0, own), send.at[2], recv.at[2], to_y)
+        copies["y1"] = remote(src.at[1], place(1, own), send.at[3], recv.at[3], to_y)
+        copies["d0"] = remote(place(0, ay), place(0, ay), send.at[4], recv.at[4], to_x)
+        copies["d1"] = remote(place(1, ax), place(1, ax), send.at[5], recv.at[5], to_y)
+        copies["p"] = remote(src, both(own), send.at[6], recv.at[6], to_p)
+        for index, (name, slot, dev) in enumerate(
+            (("x0", 0, ax), ("x1", 1, ax), ("y0", 0, ay), ("y1", 1, ay), ("d0", 0, dg), ("d1", 1, dg))
+        ):
+            copies["p" + name] = remote(
+                place(slot, dev), place(slot, dev), send.at[7 + index], recv.at[7 + index], to_p
+            )
+        self.copies = copies
+
+    def start(self):
+        for name in ("y0", "x1", "x0", "y1", "p"):
+            self.copies[name].start()
+        self.local.start()
+
+    def pass_on(self, arrived, sends):
+        self.copies[arrived].wait_recv()
+        for name in sends:
+            self.copies[name].start()
+
+    def first(self):
+        self.pass_on("y0", ("d0", "py0"))
+        self.pass_on("x1", ("d1", "px1"))
+
+    def second(self):
+        self.pass_on("x0", ("px0",))
+        self.pass_on("y1", ("py1",))
+
+    def third(self):
+        self.pass_on("d0", ("pd0",))
+        self.pass_on("d1", ("pd1",))
+
+    def finish(self):
+        for name in ("p", "px0", "px1", "py0", "py1", "pd0", "pd1"):
+            self.copies[name].wait_recv()
+        for copy in self.copies.values():
+            copy.wait_send()
+        self.local.wait()
+
+
+def wide_square(own_places):
+    _own, pair, ax, ay, _dg = own_places
+    return [{"wide": pair}, {"wide": ax}, {"wide": ay}]
+
+
+def gather_body(count, *refs):
+    srcs, dsts = refs[:count], refs[count : 2 * count]
+    send, recv, local = refs[2 * count :]
+    greet(wide_square(square_places()))
+    parts = [
+        SquareGather(srcs[i], dsts[i], send.at[i], recv.at[i], local.at[i]) for i in range(count)
+    ]
+    for part in parts:
+        part.start()
+    for part in parts:
+        part.first()
+    for part in parts:
+        part.second()
+    for part in parts:
+        part.third()
+    for part in parts:
+        part.finish()
+
+
+def square_gather(*arrays):
+    count = len(arrays)
+    width = arrays[0].shape[-1]
+    shape = jax.ShapeDtypeStruct((2, 8 * BLK, width), arrays[0].dtype)
+    return pl.pallas_call(
+        functools.partial(gather_body, count),
+        out_shape=[shape] * count,
+        in_specs=[vmem()] * count,
+        out_specs=[hbm()] * count,
+        scratch_shapes=[
+            pltpu.SemaphoreType.DMA((count, SquareGather.SENDS)),
+            pltpu.SemaphoreType.DMA((count, SquareGather.SENDS)),
+            pltpu.SemaphoreType.DMA((count,)),
+        ],
+        compiler_params=pltpu.CompilerParams(collective_id=count, has_side_effects=True),
+        name="square_gather" + str(count),
+    )(*arrays)
+
+
+def add_rows(dst, first, second, third=None):
+    step = 16
+
+    def body(index, carry):
+        rows = pl.ds(pl.multiple_of(index * step, step), step)
+        total = first[rows].astype(F32) + second[rows].astype(F32)
+        if third is not None:
+            total = total + third[rows].astype(F32)
+        dst[rows] = total.astype(dst.dtype)
+        return carry
+
+    lax.fori_loop(0, BLK // step, body, 0)
+
+
+class SquareScatter:
+    SENDS = 14
+
+    def __init__(self, src, out, from_pair, summed, from_x, from_y, send, recv):
+        own, pair, ax, ay, dg = square_places()
+        shift = pair - own
+        to_x, to_y, to_p = {"wide": ax}, {"wide": ay}, {"wide": pair}
+        self.src, self.out = src, out
+        self.from_pair, self.summed, self.from_x, self.from_y = from_pair, summed, from_x, from_y
+        self.dests = (dg, ax, ay, own)
+
+        self.order = ((0, 0), (0, 1), (1, 0), (2, 1), (2, 0), (1, 1), (3, 0), (3, 1))
+        self.pair_copies = {}
+        for index, (chip, slot) in enumerate(self.order):
+            self.pair_copies[chip, slot] = remote(
+                self.block(slot, self.dests[chip] + shift),
+                from_pair.at[chip, slot],
+                send.at[index],
+                recv.at[index],
+                to_p,
+            )
+        self.dx = remote(summed.at[0, 0], from_x.at[0], send.at[8], recv.at[8], to_x)
+        self.dy = remote(summed.at[0, 1], from_y.at[0], send.at[9], recv.at[9], to_y)
+        self.xx = remote(summed.at[1, 0], from_x.at[1], send.at[10], recv.at[10], to_x)
+        self.yy = remote(summed.at[2, 1], from_y.at[1], send.at[11], recv.at[11], to_y)
+        self.ty = remote(summed.at[2, 0], from_y.at[2], send.at[12], recv.at[12], to_y)
+        self.tx = remote(summed.at[1, 1], from_x.at[2], send.at[13], recv.at[13], to_x)
+
+    def block(self, slot, dev):
+        return self.src.at[slot, pl.ds(pl.multiple_of(dev * BLK, BLK), BLK)]
+
+    def start(self):
+        for key in self.order:
+            self.pair_copies[key].start()
+
+    def pair_sum(self, chip, slot):
+        self.pair_copies[chip, slot].wait_recv()
+        add_rows(
+            self.summed.at[chip, slot],
+            self.block(slot, self.dests[chip]),
+            self.from_pair.at[chip, slot],
+        )
+
+    def first(self):
+        self.pair_sum(0, 0)
+        self.dx.start()
+        self.pair_sum(0, 1)
+        self.dy.start()
+        self.pair_sum(1, 0)
+        self.xx.start()
+        self.pair_sum(2, 1)
+        self.yy.start()
+
+    def middle(self):
+        self.pair_copies[2, 0].wait_recv()
+        self.dx.wait_recv()
+        _own, _pair, _ax, ay, _dg = square_places()
+        add_rows(
+            self.summed.at[2, 0], self.block(0, ay), self.from_pair.at[2, 0], self.from_x.at[0]
+        )
+        self.ty.start()
+        self.pair_copies[1, 1].wait_recv()
+        self.dy.wait_recv()
+        add_rows(
+            self.summed.at[1, 1],
+            self.block(1, self.dests[1]),
+            self.from_pair.at[1, 1],
+            self.from_y.at[0],
+        )
+        self.tx.start()
+
+    def own_sums(self):
+        self.pair_sum(3, 0)
+        self.pair_sum(3, 1)
+
+    def finish(self):
+        self.xx.wait_recv()
+        self.ty.wait_recv()
+        add_rows(self.out.at[0], self.summed.at[3, 0], self.from_x.at[1], self.from_y.at[2])
+        self.yy.wait_recv()
+        self.tx.wait_recv()
+        add_rows(self.out.at[1], self.summed.at[3, 1], self.from_y.at[1], self.from_x.at[2])
+        for copy in self.pair_copies.values():
+            copy.wait_send()
+        for copy in (self.dx, self.dy, self.xx, self.yy, self.ty, self.tx):
+            copy.wait_send()
+
+
+def scatter_scratch(count, width):
+    return [
+        pltpu.VMEM((count, 4, 2, BLK, width), BF),
+        pltpu.VMEM((count, 4, 2, BLK, width), BF),
+        pltpu.VMEM((count, 3, BLK, width), BF),
+        pltpu.VMEM((count, 3, BLK, width), BF),
+        pltpu.SemaphoreType.DMA((count, SquareScatter.SENDS)),
+        pltpu.SemaphoreType.DMA((count, SquareScatter.SENDS)),
+    ]
+
+
+def scatter_parts(srcs, outs, scratch):
+    return [
+        SquareScatter(srcs[i], outs[i], *[buffer.at[i] for buffer in scratch])
+        for i in range(len(srcs))
+    ]
+
+
+def scatter_body(count, *refs):
+    srcs, outs = refs[:count], refs[count : 2 * count]
+    greet(wide_square(square_places()))
+    parts = scatter_parts(srcs, outs, refs[2 * count :])
+    for part in parts:
+        part.start()
+    for part in parts:
+        part.first()
+    for part in parts:
+        part.middle()
+    for part in parts:
+        part.own_sums()
+    for part in parts:
+        part.finish()
+
+
+def square_scatter(*arrays):
+    count = len(arrays)
+    width = arrays[0].shape[-1]
+    shape = jax.ShapeDtypeStruct((2, BLK, width), F32)
+    return pl.pallas_call(
+        functools.partial(scatter_body, count),
+        out_shape=[shape] * count,
+        in_specs=[vmem()] * count,
+        out_specs=[vmem()] * count,
+        scratch_shapes=scatter_scratch(count, width),
+        compiler_params=pltpu.CompilerParams(collective_id=4 + count, has_side_effects=True),
+        name="square_scatter" + str(count),
+    )(*arrays)
+
+
+def wide_others(own):
+    return [{"wide": (own + step) % 8} for step in range(1, 8)]
+
+
+def first_body(
+    depth,
+    hidden,
+    attn_w,
+    ffn_w,
+    vec,
+    hidden_all,
+    attn_all,
+    ffn_all,
+    vec_all,
+    attn_z,
+    vec_z,
+    send,
+    recv,
+    local,
+    z_send,
+    z_recv,
+    a_send,
+    a_recv,
+    f_send,
+    f_recv,
+    v_send,
+    v_recv,
+    own_sems,
+):
+    own, pair, ax, ay, dg = square_places()
+    layer = lax.axis_index("tp")
+    greet(wide_others(own) + [{"tp": (layer + step) % depth} for step in range(1, depth)])
+    gather = SquareGather(hidden, hidden_all, send, recv, local.at[0])
+    gather.start()
+
+    def up_copies(step):
+        index = layer - step + 1
+        sem = step - 1
+        src_w = attn_w if step == 1 else attn_z.at[index]
+        src_v = vec if step == 1 else vec_z.at[index]
+        up = {"tp": layer + 1}
+        return (
+            remote(src_w, attn_z.at[index], z_send.at[0, sem], z_recv.at[0, sem], up),
+            remote(src_v, vec_z.at[index], z_send.at[1, sem], z_recv.at[1, sem], up),
+        )
+
+    def down_copies(step):
+        index = layer + step - 1
+        sem = step - 1
+        src_w = attn_w if step == 1 else attn_z.at[index]
+        src_v = vec if step == 1 else vec_z.at[index]
+        down = {"tp": layer - 1}
+        return (
+            remote(src_w, attn_z.at[index], z_send.at[2, sem], z_recv.at[2, sem], down),
+            remote(src_v, vec_z.at[index], z_send.at[3, sem], z_recv.at[3, sem], down),
+        )
+
+    def z_start(step):
+        @pl.when((layer < depth - 1) & (layer - step + 1 >= 0))
+        def _():
+            for copy in up_copies(step):
+                copy.start()
+
+        @pl.when((layer > 0) & (layer + step - 1 < depth))
+        def _():
+            for copy in down_copies(step):
+                copy.start()
+
+    def z_arrive(step):
+        @pl.when(layer - step >= 0)
+        def _():
+            for copy in up_copies(step):
+                copy.wait_recv()
+
+        @pl.when(layer + step < depth)
+        def _():
+            for copy in down_copies(step):
+                copy.wait_recv()
+
+    def z_sent(step):
+        @pl.when((layer < depth - 1) & (layer - step + 1 >= 0))
+        def _():
+            for copy in up_copies(step):
+                copy.wait_send()
+
+        @pl.when((layer > 0) & (layer + step - 1 < depth))
+        def _():
+            for copy in down_copies(step):
+                copy.wait_send()
+
+    z_start(1)
+    own_z = [
+        pltpu.make_async_copy(attn_w, attn_z.at[layer], own_sems.at[0]),
+        pltpu.make_async_copy(vec, vec_z.at[layer], own_sems.at[1]),
+    ]
+    for copy in own_z:
+        copy.start()
+    gather.first()
+    ffn_own = pltpu.make_async_copy(ffn_w.at[own], ffn_all.at[:, own], own_sems.at[2])
+    ffn_own.start()
+    ffn_copies = []
+    for step in range(1, 8):
+        there = (own + step) % 8
+        ffn_copies.append(
+            remote(
+                ffn_w.at[there],
+                ffn_all.at[:, own],
+                f_send.at[step - 1],
+                f_recv.at[step - 1],
+                {"wide": there},
+            )
+        )
+    for copy in ffn_copies:
+        copy.start()
+    z_arrive(1)
+    if depth > 2:
+        z_start(2)
+    gather.second()
+    if depth > 2:
+        z_arrive(2)
+    if depth > 3:
+        z_start(3)
+    gather.third()
+    if depth > 3:
+        z_arrive(3)
+    for copy in own_z:
+        copy.wait()
+    per_layer = 8 // depth
+    attn_own = pltpu.make_async_copy(
+        attn_z.at[own // per_layer, own % per_layer], attn_all.at[:, own], own_sems.at[3]
+    )
+    attn_own.start()
+    vec_own = pltpu.make_async_copy(vec_z, vec_all.at[own], own_sems.at[4])
+    vec_own.start()
+    late = []
+    for step in range(1, 8):
+        there = (own + step) % 8
+        late.append(
+            remote(vec_z, vec_all.at[own], v_send.at[step - 1], v_recv.at[step - 1], {"wide": there})
+        )
+        late.append(
+            remote(
+                attn_z.at[there // per_layer, there % per_layer],
+                attn_all.at[:, own],
+                a_send.at[step - 1],
+                a_recv.at[step - 1],
+                {"wide": there},
+            )
+        )
+    for copy in late:
+        copy.start()
+    gather.finish()
+    for copy in ffn_copies + late:
+        copy.wait_recv()
+    for copy in ffn_copies + late:
+        copy.wait_send()
+    ffn_own.wait()
+    attn_own.wait()
+    vec_own.wait()
+    for step in range(1, depth):
+        z_sent(step)
+
+
+def first_exchange(depth, hidden, attn_w, ffn_w, vec):
+    width = hidden.shape[-1]
+    dma = pltpu.SemaphoreType.DMA
+    return pl.pallas_call(
+        functools.partial(first_body, depth),
+        out_shape=[
+            jax.ShapeDtypeStruct((2, 8 * BLK, width), BF),
+            jax.ShapeDtypeStruct((4, 8, BLK, BLK), BF),
+            jax.ShapeDtypeStruct((2, 8, BLK, BLK), BF),
+            jax.ShapeDtypeStruct((8, depth) + vec.shape, F32),
+        ],
+        in_specs=[vmem()] * 4,
+        out_specs=[hbm(), hbm(), hbm(), vmem()],
+        scratch_shapes=[
+            pltpu.VMEM((depth,) + attn_w.shape, BF),
+            pltpu.VMEM((depth,) + vec.shape, F32),
+            dma((SquareGather.SENDS,)),
+            dma((SquareGather.SENDS,)),
+            dma((1,)),
+            dma((4, depth - 1)),
+            dma((4, depth - 1)),
+            dma((7,)),
+            dma((7,)),
+            dma((7,)),
+            dma((7,)),
+            dma((7,)),
+            dma((7,)),
+            dma((5,)),
+        ],
+        compiler_params=pltpu.CompilerParams(collective_id=10, has_side_effects=True),
+        name="first_exchange",
+    )(hidden, attn_w, ffn_w, vec)
+
+
+def last_body(
+    depth,
+    shares,
+    attn_g,
+    ffn_g,
+    rows_out,
+    attn_out,
+    ffn_out,
+    attn_in,
+    attn_z,
+    from_pair,
+    summed,
+    from_x,
+    from_y,
+    s_send,
+    s_recv,
+    a_send,
+    a_recv,
+    z_send,
+    z_recv,
+    f_send,
+    f_recv,
+    own_sems,
+):
+    own, pair, ax, ay, dg = square_places()
+    layer = lax.axis_index("tp")
+    per_layer = 8 // depth
+    greet(wide_others(own) + [{"tp": (layer + step) % depth} for step in range(1, depth)])
+    scatter = scatter_parts(
+        [shares], [rows_out], (from_pair, summed, from_x, from_y, s_send, s_recv)
+    )[0]
+    scatter.start()
+    attn_copies = []
+    for step in range(1, 8):
+        there = (own + step) % 8
+        attn_copies.append(
+            remote(
+                attn_g.at[there],
+                attn_in.at[own],
+                a_send.at[step - 1],
+                a_recv.at[step - 1],
+                {"wide": there},
+            )
+        )
+    for copy in attn_copies:
+        copy.start()
+    own_copy = pltpu.make_async_copy(attn_g.at[own], attn_in.at[own], own_sems.at[0])
+    own_copy.start()
+    scatter.first()
+
+    def onward(index):
+        goal = index // per_layer
+        piece = index % per_layer
+        return remote(
+            attn_in.at[index],
+            attn_z.at[layer, piece],
+            z_send.at[index],
+            z_recv.at[layer, piece],
+            {"tp": goal},
+        )
+
+    def forward(index):
+        @pl.when(index // per_layer != layer)
+        def _():
+            onward(index).start()
+
+    own_copy.wait()
+    forward(own)
+    for step in range(1, 8):
+        attn_copies[step - 1].wait_recv()
+        forward((own + 8 - step) % 8)
+    ffn_own = pltpu.make_async_copy(ffn_g.at[own], ffn_out.at[own], own_sems.at[1])
+    ffn_own.start()
+    ffn_copies = []
+    for step in range(1, 8):
+        there = (own + step) % 8
+        ffn_copies.append(
+            remote(
+                ffn_g.at[there],
+                ffn_out.at[own],
+                f_send.at[step - 1],
+                f_recv.at[step - 1],
+                {"wide": there},
+            )
+        )
+    scatter.middle()
+    for copy in ffn_copies:
+        copy.start()
+    scatter.own_sums()
+    scatter.finish()
+    for step in range(1, depth):
+        source = (layer + step) % depth
+        for piece in range(per_layer):
+            remote(
+                attn_in.at[piece],
+                attn_z.at[source, piece],
+                z_send.at[piece],
+                z_recv.at[source, piece],
+                {"tp": source},
+            ).wait_recv()
+    for piece in range(per_layer):
+        for kind in range(4):
+            total = attn_in[layer * per_layer + piece, kind].astype(F32)
+            for step in range(1, depth):
+                total = total + attn_z[(layer + step) % depth, piece, kind].astype(F32)
+            attn_out[piece, kind] = total
+    for copy in attn_copies:
+        copy.wait_send()
+    for index in range(8):
+        @pl.when(index // per_layer != layer)
+        def _(index=index):
+            onward(index).wait_send()
+
+    for copy in ffn_copies:
+        copy.wait_recv()
+    for copy in ffn_copies:
+        copy.wait_send()
+    ffn_own.wait()
+
+
+def last_exchange(depth, shares, attn_g, ffn_g):
+    width = shares.shape[-1]
+    dma = pltpu.SemaphoreType.DMA
+    per_layer = 8 // depth
+    return pl.pallas_call(
+        functools.partial(last_body, depth),
+        out_shape=[
+            jax.ShapeDtypeStruct((2, BLK, width), F32),
+            jax.ShapeDtypeStruct((per_layer, 4, BLK, BLK), F32),
+            jax.ShapeDtypeStruct((8, 2, BLK, BLK), BF),
+        ],
+        in_specs=[vmem()] * 3,
+        out_specs=[vmem()] * 3,
+        scratch_shapes=[
+            pltpu.VMEM((8, 4, BLK, BLK), BF),
+            pltpu.VMEM((depth, per_layer, 4, BLK, BLK), BF),
+        ]
+        + scatter_scratch(1, width)
+        + [
+            dma((7,)),
+            dma((7,)),
+            dma((8,)),
+            dma((depth, per_layer)),
+            dma((7,)),
+            dma((7,)),
+            dma((2,)),
+        ],
+        compiler_params=pltpu.CompilerParams(collective_id=11, has_side_effects=True),
+        name="last_exchange",
+    )(shares, attn_g, ffn_g)
+
+
+def sums_body(depth, parts, gathered, send, recv, local):
+    own = lax.axis_index("wide")
+    layer = lax.axis_index("tp")
+    others = []
+    for up in range(depth):
+        for step in range(8):
+            if up or step:
+                others.append(((own + step) % 8, (layer + up) % depth))
+    greet([{"wide": wide, "tp": tp} for wide, tp in others])
+    keep = pltpu.make_async_copy(parts.at[own], gathered.at[own, layer], local.at[0])
+    keep.start()
+    copies = [
+        remote(
+            parts.at[wide],
+            gathered.at[own, layer],
+            send.at[index],
+            recv.at[index],
+            {"wide": wide, "tp": tp},
+        )
+        for index, (wide, tp) in enumerate(others)
+    ]
+    for copy in copies:
+        copy.start()
+    for copy in copies:
+        copy.wait_recv()
+    for copy in copies:
+        copy.wait_send()
+    keep.wait()
+
+
+def share_sums(depth, parts):
+    dma = pltpu.SemaphoreType.DMA
+    return pl.pallas_call(
+        functools.partial(sums_body, depth),
+        out_shape=jax.ShapeDtypeStruct((8, depth) + parts.shape[1:], F32),
+        in_specs=[vmem()],
+        out_specs=vmem(),
+        scratch_shapes=[dma((8 * depth - 1,)), dma((8 * depth - 1,)), dma((1,))],
+        compiler_params=pltpu.CompilerParams(collective_id=12, has_side_effects=True),
+        name="share_sums",
+    )(parts)
+
+
+def head_bias(length, slope, rows):
+    place = lax.broadcasted_iota(jnp.int32, (rows, QB), 0)
+    bias = slope * place.astype(F32)
+    return jnp.where(place < length, bias, NEG)
+
+
+QB = 256
+
+
+def dot_nt(first, second):
+    return lax.dot_general(first, second, (((1,), (1,)), ((), ())), preferred_element_type=F32)
+
+
+def dot_nn(first, second):
+    return lax.dot_general(first, second, (((1,), (0,)), ((), ())), preferred_element_type=F32)
+
+
+def later_key(size):
+    key_place = lax.broadcasted_iota(jnp.int32, (size, size), 0)
+    query_place = lax.broadcasted_iota(jnp.int32, (size, size), 1)
+    return key_place > query_place
+
+
+def attend_body(lengths, slopes, qkv, out, totals, bias):
+    slot = pl.program_id(0)
+    rows = qkv.shape[1]
+    length = lengths[slot]
+    scale = 0.125 * LOG2E
+    for head in range(2):
+        lanes = pl.ds(head * HEAD, HEAD)
+        bias[...] = head_bias(length, slopes[head], rows)
+        key = qkv[0, :, pl.ds(2 * HEAD + head * HEAD, HEAD)]
+        value = qkv[0, :, pl.ds(4 * HEAD + head * HEAD, HEAD)]
+        value_t = value.T
+        for step in range(rows // QB):
+            here = pl.ds(step * QB, QB)
+            extent = (step + 1) * QB
+            query = qkv[0, here, lanes]
+            scores = dot_nt(key[:extent], query) * scale + bias[:extent]
+            low_part = jnp.where(later_key(QB), NEG, scores[extent - QB :])
+            scores = low_part if step == 0 else jnp.concatenate([scores[: extent - QB], low_part], 0)
+            highest = jnp.max(scores, axis=0, keepdims=True)
+            weights = jnp.exp2(scores - highest)
+            total = jnp.sum(weights, axis=0, keepdims=True)
+            mixed = dot_nn(value_t[:, :extent], weights.astype(BF)) / total
+            out[0, here, lanes] = mixed.T.astype(BF)
+            totals[0, pl.ds(head, 1), here] = highest + jnp.log2(total)
+
+
+def attend(lengths, slopes, qkv):
+    slots, rows, _width = qkv.shape
+    return pl.pallas_call(
+        attend_body,
+        grid=(slots,),
+        out_shape=[
+            jax.ShapeDtypeStruct((slots, rows, 2 * HEAD), BF),
+            jax.ShapeDtypeStruct((slots, 2, rows), F32),
+        ],
+        in_specs=[
+            pl.BlockSpec(memory_space=pltpu.SMEM),
+            pl.BlockSpec(memory_space=pltpu.SMEM),
+            pl.BlockSpec((1, rows, 6 * HEAD), lambda s: (s, 0, 0)),
+        ],
+        out_specs=[
+            pl.BlockSpec((1, rows, 2 * HEAD), lambda s: (s, 0, 0)),
+            pl.BlockSpec((1, 2, rows), lambda s: (s, 0, 0)),
+        ],
+        scratch_shapes=[pltpu.VMEM((rows, QB), F32)],
+        name="attend",
+    )(lengths, slopes, qkv)
+
+
+def attend_back_body(lengths, slopes, qkv, attention, grad, totals, out, bias, key_sum, value_sum):
+    slot = pl.program_id(0)
+    rows = qkv.shape[1]
+    length = lengths[slot]
+    scale = 0.125 * LOG2E
+    for head in range(2):
+        lanes = pl.ds(head * HEAD, HEAD)
+        key_lanes = pl.ds(2 * HEAD + head * HEAD, HEAD)
+        value_lanes = pl.ds(4 * HEAD + head * HEAD, HEAD)
+        bias[...] = head_bias(length, slopes[head], rows)
+        key = qkv[0, :, key_lanes]
+        value = qkv[0, :, value_lanes]
+        key_t = key.T
+        key_sum[...] = jnp.zeros_like(key_sum)
+        value_sum[...] = jnp.zeros_like(value_sum)
+        for step in range(rows // QB):
+            here = pl.ds(step * QB, QB)
+            extent = (step + 1) * QB
+            query = qkv[0, here, lanes]
+            grad_rows = grad[0, here, lanes]
+            product = grad_rows.astype(F32) * attention[0, here, lanes].astype(F32)
+            delta = jnp.sum(product.T, axis=0, keepdims=True)
+            scores = dot_nt(key[:extent], query) * scale + bias[:extent]
+            low_part = jnp.where(later_key(QB), NEG, scores[extent - QB :])
+            scores = low_part if step == 0 else jnp.concatenate([scores[: extent - QB], low_part], 0)
+            probs = jnp.exp2(scores - totals[0, pl.ds(head, 1), here])
+            grad_probs = dot_nt(value[:extent], grad_rows)
+            grad_scores = (probs * (grad_probs - delta)).astype(BF)
+            span = pl.ds(0, extent)
+            value_sum[span] += dot_nn(probs.astype(BF), grad_rows)
+            key_sum[span] += dot_nn(grad_scores, query)
+            grad_query = dot_nn(key_t[:, :extent], grad_scores)
+            out[0, here, lanes] = (grad_query.T * 0.125).astype(BF)
+        out[0, :, key_lanes] = (key_sum[...] * 0.125).astype(BF)
+        out[0, :, value_lanes] = value_sum[...].astype(BF)
+
+
+def attend_back(lengths, slopes, qkv, attention, grad, totals):
+    slots, rows, _width = qkv.shape
+    return pl.pallas_call(
+        attend_back_body,
+        grid=(slots,),
+        out_shape=jax.ShapeDtypeStruct((slots, rows, 6 * HEAD), BF),
+        in_specs=[
+            pl.BlockSpec(memory_space=pltpu.SMEM),
+            pl.BlockSpec(memory_space=pltpu.SMEM),
+            pl.BlockSpec((1, rows, 6 * HEAD), lambda s: (s, 0, 0)),
+            pl.BlockSpec((1, rows, 2 * HEAD), lambda s: (s, 0, 0)),
+            pl.BlockSpec((1, rows, 2 * HEAD), lambda s: (s, 0, 0)),
+            pl.BlockSpec((1, 2, rows), lambda s: (s, 0, 0)),
+        ],
+        out_specs=pl.BlockSpec((1, rows, 6 * HEAD), lambda s: (s, 0, 0)),
+        scratch_shapes=[
+            pltpu.VMEM((rows, QB), F32),
+            pltpu.VMEM((rows, HEAD), F32),
+            pltpu.VMEM((rows, HEAD), F32),
+        ],
+        name="attend_back",
+    )(lengths, slopes, qkv, attention, grad, totals)
+
+
+def norm_stats(values):
+    middle = jnp.mean(values, axis=-1, keepdims=True)
+    centred = values - middle
+    spread = jnp.mean(centred * centred, axis=-1, keepdims=True)
+    inverse = lax.rsqrt(spread + 1e-05)
+    return centred * inverse, inverse
+
+
+def norm_back_rows(grad, hat, inverse, gain):
+    scaled = grad * gain
+    first = jnp.mean(scaled, axis=-1, keepdims=True)
+    second = jnp.mean(scaled * hat, axis=-1, keepdims=True)
+    return (scaled - first - hat * second) * inverse
+
+
+def gelu_parts(values):
+    root = math.sqrt(2 / math.pi)
+    squared = values * values
+    inner = jnp.tanh(root * values * (1.0 + 0.044715 * squared))
+    half = 0.5 * (1.0 + inner)
+    slope = half + 0.5 * values * (1.0 - inner * inner) * root * (1.0 + 3 * 0.044715 * squared)
+    return values * half, slope
+
+
+def square_device(
+    hidden_in,
+    lengths,
+    pre_gain,
+    pre_shift,
+    w_query,
+    w_key,
+    w_value,
+    b_query,
+    b_value,
+    w_dense,
+    b_dense,
+    mid_gain,
+    mid_shift,
+    w_up,
+    b_up,
+    w_down,
+    b_down,
+    cotangent,
+):
+    depth = lax.axis_size("tp")
+    own = lax.axis_index("wide")
+    layer = lax.axis_index("tp")
+    width = hidden_in.shape[-1]
+    rows = 8 * BLK
+    per_layer = 8 // depth
+    heads_dev = b_query.shape[0]
+    own_lengths = lax.dynamic_slice_in_dim(lengths, layer * 2, 2, 0)
+    head_index = 2 * own + jnp.arange(2, dtype=jnp.int32)
+    slopes = jnp.exp2(-0.5 * (head_index.astype(F32) + 1.0)) * LOG2E
+
+    def halves(weight):
+        return weight.reshape(BLK, per_layer, BLK).transpose(1, 0, 2)
+
+    attn_w = jnp.stack(
+        [halves(w_query), halves(w_key), halves(w_value), w_dense.reshape(per_layer, BLK, BLK)], 1
+    )
+    ffn_w = jnp.stack(
+        [w_up.reshape(BLK, 8, BLK).transpose(1, 0, 2), w_down.reshape(8, BLK, BLK)], 1
+    )
+    head_row = jnp.concatenate(
+        [b_query.reshape(-1), b_value.reshape(-1), jnp.zeros((BLK - 16 * heads_dev,), BF)]
+    )
+    vec = jnp.stack(
+        [pre_gain, pre_shift, mid_gain, mid_shift, b_dense, b_down, b_up.reshape(-1), head_row]
+    ).astype(F32)
+    hidden_all, attn_all, ffn_all, vec_all = first_exchange(depth, hidden_in, attn_w, ffn_w, vec)
+    ffn_z = lax.all_gather(ffn_all, "tp", axis=0, tiled=False)
+
+    def wide_vector(index):
+        return vec_all[:, 0, index].reshape(width)
+
+    gain_one, shift_one, gain_two, shift_two, dense_b, down_b = [wide_vector(i) for i in range(6)]
+    up_b = vec_all[:, :, 6].reshape(8, depth, heads_dev, 4 * 8).transpose(1, 2, 0, 3)
+    up_b = lax.dynamic_index_in_dim(up_b.reshape(depth, 8, BLK), own, 1, False).reshape(-1)
+    span = heads_dev * 8
+
+    def head_vector(index):
+        full = vec_all[:, :, 7, index * span : (index + 1) * span]
+        full = full.reshape(8, depth, heads_dev, 8).transpose(1, 2, 0, 3).reshape(8, 2 * HEAD)
+        return lax.dynamic_index_in_dim(full, own, 0, False)
+
+    qkv_b = jnp.concatenate([head_vector(0), jnp.zeros((2 * HEAD,), F32), head_vector(1)])
+    qkv_w = attn_all[:3].reshape(3, width, BLK).transpose(1, 0, 2).reshape(width, 3 * BLK)
+    dense_w = attn_all[3].transpose(1, 0, 2).reshape(BLK, width)
+    normed = norm_stats(hidden_all.astype(F32))[0] * gain_one + shift_one
+    normed = normed.astype(BF)
+    qkv = (row_product(normed, qkv_w) + qkv_b).astype(BF)
+    attention, totals = attend(own_lengths, slopes, qkv)
+    branch = square_scatter(row_product(attention, dense_w).astype(BF))[0]
+
+    hidden = hidden_in.astype(F32)
+    residual = hidden + branch + dense_b
+    hat_two, inverse_two = norm_stats(residual)
+    second = (hat_two * gain_two + shift_two).astype(BF)
+    places = own * BLK + jnp.arange(BLK, dtype=jnp.int32)
+    validity = (places[None, :] < own_lengths[:, None]).astype(F32)[:, :, None]
+    grad_output = validity * cotangent.astype(F32)
+    second_all, down_all = square_gather(second, grad_output.astype(BF))
+
+    up_w = ffn_z[:, 0].reshape(depth, width, BLK).transpose(1, 0, 2).reshape(width, depth * BLK)
+    down_w = ffn_z[:, 1].transpose(0, 2, 1, 3).reshape(depth * BLK, width)
+    pre_act = row_product(second_all, up_w) + up_b
+    act_value, act_slope = gelu_parts(pre_act)
+    activated = act_value.astype(BF)
+    grad_pre = (times_transposed(down_all, down_w) * act_slope).astype(BF)
+    down_share = row_product(activated, down_w).astype(BF)
+    second_share = times_transposed(grad_pre, up_w).astype(BF)
+    grad_up = inner_rows(second_all, grad_pre).astype(BF)
+    grad_down = inner_rows(activated, down_all).astype(BF)
+    grad_up_b = jnp.sum(flatten_rows(grad_pre), axis=0, dtype=F32)
+    ffn_g = jnp.stack(
+        [
+            grad_up.reshape(8, BLK, depth, BLK).transpose(2, 0, 1, 3),
+            grad_down.reshape(depth, BLK, 8, BLK).transpose(0, 2, 1, 3),
+        ],
+        2,
+    )
+    ffn_g = lax.psum_scatter(ffn_g, "tp", scatter_dimension=0, tiled=False)
+    down_out, grad_second = square_scatter(down_share, second_share)
+
+    output = (validity * (residual + down_out + down_b)).astype(BF)
+    grad_resid = grad_output + norm_back_rows(grad_second, hat_two, inverse_two, gain_two)
+    branch_all = square_gather(grad_resid.astype(BF))[0]
+    grad_attention = times_transposed(branch_all, dense_w).astype(BF)
+    grad_dense = inner_rows(attention, branch_all).astype(BF)
+    grad_qkv = attend_back(own_lengths, slopes, qkv, attention, grad_attention, totals)
+    normed_share = times_transposed(grad_qkv, qkv_w).astype(BF)
+    grad_qkv_w = inner_rows(normed, grad_qkv).astype(BF)
+    grad_qkv_b = jnp.sum(flatten_rows(grad_qkv), axis=0, dtype=F32)
+    attn_g = jnp.concatenate(
+        [
+            grad_qkv_w.reshape(8, BLK, 3, BLK).transpose(0, 2, 1, 3),
+            grad_dense.reshape(BLK, 8, BLK).transpose(1, 0, 2)[:, None],
+        ],
+        1,
+    )
+    grad_normed, attn_sum, ffn_sum = last_exchange(depth, normed_share, attn_g, ffn_g)
+
+    hat_one, inverse_one = norm_stats(hidden)
+    grad_in = (grad_resid + norm_back_rows(grad_normed, hat_one, inverse_one, gain_one)).astype(BF)
+
+    def token_sum(values):
+        return jnp.sum(values, axis=(0, 1))
+
+    parts = jnp.stack(
+        [
+            token_sum(grad_normed * hat_one),
+            token_sum(grad_normed),
+            token_sum(grad_resid),
+            token_sum(grad_second * hat_two),
+            token_sum(grad_second),
+            token_sum(grad_output),
+        ]
+    )
+    parts = parts.reshape(6, 8, BLK).transpose(1, 0, 2)
+    own_sums = jnp.concatenate([grad_up_b, grad_qkv_b[: 2 * HEAD], grad_qkv_b[4 * HEAD :]])
+    own_sums = jnp.broadcast_to(own_sums.reshape(1, -1, BLK), (8, depth + 2, BLK))
+    pad = jnp.zeros((8, 16 - 8 - depth, BLK), F32)
+    sums = share_sums(depth, jnp.concatenate([parts, own_sums, pad], 1))
+    vec_sums = jnp.sum(sums[:, :, :6], axis=(0, 1))
+    unit_sums = jnp.sum(sums[:, :, 6 : 8 + depth], axis=1)
+    up_sum = unit_sums[:, :depth].transpose(1, 0, 2).reshape(2 * HEAD // 8, 8 * depth * BLK // 16)
+    head_sums = unit_sums[:, depth:].transpose(1, 0, 2).reshape(2, 16, HEAD)
+
+    def own_block(tensor, size):
+        return lax.dynamic_slice(tensor, (layer * heads_dev, own * size), (heads_dev, size))
+
+    def side_by_side(blocks):
+        return blocks.transpose(1, 0, 2).reshape(BLK, -1)
+
+    ffn_sum = ffn_sum.astype(F32)
+    return (
+        output,
+        grad_in,
+        vec_sums[0],
+        vec_sums[1],
+        side_by_side(attn_sum[:, 0]),
+        side_by_side(attn_sum[:, 1]),
+        side_by_side(attn_sum[:, 2]),
+        own_block(head_sums[0], 8),
+        own_block(head_sums[1], 8),
+        attn_sum[:, 3].reshape(per_layer * BLK, BLK),
+        vec_sums[2],
+        vec_sums[3],
+        vec_sums[4],
+        side_by_side(ffn_sum[:, 0]),
+        own_block(up_sum, 4 * 8),
+        ffn_sum[:, 1].reshape(8 * BLK, BLK),
+        vec_sums[5],
+    )
+
+
 def solution(mesh):
+    square = mesh.shape["wide"] == 8 and mesh.shape["tp"] == 4
     return jax.shard_map(
-        per_device,
+        square_device if square else per_device,
         mesh=mesh,
         in_specs=(
             P("tp", "wide", None),

time: 1200 us -> 400 us (0.33)
  waiting for transfers between devices: 758 us -> 0.06 us
  Pallas kernels: 0 us -> 251 us
  blocking collectives: 172 us -> 0 us
  matrix products: 108 us -> 57.3 us
  local copies, waits for them, and re-layouts: 86.3 us -> 42.3 us
  other arithmetic: 54.7 us -> 30.2 us
    reduce_scatter x9 -> x1, waiting for transfers between devices: 350 us -> 0.01 us  [square_device(): ffn_g = lax.psum_scatter(ffn_g, 'tp', scatter_dimension=0, tiled=False)]
    all_gather x9 -> x1, waiting for transfers between devices: 304 us -> 0.02 us  [square_device(): ffn_z = lax.all_gather(ffn_all, 'tp', axis=0, tiled=False)]
    pallas_call x0 -> x9, Pallas kernels: none -> 251 us  [the longest x2 70.9 us: square_scatter(): pl.pallas_call(functools.partial(scatter_body, count), out_shape=[shape]...]
    all_gather x13 -> x0, blocking collectives: 120 us -> none  [the longest x1 12.5 us: per_device(): lax.all_gather(w_query, 'wide', axis=0, tiled=True)]
    unnamed x24 -> x2, waiting for transfers between devices: 104 us -> 0.03 us
    psum x1 -> x0, blocking collectives: 39.7 us -> none  [per_device(): lax.psum((grad_gain_one, grad_shift_one, grad_dense_b, grad_gain_two, gra...]
    dot_general x18 -> x0, matrix products: 34.6 us -> none  [the longest x6 15.5 us: masked_scores(): jnp.einsum('gihd,gjhd->ghij', query_blk, key_blk, preferred_element_type=...]
    all_gather x2 -> x0, local copies, waits for them, and re-layouts: 23 us -> none  [attention_forward(): pairs_all = lax.all_gather(pairs, 'wide', axis=1, tiled=True)]
  transfers between devices with their start and end apart: 21 -> 2, of which waited for: 21 -> 0; matrix products, arithmetic and copies ran while one was open for 7% -> 17% of each run, Pallas kernels for 0% -> 39%
where the time goes in v1:
time: 400 us; the launch traced here: 395 us
  Pallas kernels  251 us (63%)
  matrix products  57.3 us (14%)
  local copies, waits for them, and re-layouts  42.3 us (11%)
  other arithmetic  30.2 us (8%)
  between operations  14.9 us (4%)
    pallas_call x2, Pallas kernels, square_scatter(): pl.pallas_call(functools.partial(scatter_body, count), out_shape=[shape]...  70.9 us
    pallas_call x2, Pallas kernels, square_gather(): pl.pallas_call(functools.partial(gather_body, count), out_shape=[shape] *...  62.2 us
    pallas_call x1, Pallas kernels, first_exchange(): pl.pallas_call(functools.partial(first_body, depth), out_shape=[jax.Shape...  43.1 us
    pallas_call x1, Pallas kernels, last_exchange(): pl.pallas_call(functools.partial(last_body, depth), out_shape=[jax.ShapeD...  42.2 us
    dot_general x4, matrix products, row_product(): return jnp.dot(first_op, second_op, preferred_element_type=jnp.float32)  22.6 us
    dot_general x4, matrix products, times_transposed(): lax.dot_general(first_op, second_op, (((first_op.ndim - 1,), (1,)), ((),...  18.6 us
    dot_general x4, matrix products, inner_rows(): lax.dot_general(flatten_rows(first_op), flatten_rows(second_op), (((0,),...  16.2 us
    unnamed x44, local copies, waits for them, and re-layouts  13 us
  transfers between devices with their start and end apart: 2, of which 0 were waited for; matrix products, arithmetic and copies ran while one was open for 17% of the time, Pallas kernels for 39%

profile of v1, /device:TPU:0, one launch (start us, length us, event | category | flops | bytes accessed | tf_op | source)
XLA Modules:
  0.0 395.4 jit_solution(5187596181725990501)
XLA Ops:
  7.2 1.1 copy.126
  8.5 1.0 copy.120
  9.6 1.0 copy.122
  10.7 1.0 copy.124
  11.8 0.8 reshape.231
  12.6 0.8 reshape.232
  14.2 0.8 stack.85
  15.6 1.8 pad_maximum_fusion.2.ffn_w
  17.4 1.6 pad_maximum_fusion.3.attn_w
  18.9 43.1 %first_exchange.1 = (bf16[2,1024,1024]{2,1,0:T(8,128)(2,1)}, bf16[4,8,128,128]{3,2,1,0:T(8,128)(2,1)}, bf16[2,8,128,128]{3,2,1,0:T(8,128)(2,1)}, f32[8,4,8,128]{3,2,1,0:T(8,128)}) custom-call(bf16[2,128,1024]{2,1,0:T(8,128)(2,1)} %hidden.1, bf16[2,4,128,128]{3,2,1,0:T(8,128)(2,1)} %pad_maximum_fusion.3.attn_w, ...), custom_call_target="tpu_custom_call" | custom-call | tf_op jit(solution)/shard_map/first_exchange/pallas_call | solution.py:834
  62.1 1.1 slice_reduce_fusion.4
  63.2 1.1 fusion.38
  64.8 3.0 convert_reduce_fusion
  68.2 1.5 fusion.2
  70.2 0.8 copy-done.11
  71.1 6.2 %add_convert_fusion.qkv = bf16[2,1024,384]{2,1,0:T(8,128)(2,1)} fusion(f32[384]{0:T(512)S(1)} %pad_maximum_fusion.4, bf16[1024,384,1]{0,1,2:T(8,128)(2,1)S(1)} %bitcast.190, bf16[2,1024,1024]{2,1,0:T(8,128)(2,1)} %get-tuple-element.30, f32[1024]{0:T(1024)S(1)} %bitcast.226, f32[1024]{0:T(1024)S(1)} %bitcast.213, f32[2,1024]{1,0:T(2,128)S(1)} %add_rsqrt_fusion, ...), kind=kOutput, calls=%fused_computation.14 | convolution fusion | flops 1624768512 | bytes 6579712 | tf_op jit(solution)/shard_map/dot_general | solution.py:27
  78.6 9.2 %attend.1 = (bf16[2,1024,128]{2,1,0:T(8,128)(2,1)}, f32[2,2,1024]{2,1,0:T(2,128)}) custom-call(s32[2]{0:T(128)} %dynamic_slice.23.lengths, f32[2]{0:T(128)} %exponential_multiply_fusion.slopes, bf16[2,1024,384]{2,1,0:T(8,128)(2,1)} %add_convert_fusion.qkv), custom_call_target="tpu_custom_call" | custom-call | tf_op jit(solution)/shard_map/attend/pallas_call | solution.py:1111
  87.8 4.3 %convolution_convert_fusion.3.refs_0_ = bf16[2,1024,1024]{2,1,0:T(8,128)(2,1)} fusion(bf16[2,1024,128]{2,1,0:T(8,128)(2,1)} %get-tuple-element.33.attention, bf16[128,1024,1]{0,1,2:T(8,128)(2,1)S(1)} %bitcast.182), kind=kOutput, calls=%fused_computation.18 | convolution fusion | flops 538968064 | bytes 4980736 | tf_op jit(solution)/shard_map/dot_general | solution.py:27
  92.1 26.8 %square_scatter1.1 = f32[2,128,1024]{2,1,0:T(8,128)} custom-call(bf16[2,1024,1024]{2,1,0:T(8,128)(2,1)} %convolution_convert_fusion.3.refs_0_), custom_call_target="tpu_custom_call" | custom-call | tf_op jit(solution)/shard_map/square_scatter1/pallas_call | solution.py:657
  118.9 1.0 slice_reduce_fusion.2
  120.2 1.6 fusion.34
  122.2 0.9 fusion.30.refs_1_
  123.2 1.0 add_convert_fusion.1.refs_0_
  124.2 39.6 %square_gather2.1 = (bf16[2,1024,1024]{2,1,0:T(8,128)(2,1)}, bf16[2,1024,1024]{2,1,0:T(8,128)(2,1)}) custom-call(bf16[2,128,1024]{2,1,0:T(8,128)(2,1)} %add_convert_fusion.1.refs_0_, bf16[2,128,1024]{2,1,0:T(8,128)(2,1)} %fusion.30.refs_1_), custom_call_target="tpu_custom_call" | custom-call | tf_op jit(solution)/shard_map/square_gather2/pallas_call | solution.py:502
  164.0 2.7 fusion.36
  166.7 0.8 copy.134
  167.5 1.4 reshape.253
  168.9 1.9 copy.182
  170.9 1.3 reshape.254
  172.1 5.0 %fusion.40 = f32[2,1024,512]{2,1,0:T(8,128)S(1)} fusion(bf16[2,1024,1024]{2,1,0:T(8,128)(2,1)} %get-tuple-element.34, bf16[1024,512,1]{1,0,2:T(8,128)(2,1)} %reshape.253), kind=kOutput, calls=%fused_computation.113 | convolution fusion | flops 2147483648 | bytes 9437184 | tf_op jit(solution)/shard_map/dot_general | solution.py:27
  177.1 3.5 fusion.14
  180.7 4.6 %convert_reduce_fusion.1 = (f32[512]{0:T(512)S(1)}, bf16[2,1024,512]{2,1,0:T(8,128)(2,1)S(1)}) fusion(f32[2,1024,512]{2,1,0:T(8,128)S(1)} %fusion.40, f32[512]{0:T(512)S(1)} %bitcast.229, bf16[2,1024,1024]{2,1,0:T(8,128)(2,1)S(1)} %copy-done.14, bf16[512,1024,1]{1,0,2:T(8,128)(2,1)S(1)} %copy-done.8), kind=kOutput, calls=%fused_computation.8 | convolution fusion | flops 2169503232 | bytes 11538432 | tf_op jit(solution)/shard_map/dot_general | solution.py:40
  185.3 3.4 bitcast_convert_fusion.1
  188.7 4.4 %convolution_convert_fusion.1.refs_1_ = bf16[2,1024,1024]{2,1,0:T(8,128)(2,1)} fusion(bf16[2,1024,512]{2,1,0:T(8,128)(2,1)S(1)} %get-tuple-element.136, bf16[1024,512,1]{1,0,2:T(8,128)(2,1)S(1)} %copy-done.10), kind=kOutput, calls=%fused_computation.16 | convolution fusion | flops 2149580800 | bytes 7340032 | tf_op jit(solution)/shard_map/dot_general | solution.py:40
  193.1 1.7 reshape.264
  195.1 1.5 copy.176
  196.9 1.5 pad_maximum_fusion
  198.4 7.0 %convolution_convert_fusion.2.refs_0_ = bf16[2,1024,1024]{2,1,0:T(8,128)(2,1)} fusion(bf16[512,1024,1]{1,0,2:T(8,128)(2,1)S(1)} %copy-done.9, f32[2,1024,512]{2,1,0:T(8,128)} %copy-done.16, f32[512]{0:T(512)S(1)} %bitcast.230), kind=kOutput, calls=%fused_computation.17 | convolution fusion | flops 2160066560 | bytes 9439232 | tf_op jit(solution)/shard_map/dot_general | solution.py:27
  205.5 44.2 %square_scatter2.1 = (f32[2,128,1024]{2,1,0:T(8,128)}, f32[2,128,1024]{2,1,0:T(8,128)}) custom-call(bf16[2,1024,1024]{2,1,0:T(8,128)(2,1)} %convolution_convert_fusion.2.refs_0_, bf16[2,1024,1024]{2,1,0:T(8,128)(2,1)} %convolution_convert_fusion.1.refs_1_), custom_call_target="tpu_custom_call" | custom-call | tf_op jit(solution)/shard_map/square_scatter2/pallas_call | solution.py:657
  249.6 1.7 multiply_reduce_fusion
  251.4 3.0 fusion.33
  254.3 0.9 convert_element_type.103.refs_0_
  255.2 22.6 %square_gather1.1 = bf16[2,1024,1024]{2,1,0:T(8,128)(2,1)} custom-call(bf16[2,128,1024]{2,1,0:T(8,128)(2,1)} %convert_element_type.103.refs_0_), custom_call_target="tpu_custom_call" | custom-call | tf_op jit(solution)/shard_map/square_gather1/pallas_call | solution.py:502
  277.8 4.2 %convolution_convert_fusion.4.grad = bf16[2,1024,128]{2,1,0:T(8,128)(2,1)} fusion(bf16[2,1024,1024]{2,1,0:T(8,128)(2,1)} %square_gather1.1, bf16[128,1024,1]{0,1,2:T(8,128)(2,1)S(1)} %bitcast.183), kind=kOutput, calls=%fused_computation.29 | convolution fusion | flops 537133056 | bytes 4980736 | tf_op jit(solution)/shard_map/dot_general | solution.py:40
  282.0 10.7 %attend_back.1 = bf16[2,1024,384]{2,1,0:T(8,128)(2,1)} custom-call(s32[2]{0:T(128)} %dynamic_slice.23.lengths, f32[2]{0:T(128)} %exponential_multiply_fusion.slopes, bf16[2,1024,384]{2,1,0:T(8,128)(2,1)} %add_convert_fusion.qkv, bf16[2,1024,128]{2,1,0:T(8,128)(2,1)} %get-tuple-element.33.attention, bf16[2,1024,128]{2,1,0:T(8,128)(2,1)} %convolution_convert_fusion.4.grad, ...), custom_call_target="tpu_custom_call" | custom-call | tf_op jit(solution)/shard_map/attend_back/pallas_call | solution.py:1171
  292.7 6.3 %bitcast_convert_fusion.2 = bf16[1024,384]{1,0:T(8,128)(2,1)} fusion(bf16[2,1024,384]{2,1,0:T(8,128)(2,1)} %attend_back.1, bf16[2,1024,1024]{2,1,0:T(8,128)(2,1)} %get-tuple-element.30, f32[1024]{0:T(1024)S(1)} %bitcast.227, f32[1024]{0:T(1024)S(1)} %bitcast.214, f32[2,1024]{1,0:T(2,128)S(1)} %add_rsqrt_fusion, f32[2,1024]{1,0:T(2,128)S(1)} %broadcast_multiply_fusion), kind=kOutput, calls=%fused_computation.24 | convolution fusion | flops 1623588864 | bytes 6578176 | tf_op jit(solution)/shard_map/dot_general | solution.py:31
  299.0 2.4 reshape.263
  301.5 1.1 copy.185
  302.6 2.9 fusion.20
  305.5 0.8 copy.143
  306.4 1.1 copy.144
  307.5 1.7 convert_reduce_fusion.2
  309.2 2.2 pad_maximum_fusion.1.attn_g
  311.4 5.4 %convolution_convert_fusion.shares = bf16[2,1024,1024]{2,1,0:T(8,128)(2,1)} fusion(bf16[2,1024,384]{2,1,0:T(8,128)(2,1)S(1)} %copy-done.3, bf16[1024,384,1]{0,1,2:T(8,128)(2,1)} %bitcast.191), kind=kOutput, calls=%fused_computation.15 | convolution fusion | flops 1612709888 | bytes 6553600 | tf_op jit(solution)/shard_map/dot_general | solution.py:40
  316.8 42.2 %last_exchange.1 = (f32[2,128,1024]{2,1,0:T(8,128)}, f32[2,4,128,128]{3,2,1,0:T(8,128)}, bf16[8,2,128,128]{3,2,1,0:T(8,128)(2,1)}) custom-call(bf16[2,1024,1024]{2,1,0:T(8,128)(2,1)} %convolution_convert_fusion.shares, bf16[8,4,128,128]{3,2,1,0:T(8,128)(2,1)} %pad_maximum_fusion.1.attn_g, bf16[8,2,128,128]{3,2,1,0:T(8,128)(2,1)} %bitcast.196), custom_call_target="tpu_custom_call" | custom-call | tf_op jit(solution)/shard_map/last_exchange/pallas_call | solution.py:989
  359.0 1.8 fusion.26
  361.6 12.3 %share_sums.1 = f32[8,4,16,128]{3,2,1,0:T(8,128)} custom-call(f32[8,16,128]{2,1,0:T(8,128)} %maximum_maximum_fusion.parts), custom_call_target="tpu_custom_call" | custom-call | tf_op jit(solution)/shard_map/share_sums/pallas_call | solution.py:1049
  374.0 1.0 slice_reduce_fusion
  375.0 1.2 convert_element_type.113
  376.3 0.8 slice.141
  377.1 1.0 copy.153
  378.1 2.0 copy.158
  382.2 1.8 fusion.37
  387.2 1.2 fusion.25
  (107 shorter events, 12.1 us)
Async XLA Ops:
  7.2 156.8 %all-gather.3.cloned.1.call-start = ((), (), s32[]{:S(2)}) async-start(), calls=%async_computation.2 | async-start | bytes 2621440 | tf_op jit(solution)/shard_map/all_gather | solution.py:1264
  62.0 254.8 %reduce-scatter.2.cloned.1.call-start = ((), (), s32[]{:S(2)}) async-start(), calls=%async_computation.1 | async-start | bytes 2621440 | tf_op jit(solution)/shard_map/reduce_scatter | solution.py:1315
  64.8 3.5 copy-start
  64.8 5.0 %copy-start.7 = (bf16[4,8,128,128]{3,2,1,0:T(8,128)(2,1)S(1)}, bf16[4,8,128,128]{3,2,1,0:T(8,128)(2,1)}, u32[]{:S(2)}) copy-start(bf16[4,8,128,128]{3,2,1,0:T(8,128)(2,1)} %get-tuple-element.32) | copy-start | bytes 3145732
  70.2 0.9 copy-start.11
  71.1 6.4 %copy-start.15 = (s32[8]{0:T(128)S(1)}, s32[8]{0:T(128)}, u32[]{:S(2)}) copy-start(s32[8]{0:T(128)} %param.19) | copy-start | bytes 100
  87.8 32.3 %copy-start.1 = (bf16[2,128,1024]{2,1,0:T(8,128)(2,1)S(1)}, bf16[2,128,1024]{2,1,0:T(8,128)(2,1)}, u32[]{:S(2)}) copy-start(bf16[2,128,1024]{2,1,0:T(8,128)(2,1)} %hidden.1) | copy-start | bytes 1572868
  92.1 30.0 %copy-start.12 = (s32[2]{0:T(128)S(1)}, s32[2]{0:T(128)}, u32[]{:S(2)}) copy-start(s32[2]{0:T(128)} %dynamic_slice.23.lengths) | copy-start | bytes 28
  92.1 30.1 %copy-start.5 = (bf16[2,128,1024]{2,1,0:T(8,128)(2,1)S(1)}, bf16[2,128,1024]{2,1,0:T(8,128)(2,1)}, u32[]{:S(2)}) copy-start(bf16[2,128,1024]{2,1,0:T(8,128)(2,1)} %param.35) | copy-start | bytes 1572868
  172.1 5.0 %copy-start.14 = (bf16[2,1024,1024]{2,1,0:T(8,128)(2,1)S(1)}, bf16[2,1024,1024]{2,1,0:T(8,128)(2,1)}, u32[]{:S(2)}) copy-start(bf16[2,1024,1024]{2,1,0:T(8,128)(2,1)} %get-tuple-element.36) | copy-start | bytes 12582916
  177.1 3.6 copy-start.16
  177.1 3.5 copy-start.8
  180.7 4.6 %copy-start.13 = (bf16[2,1024,1024]{2,1,0:T(8,128)(2,1)S(1)}, bf16[2,1024,1024]{2,1,0:T(8,128)(2,1)}, u32[]{:S(2)}) copy-start(bf16[2,1024,1024]{2,1,0:T(8,128)(2,1)} %get-tuple-element.34) | copy-start | bytes 12582916
  185.3 3.4 copy-start.10
  196.6 1.8 copy-start.9
  292.7 9.9 %copy-start.2 = (bf16[2,1024,128]{2,1,0:T(8,128)(2,1)S(1)}, bf16[2,1024,128]{2,1,0:T(8,128)(2,1)}, u32[]{:S(2)}) copy-start(bf16[2,1024,128]{2,1,0:T(8,128)(2,1)} %get-tuple-element.33.attention) | copy-start | bytes 1572868
  305.5 5.9 %copy-start.3 = (bf16[2,1024,384]{2,1,0:T(8,128)(2,1)S(1)}, bf16[2,1024,384]{2,1,0:T(8,128)(2,1)}, u32[]{:S(2)}) copy-start(bf16[2,1024,384]{2,1,0:T(8,128)(2,1)} %attend_back.1) | copy-start | bytes 4718596
  359.0 17.2 %copy-start.6 = (bf16[8,2,128,128]{3,2,1,0:T(8,128)(2,1)S(1)}, bf16[8,2,128,128]{3,2,1,0:T(8,128)(2,1)}, u32[]{:S(2)}) copy-start(bf16[8,2,128,128]{3,2,1,0:T(8,128)(2,1)} %get-tuple-element.42) | copy-start | bytes 1572868
  375.0 12.2 %copy-start.4 = (f32[2,128,1024]{2,1,0:T(8,128)S(1)}, f32[2,128,1024]{2,1,0:T(8,128)}, u32[]{:S(2)}) copy-start(f32[2,128,1024]{2,1,0:T(8,128)} %get-tuple-element.40) | copy-start | bytes 3145732
Sparse Core Ops, SparseCore 0:
  62.1 46.7 all-gather.2
  198.5 42.6 reduce-scatter.1

commit v2 on v1

--- a/solution.py
+++ b/solution.py
@@ -463,11 +463,17 @@
         self.pass_on("d0", ("pd0",))
         self.pass_on("d1", ("pd1",))
 
-    def finish(self):
-        for name in ("p", "px0", "px1", "py0", "py1", "pd0", "pd1"):
+    def arrive(self, *names):
+        for name in names:
             self.copies[name].wait_recv()
+
+    def sent(self):
         for copy in self.copies.values():
             copy.wait_send()
+
+    def finish(self):
+        self.arrive("p", "px0", "px1", "py0", "py1", "pd0", "pd1")
+        self.sent()
         self.local.wait()
 
 
@@ -529,7 +535,7 @@
 
 
 class SquareScatter:
-    SENDS = 14
+    SENDS = 10
 
     def __init__(self, src, out, from_pair, summed, from_x, from_y, send, recv):
         own, pair, ax, ay, dg = square_places()
@@ -538,70 +544,66 @@
         self.src, self.out = src, out
         self.from_pair, self.summed, self.from_x, self.from_y = from_pair, summed, from_x, from_y
         self.dests = (dg, ax, ay, own)
-
-        self.order = ((0, 0), (0, 1), (1, 0), (2, 1), (2, 0), (1, 1), (3, 0), (3, 1))
-        self.pair_copies = {}
-        for index, (chip, slot) in enumerate(self.order):
-            self.pair_copies[chip, slot] = remote(
-                self.block(slot, self.dests[chip] + shift),
-                from_pair.at[chip, slot],
-                send.at[index],
-                recv.at[index],
-                to_p,
+        self.pairs = []
+        for chip in range(4):
+            rows = pl.ds(pl.multiple_of((self.dests[chip] + shift) * BLK, BLK), BLK)
+            self.pairs.append(
+                remote(src.at[:, rows], from_pair.at[chip], send.at[chip], recv.at[chip], to_p)
             )
-        self.dx = remote(summed.at[0, 0], from_x.at[0], send.at[8], recv.at[8], to_x)
-        self.dy = remote(summed.at[0, 1], from_y.at[0], send.at[9], recv.at[9], to_y)
-        self.xx = remote(summed.at[1, 0], from_x.at[1], send.at[10], recv.at[10], to_x)
-        self.yy = remote(summed.at[2, 1], from_y.at[1], send.at[11], recv.at[11], to_y)
-        self.ty = remote(summed.at[2, 0], from_y.at[2], send.at[12], recv.at[12], to_y)
-        self.tx = remote(summed.at[1, 1], from_x.at[2], send.at[13], recv.at[13], to_x)
-
-    def block(self, slot, dev):
-        return self.src.at[slot, pl.ds(pl.multiple_of(dev * BLK, BLK), BLK)]
-
-    def start(self):
-        for key in self.order:
-            self.pair_copies[key].start()
-
-    def pair_sum(self, chip, slot):
-        self.pair_copies[chip, slot].wait_recv()
+        self.dx = remote(summed.at[0, 0], from_x.at[0], send.at[4], recv.at[4], to_x)
+        self.dy = remote(summed.at[0, 1], from_y.at[0], send.at[5], recv.at[5], to_y)
+        self.xx = remote(summed.at[1, 0], from_x.at[1], send.at[6], recv.at[6], to_x)
+        self.yy = remote(summed.at[2, 1], from_y.at[1], send.at[7], recv.at[7], to_y)
+        self.ty = remote(summed.at[2, 0], from_y.at[2], send.at[8], recv.at[8], to_y)
+        self.tx = remote(summed.at[1, 1], from_x.at[2], send.at[9], recv.at[9], to_x)
+
+    def block(self, slot, chip):
+        rows = pl.ds(pl.multiple_of(self.dests[chip] * BLK, BLK), BLK)
+        return self.src.at[slot, rows]
+
+    def pair_sum(self, chip, slot, third=None):
         add_rows(
             self.summed.at[chip, slot],
-            self.block(slot, self.dests[chip]),
+            self.block(slot, chip),
             self.from_pair.at[chip, slot],
-        )
+            third,
+        )
+
+    def near(self, chip):
+        self.pairs[chip].wait_recv()
+        if chip == 0:
+            self.pair_sum(0, 0)
+            self.dx.start()
+            self.pair_sum(0, 1)
+            self.dy.start()
+        elif chip == 1:
+            self.pair_sum(1, 0)
+            self.xx.start()
+        elif chip == 2:
+            self.pair_sum(2, 1)
+            self.yy.start()
+        else:
+            self.pair_sum(3, 0)
+            self.pair_sum(3, 1)
+
+    def middle(self):
+        self.dx.wait_recv()
+        self.pair_sum(2, 0, self.from_x.at[0])
+        self.ty.start()
+        self.dy.wait_recv()
+        self.pair_sum(1, 1, self.from_y.at[0])
+        self.tx.start()
+
+    def start(self):
+        for chip in range(4):
+            self.pairs[chip].start()
 
     def first(self):
-        self.pair_sum(0, 0)
-        self.dx.start()
-        self.pair_sum(0, 1)
-        self.dy.start()
-        self.pair_sum(1, 0)
-        self.xx.start()
-        self.pair_sum(2, 1)
-        self.yy.start()
-
-    def middle(self):
-        self.pair_copies[2, 0].wait_recv()
-        self.dx.wait_recv()
-        _own, _pair, _ax, ay, _dg = square_places()
-        add_rows(
-            self.summed.at[2, 0], self.block(0, ay), self.from_pair.at[2, 0], self.from_x.at[0]
-        )
-        self.ty.start()
-        self.pair_copies[1, 1].wait_recv()
-        self.dy.wait_recv()
-        add_rows(
-            self.summed.at[1, 1],
-            self.block(1, self.dests[1]),
-            self.from_pair.at[1, 1],
-            self.from_y.at[0],
-        )
-        self.tx.start()
+        for chip in range(3):
+            self.near(chip)
 
     def own_sums(self):
-        self.pair_sum(3, 0)
-        self.pair_sum(3, 1)
+        self.near(3)
 
     def finish(self):
         self.xx.wait_recv()
@@ -610,7 +612,7 @@
         self.yy.wait_recv()
         self.tx.wait_recv()
         add_rows(self.out.at[1], self.summed.at[3, 1], self.from_y.at[1], self.from_x.at[2])
-        for copy in self.pair_copies.values():
+        for copy in self.pairs:
             copy.wait_send()
         for copy in (self.dx, self.dy, self.xx, self.yy, self.ty, self.tx):
             copy.wait_send()
@@ -1214,6 +1216,227 @@
     return values * half, slope
 
 
+def relation(index):
+    own = lax.axis_index("wide")
+    core = (own + index) % 2
+    col = (own // 2 + index // 2) % 2
+    row = (own // 4 + index // 4) % 2
+    return row * 4 + col * 2 + core
+
+
+def middle_body(
+    depth,
+    hidden,
+    branch,
+    vectors,
+    up_b,
+    cotangent,
+    valid,
+    down_all,
+    ffn_z,
+    branch_all,
+    down_share,
+    residual,
+    grad_resid,
+    sums,
+    ffn_g,
+    grad_up_b,
+    second_all,
+    second_share,
+    up_w,
+    down_w,
+    act_t,
+    pre_t,
+    own_rows,
+    grad_second,
+    from_pair,
+    summed,
+    from_x,
+    from_y,
+    s_send,
+    s_recv,
+    g_send,
+    g_recv,
+    h_send,
+    h_recv,
+    local,
+    w_sems,
+):
+    width = hidden.shape[-1]
+    units = depth * BLK
+    loads = []
+    for up in range(depth):
+        lanes = pl.ds(up * BLK, BLK)
+        for blk in range(8):
+            rows = pl.ds(blk * BLK, BLK)
+            loads.append(
+                pltpu.make_async_copy(ffn_z.at[up, 0, blk], up_w.at[rows, lanes], w_sems.at[0, up * 8 + blk])
+            )
+            loads.append(
+                pltpu.make_async_copy(ffn_z.at[up, 1, blk], down_w.at[lanes, rows], w_sems.at[1, up * 8 + blk])
+            )
+    for load in loads:
+        load.start()
+    greet(wide_square(square_places()))
+    step = 32
+
+    def norm_part(index, carry):
+        rows = pl.ds(pl.multiple_of(index * step, step), step)
+        for slot in range(2):
+            values = hidden[slot, rows].astype(F32) + branch[slot, rows] + vectors[4:5]
+            residual[slot, rows] = values
+            hat, _inverse = norm_stats(values)
+            own_rows[slot, rows] = (hat * vectors[2:3] + vectors[3:4]).astype(BF)
+        return carry
+
+    lax.fori_loop(0, BLK // step, norm_part, 0)
+    gather = SquareGather(own_rows, second_all, g_send, g_recv, local.at[0])
+    gather.start()
+    scatter = SquareScatter(
+        second_share, grad_second, from_pair, summed, from_x, from_y, s_send, s_recv
+    )
+    for load in loads:
+        load.wait()
+
+    def compute(index, carry):
+        source = relation(index)
+        rows = pl.ds(pl.multiple_of(source * BLK, BLK), BLK)
+        values = second_all[:, rows].reshape(2 * BLK, width)
+        pre_act = dot_nn(values, up_w[...]) + up_b[...]
+        act_value, act_slope = gelu_parts(pre_act)
+        activated = act_value.astype(BF)
+        grad_rows = down_all[:, rows].reshape(2 * BLK, width)
+        grad_pre = (dot_nt(grad_rows, down_w[...]) * act_slope).astype(BF)
+        down_share[:, rows] = dot_nn(activated, down_w[...]).astype(BF).reshape(2, BLK, width)
+        second_share[:, rows] = dot_nt(grad_pre, up_w[...]).astype(BF).reshape(2, BLK, width)
+        grad_up_b[...] += jnp.sum(grad_pre.astype(F32), axis=0, keepdims=True)
+        for slot in range(2):
+            lanes = pl.ds(pl.multiple_of(slot * 8 * BLK + source * BLK, BLK), BLK)
+            part = slice(slot * BLK, (slot + 1) * BLK)
+            act_t[:, lanes] = activated[part].T
+            pre_t[:, lanes] = grad_pre[part].T
+        return carry
+
+    grad_up_b[...] = jnp.zeros_like(grad_up_b)
+    gather.arrive("p")
+    gather.local.wait()
+    lax.fori_loop(0, 2, compute, 0)
+    scatter.pairs[3].start()
+    gather.first()
+    gather.second()
+    gather.arrive("px0", "px1", "py0", "py1")
+    lax.fori_loop(2, 4, compute, 0)
+    scatter.pairs[1].start()
+    scatter.near(3)
+    lax.fori_loop(4, 6, compute, 0)
+    scatter.pairs[2].start()
+    gather.third()
+    scatter.near(1)
+    gather.arrive("pd0", "pd1")
+    lax.fori_loop(6, 8, compute, 0)
+    scatter.pairs[0].start()
+    scatter.near(2)
+    scatter.near(0)
+
+    def weight_grads(left, right, kind):
+        def one(up, carry):
+            rows = pl.ds(pl.multiple_of(up * BLK, BLK), BLK)
+            total = dot_nn(left[rows, pl.ds(0, 8 * BLK)], right[0])
+            total = total + dot_nn(left[rows, pl.ds(8 * BLK, 8 * BLK)], right[1])
+            total = total.astype(BF)
+            for blk in range(8):
+                ffn_g[up, blk, kind] = total[:, blk * BLK : (blk + 1) * BLK]
+            return carry
+
+        lax.fori_loop(0, depth, one, 0)
+
+    weight_grads(pre_t, second_all, 0)
+    scatter.middle()
+    weight_grads(act_t, down_all, 1)
+    scatter.finish()
+    gather.sent()
+
+    sums[...] = jnp.zeros_like(sums)
+
+    def back_part(index, carry):
+        rows = pl.ds(pl.multiple_of(index * step, step), step)
+        for slot in range(2):
+            hat, inverse = norm_stats(residual[slot, rows])
+            grad = grad_second[slot, rows]
+            mask = valid[slot, rows][:, :1]
+            grad_out = mask * cotangent[slot, rows].astype(F32)
+            total = grad_out + norm_back_rows(grad, hat, inverse, vectors[2:3])
+            grad_resid[slot, rows] = total
+            own_rows[slot, rows] = total.astype(BF)
+            for place, value in enumerate((total, grad * hat, grad, grad_out)):
+                sums[pl.ds(place, 1)] += jnp.sum(value, axis=0, keepdims=True)
+        return carry
+
+    lax.fori_loop(0, BLK // step, back_part, 0)
+    again = SquareGather(own_rows, branch_all, h_send, h_recv, local.at[1])
+    again.start()
+    again.first()
+    again.second()
+    again.third()
+    again.finish()
+
+
+def middle(depth, hidden, branch, vectors, up_b, cotangent, valid, down_all, ffn_z):
+    width = hidden.shape[-1]
+    units = depth * BLK
+    dma = pltpu.SemaphoreType.DMA
+    tokens = jax.ShapeDtypeStruct((2, 8 * BLK, width), BF)
+    rows = jax.ShapeDtypeStruct((2, BLK, width), F32)
+    return pl.pallas_call(
+        functools.partial(middle_body, depth),
+        out_shape=[
+            tokens,
+            tokens,
+            rows,
+            rows,
+            jax.ShapeDtypeStruct((8, width), F32),
+            jax.ShapeDtypeStruct((depth, 8, 2, BLK, BLK), BF),
+            jax.ShapeDtypeStruct((1, units), F32),
+        ],
+        in_specs=[vmem()] * 7 + [hbm()],
+        out_specs=[hbm()] + [vmem()] * 6,
+        scratch_shapes=[
+            pltpu.VMEM((2, 8 * BLK, width), BF),
+            pltpu.VMEM((2, 8 * BLK, width), BF),
+            pltpu.VMEM((width, units), BF),
+            pltpu.VMEM((units, width), BF),
+            pltpu.VMEM((units, 16 * BLK), BF),
+            pltpu.VMEM((units, 16 * BLK), BF),
+            pltpu.VMEM((2, BLK, width), BF),
+            pltpu.VMEM((2, BLK, width), F32),
+        ]
+        + single_scratch(width)
+        + [
+            dma((SquareGather.SENDS,)),
+            dma((SquareGather.SENDS,)),
+            dma((SquareGather.SENDS,)),
+            dma((SquareGather.SENDS,)),
+            dma((2,)),
+            dma((2, 8 * depth)),
+        ],
+        compiler_params=pltpu.CompilerParams(
+            collective_id=13, has_side_effects=True, vmem_limit_bytes=62 * 1024 * 1024
+        ),
+        name="middle",
+    )(hidden, branch, vectors, up_b, cotangent, valid, down_all, ffn_z)
+
+
+def single_scratch(width):
+    return [
+        pltpu.VMEM((4, 2, BLK, width), BF),
+        pltpu.VMEM((4, 2, BLK, width), BF),
+        pltpu.VMEM((3, BLK, width), BF),
+        pltpu.VMEM((3, BLK, width), BF),
+        pltpu.SemaphoreType.DMA((SquareScatter.SENDS,)),
+        pltpu.SemaphoreType.DMA((SquareScatter.SENDS,)),
+    ]
+
+
 def square_device(
     hidden_in,
     lengths,
@@ -1263,10 +1486,8 @@
     hidden_all, attn_all, ffn_all, vec_all = first_exchange(depth, hidden_in, attn_w, ffn_w, vec)
     ffn_z = lax.all_gather(ffn_all, "tp", axis=0, tiled=False)
 
-    def wide_vector(index):
-        return vec_all[:, 0, index].reshape(width)
-
-    gain_one, shift_one, gain_two, shift_two, dense_b, down_b = [wide_vector(i) for i in range(6)]
+    vectors = vec_all[:, 0].transpose(1, 0, 2).reshape(8, width)
+    gain_one, shift_one = vectors[0], vectors[1]
     up_b = vec_all[:, :, 6].reshape(8, depth, heads_dev, 4 * 8).transpose(1, 2, 0, 3)
     up_b = lax.dynamic_index_in_dim(up_b.reshape(depth, 8, BLK), own, 1, False).reshape(-1)
     span = heads_dev * 8
@@ -1286,38 +1507,25 @@
     branch = square_scatter(row_product(attention, dense_w).astype(BF))[0]
 
     hidden = hidden_in.astype(F32)
-    residual = hidden + branch + dense_b
-    hat_two, inverse_two = norm_stats(residual)
-    second = (hat_two * gain_two + shift_two).astype(BF)
     places = own * BLK + jnp.arange(BLK, dtype=jnp.int32)
     validity = (places[None, :] < own_lengths[:, None]).astype(F32)[:, :, None]
     grad_output = validity * cotangent.astype(F32)
-    second_all, down_all = square_gather(second, grad_output.astype(BF))
-
-    up_w = ffn_z[:, 0].reshape(depth, width, BLK).transpose(1, 0, 2).reshape(width, depth * BLK)
-    down_w = ffn_z[:, 1].transpose(0, 2, 1, 3).reshape(depth * BLK, width)
-    pre_act = row_product(second_all, up_w) + up_b
-    act_value, act_slope = gelu_parts(pre_act)
-    activated = act_value.astype(BF)
-    grad_pre = (times_transposed(down_all, down_w) * act_slope).astype(BF)
-    down_share = row_product(activated, down_w).astype(BF)
-    second_share = times_transposed(grad_pre, up_w).astype(BF)
-    grad_up = inner_rows(second_all, grad_pre).astype(BF)
-    grad_down = inner_rows(activated, down_all).astype(BF)
-    grad_up_b = jnp.sum(flatten_rows(grad_pre), axis=0, dtype=F32)
-    ffn_g = jnp.stack(
-        [
-            grad_up.reshape(8, BLK, depth, BLK).transpose(2, 0, 1, 3),
-            grad_down.reshape(depth, BLK, 8, BLK).transpose(0, 2, 1, 3),
-        ],
-        2,
-    )
+    down_all = square_gather(grad_output.astype(BF))[0]
+    branch_all, down_share, residual, grad_resid, mid_sums, ffn_g, grad_up_b = middle(
+        depth,
+        hidden_in,
+        branch,
+        vectors,
+        up_b.reshape(1, -1),
+        cotangent,
+        jnp.broadcast_to(validity, (2, BLK, BLK)),
+        down_all,
+        ffn_z,
+    )
+    grad_up_b = grad_up_b[0]
     ffn_g = lax.psum_scatter(ffn_g, "tp", scatter_dimension=0, tiled=False)
-    down_out, grad_second = square_scatter(down_share, second_share)
-
-    output = (validity * (residual + down_out + down_b)).astype(BF)
-    grad_resid = grad_output + norm_back_rows(grad_second, hat_two, inverse_two, gain_two)
-    branch_all = square_gather(grad_resid.astype(BF))[0]
+    down_out = square_scatter(down_share)[0]
+    output = (validity * (residual + down_out + vectors[5])).astype(BF)
     grad_attention = times_transposed(branch_all, dense_w).astype(BF)
     grad_dense = inner_rows(attention, branch_all).astype(BF)
     grad_qkv = attend_back(own_lengths, slopes, qkv, attention, grad_attention, totals)
@@ -1339,15 +1547,8 @@
     def token_sum(values):
         return jnp.sum(values, axis=(0, 1))
 
-    parts = jnp.stack(
-        [
-            token_sum(grad_normed * hat_one),
-            token_sum(grad_normed),
-            token_sum(grad_resid),
-            token_sum(grad_second * hat_two),
-            token_sum(grad_second),
-            token_sum(grad_output),
-        ]
+    parts = jnp.concatenate(
+        [jnp.stack([token_sum(grad_normed * hat_one), token_sum(grad_normed)]), mid_sums[:4]]
     )
     parts = parts.reshape(6, 8, BLK).transpose(1, 0, 2)
     own_sums = jnp.concatenate([grad_up_b, grad_qkv_b[: 2 * HEAD], grad_qkv_b[4 * HEAD :]])
@@ -1380,7 +1581,7 @@
         vec_sums[2],
         vec_sums[3],
         vec_sums[4],
-        side_by_side(ffn_sum[:, 0]),
+        ffn_sum[:, 0].reshape(8 * BLK, BLK).T,
         own_block(up_sum, 4 * 8),
         ffn_sum[:, 1].reshape(8 * BLK, BLK),
         vec_sums[5],

time: 400 us -> 354 us (0.89)
  matrix products: 57.3 us -> 24.8 us
  local copies, waits for them, and re-layouts: 42.3 us -> 24.3 us
  Pallas kernels: 251 us -> 267 us
  other arithmetic: 30.2 us -> 22.7 us
    pallas_call x0 -> x1, Pallas kernels: none -> 75.5 us  [middle(): pl.pallas_call(functools.partial(middle_body, depth), out_shape=[tokens,...]
    pallas_call x2 -> x1, Pallas kernels: 62.2 us -> 22.5 us  [square_gather(): pl.pallas_call(functools.partial(gather_body, count), out_shape=[shape] *...]
    pallas_call x2, Pallas kernels: 70.9 us -> 52.7 us  [square_scatter(): pl.pallas_call(functools.partial(scatter_body, count), out_shape=[shape]...]
    dot_general x4 -> x2, matrix products: 22.6 us -> 7.91 us  [row_product(): return jnp.dot(first_op, second_op, preferred_element_type=jnp.float32)]
    dot_general x4 -> x2, matrix products: 18.6 us -> 8.52 us  [times_transposed(): lax.dot_general(first_op, second_op, (((first_op.ndim - 1,), (1,)), ((),...]
    dot_general x4 -> x2, matrix products: 16.2 us -> 8.37 us  [inner_rows(): lax.dot_general(flatten_rows(first_op), flatten_rows(second_op), (((0,),...]
    unnamed x44 -> x39, local copies, waits for them, and re-layouts: 13 us -> 6.32 us
    slice x3 -> x1, local copies, waits for them, and re-layouts: 4.63 us -> 0.01 us  [square_device(): output = (validity * (residual + down_out + vectors[5])).astype(BF)]
  transfers between devices with their start and end apart: 2 -> 2, of which waited for: 0 -> 0; matrix products, arithmetic and copies ran while one was open for 17% -> 13% of each run, Pallas kernels for 39% -> 27%
where the time goes in v2:
time: 354 us; the launch traced here: 353 us
  Pallas kernels  267 us (75%)
  matrix products  24.8 us (7%)
  local copies, waits for them, and re-layouts  24.3 us (7%)
  other arithmetic  22.7 us (6%)
  between operations  14.6 us (4%)
    pallas_call x1, Pallas kernels, middle(): pl.pallas_call(functools.partial(middle_body, depth), out_shape=[tokens,...  75.5 us
    pallas_call x2, Pallas kernels, square_scatter(): pl.pallas_call(functools.partial(scatter_body, count), out_shape=[shape]...  52.7 us
    pallas_call x1, Pallas kernels, first_exchange(): pl.pallas_call(functools.partial(first_body, depth), out_shape=[jax.Shape...  43.1 us
    pallas_call x1, Pallas kernels, last_exchange(): pl.pallas_call(functools.partial(last_body, depth), out_shape=[jax.ShapeD...  41.1 us
    pallas_call x1, Pallas kernels, square_gather(): pl.pallas_call(functools.partial(gather_body, count), out_shape=[shape] *...  22.5 us
    pallas_call x1, Pallas kernels, share_sums(): pl.pallas_call(functools.partial(sums_body, depth), out_shape=jax.ShapeDt...  12.2 us
    pallas_call x1, Pallas kernels, attend_back(): pl.pallas_call(attend_back_body, grid=(slots,), out_shape=jax.ShapeDtypeS...  10.6 us
    pallas_call x1, Pallas kernels, attend(): pl.pallas_call(attend_body, grid=(slots,), out_shape=[jax.ShapeDtypeStruc...  9.18 us
  transfers between devices with their start and end apart: 2, of which 0 were waited for; matrix products, arithmetic and copies ran while one was open for 13% of the time, Pallas kernels for 27%

profile of v2, /device:TPU:0, one launch (start us, length us, event | category | flops | bytes accessed | tf_op | source)
XLA Modules:
  0.0 353.3 jit_solution(11849957983573508702)
XLA Ops:
  7.2 1.1 copy.107
  8.4 0.2 copy.108
  8.5 1.0 copy.101
  9.5 0.1 copy.102
  9.6 1.0 copy.103
  10.6 0.1 copy.104
  10.7 1.0 copy.105
  11.8 0.8 reshape.189
  12.6 0.8 reshape.190
  13.4 0.8 stack_reshape.11
  14.2 0.8 stack.57
  15.0 0.6 convert_element_type.61.vec
  15.6 1.8 pad_maximum_fusion.1.ffn_w
  17.4 1.6 pad_maximum_fusion.2.attn_w
  18.9 43.1 %first_exchange.1 = (bf16[2,1024,1024]{2,1,0:T(8,128)(2,1)}, bf16[4,8,128,128]{3,2,1,0:T(8,128)(2,1)}, bf16[2,8,128,128]{3,2,1,0:T(8,128)(2,1)}, f32[8,4,8,128]{3,2,1,0:T(8,128)}) custom-call(bf16[2,128,1024]{2,1,0:T(8,128)(2,1)} %hidden.3, bf16[2,4,128,128]{3,2,1,0:T(8,128)(2,1)} %pad_maximum_fusion.2.attn_w, ...), custom_call_target="tpu_custom_call" | custom-call | tf_op jit(solution)/shard_map/first_exchange/pallas_call | solution.py:836
  62.1 1.2 slice_reduce_fusion.4
  63.8 2.8 convert_reduce_fusion
  66.6 0.5 exponential_multiply_fusion.slopes
  67.2 0.3 copy.109
  67.5 0.2 copy.113
  67.7 0.6 dynamic_slice.23.lengths
  68.3 3.9 %fusion.2 = f32[2,1024]{1,0:T(2,128)S(1)} fusion(bf16[2,1024,1024]{2,1,0:T(8,128)(2,1)} %get-tuple-element.33, f32[2,1024]{1,0:T(2,128)S(1)} %broadcast_multiply_fusion), kind=kLoop, calls=%fused_computation.4 | loop fusion | flops 8386560 | bytes 4210688 | tf_op jit(solution)/shard_map/reduce_sum | solution.py:1198
  72.3 1.4 slice_bitcast_fusion.4
  73.7 3.6 %add_convert_fusion.qkv = bf16[2,1024,384]{2,1,0:T(8,128)(2,1)} fusion(f32[384]{0:T(512)S(1)} %pad_maximum_fusion.3, bf16[1024,384,1]{0,1,2:T(8,128)(2,1)S(1)} %bitcast.147, bf16[2,1024,1024]{2,1,0:T(8,128)(2,1)S(1)} %copy-done.1, f32[1024]{0:T(1024)S(1)} %bitcast.174, f32[1024]{0:T(1024)S(1)} %bitcast.167, f32[2,1024]{1,0:T(2,128)S(1)} %add_rsqrt_fusion, ...), kind=kOutput, calls=%fused_computation.9 | convolution fusion | flops 1624768512 | bytes 6579712 | tf_op jit(solution)/shard_map/dot_general | solution.py:27
  77.3 9.2 %attend.1 = (bf16[2,1024,128]{2,1,0:T(8,128)(2,1)}, f32[2,2,1024]{2,1,0:T(2,128)}) custom-call(s32[2]{0:T(128)} %dynamic_slice.23.lengths, f32[2]{0:T(128)} %exponential_multiply_fusion.slopes, bf16[2,1024,384]{2,1,0:T(8,128)(2,1)} %add_convert_fusion.qkv), custom_call_target="tpu_custom_call" | custom-call | tf_op jit(solution)/shard_map/attend/pallas_call | solution.py:1113
  86.5 4.3 %convolution_convert_fusion.1.refs_0_ = bf16[2,1024,1024]{2,1,0:T(8,128)(2,1)} fusion(bf16[2,1024,128]{2,1,0:T(8,128)(2,1)} %get-tuple-element.36.attention, bf16[128,1024,1]{0,1,2:T(8,128)(2,1)S(1)} %bitcast.139), kind=kOutput, calls=%fused_computation.11 | convolution fusion | flops 538968064 | bytes 4980736 | tf_op jit(solution)/shard_map/dot_general | solution.py:27
  90.8 27.1 %square_scatter1.2.branch = f32[2,128,1024]{2,1,0:T(8,128)} custom-call(bf16[2,1024,1024]{2,1,0:T(8,128)(2,1)} %convolution_convert_fusion.1.refs_0_), custom_call_target="tpu_custom_call" | custom-call | tf_op jit(solution)/shard_map/square_scatter1/pallas_call | solution.py:659
  117.8 1.0 slice_reduce_fusion.2
  119.1 0.9 multiply_convert_fusion.1.refs_0_
  120.1 22.5 %square_gather1.1.down_all = bf16[2,1024,1024]{2,1,0:T(8,128)(2,1)} custom-call(bf16[2,128,1024]{2,1,0:T(8,128)(2,1)} %multiply_convert_fusion.1.refs_0_), custom_call_target="tpu_custom_call" | custom-call | tf_op jit(solution)/shard_map/square_gather1/pallas_call | solution.py:508
  142.5 0.6 dynamic-slice_bitcast_fusion.up_b
  143.1 0.8 broadcast_in_dim.16.valid
  143.9 75.5 %middle.1 = (bf16[2,1024,1024]{2,1,0:T(8,128)(2,1)}, bf16[2,1024,1024]{2,1,0:T(8,128)(2,1)}, f32[2,128,1024]{2,1,0:T(8,128)}, f32[2,128,1024]{2,1,0:T(8,128)}, f...) custom-call(bf16[2,128,1024]{2,1,0:T(8,128)(2,1)} %hidden.3, ...), custom_call_target="tpu_custom_call" | custom-call | tf_op jit(solution)/shard_map/middle/pallas_call | solution.py:1390
  219.5 0.1 convert_reduce_fusion.2
  219.6 0.3 fusion.26
  219.9 4.2 %convolution_convert_fusion.2.grad = bf16[2,1024,128]{2,1,0:T(8,128)(2,1)} fusion(bf16[2,1024,1024]{2,1,0:T(8,128)(2,1)} %get-tuple-element.41, bf16[128,1024,1]{0,1,2:T(8,128)(2,1)S(1)} %bitcast.140), kind=kOutput, calls=%fused_computation.17 | convolution fusion | flops 537133056 | bytes 4980736 | tf_op jit(solution)/shard_map/dot_general | solution.py:40
  224.2 10.6 %attend_back.1 = bf16[2,1024,384]{2,1,0:T(8,128)(2,1)} custom-call(s32[2]{0:T(128)} %dynamic_slice.23.lengths, f32[2]{0:T(128)} %exponential_multiply_fusion.slopes, bf16[2,1024,384]{2,1,0:T(8,128)(2,1)} %add_convert_fusion.qkv, bf16[2,1024,128]{2,1,0:T(8,128)(2,1)} %get-tuple-element.36.attention, bf16[2,1024,128]{2,1,0:T(8,128)(2,1)} %convolution_convert_fusion.2.grad, ...), custom_call_target="tpu_custom_call" | custom-call | tf_op jit(solution)/shard_map/attend_back/pallas_call | solution.py:1173
  234.8 5.4 %bitcast_convert_fusion = bf16[1024,384]{1,0:T(8,128)(2,1)S(1)} fusion(bf16[2,1024,384]{2,1,0:T(8,128)(2,1)} %attend_back.1, bf16[2,1024,1024]{2,1,0:T(8,128)(2,1)} %get-tuple-element.33, f32[1024]{0:T(1024)S(1)} %bitcast.175, f32[1024]{0:T(1024)S(1)} %bitcast.168, f32[2,1024]{1,0:T(2,128)S(1)} %add_rsqrt_fusion, f32[2,1024]{1,0:T(2,128)S(1)} %broadcast_multiply_fusion), kind=kOutput, calls=%fused_computation.14 | convolution fusion | flops 1623588864 | bytes 6578176 | tf_op jit(solution)/shard_map/dot_general | solution.py:31
  240.2 0.5 reshape.211
  240.7 0.2 copy.146
  240.9 3.0 fusion.19
  243.9 0.2 copy.122
  244.1 0.2 copy.123
  244.3 25.6 %square_scatter1.3 = f32[2,128,1024]{2,1,0:T(8,128)} custom-call(bf16[2,1024,1024]{2,1,0:T(8,128)(2,1)} %get-tuple-element.39.refs_0_), custom_call_target="tpu_custom_call" | custom-call | tf_op jit(solution)/shard_map/square_scatter1/pallas_call | solution.py:659
  270.0 1.9 convert_reduce_fusion.1
  271.9 1.1 pad_maximum_fusion.attn_g
  272.9 1.0 multiply_convert_fusion
  273.9 4.3 %convolution_convert_fusion.shares = bf16[2,1024,1024]{2,1,0:T(8,128)(2,1)} fusion(bf16[2,1024,384]{2,1,0:T(8,128)(2,1)S(1)} %copy-done.3, bf16[1024,384,1]{0,1,2:T(8,128)(2,1)S(1)} %bitcast.148), kind=kOutput, calls=%fused_computation.10 | convolution fusion | flops 1612709888 | bytes 6553600 | tf_op jit(solution)/shard_map/dot_general | solution.py:40
  278.2 41.1 %last_exchange.1 = (f32[2,128,1024]{2,1,0:T(8,128)}, f32[2,4,128,128]{3,2,1,0:T(8,128)}, bf16[8,2,128,128]{3,2,1,0:T(8,128)(2,1)}) custom-call(bf16[2,1024,1024]{2,1,0:T(8,128)(2,1)} %convolution_convert_fusion.shares, bf16[8,4,128,128]{3,2,1,0:T(8,128)(2,1)} %pad_maximum_fusion.attn_g, bf16[8,2,128,128]{3,2,1,0:T(8,128)(2,1)} %bitcast.154), custom_call_target="tpu_custom_call" | custom-call | tf_op jit(solution)/shard_map/last_exchange/pallas_call | solution.py:991
  319.3 1.9 fusion.25
  321.2 0.7 maximum_maximum_fusion.parts
  321.9 12.2 %share_sums.1 = f32[8,4,16,128]{3,2,1,0:T(8,128)} custom-call(f32[8,16,128]{2,1,0:T(8,128)} %maximum_maximum_fusion.parts), custom_call_target="tpu_custom_call" | custom-call | tf_op jit(solution)/shard_map/share_sums/pallas_call | solution.py:1051
  334.1 1.0 slice_reduce_fusion
  335.1 1.9 fusion.29
  337.1 1.0 copy.127
  338.3 0.7 dynamic_slice.27
  338.9 0.7 dynamic_slice.28
  339.6 0.5 slice_bitcast_fusion.9
  340.1 0.7 fusion.30
  340.9 0.8 copy.129
  341.7 0.8 copy.130
  342.6 0.8 copy.131
  343.4 0.7 dynamic_slice.29
  344.0 2.4 fusion.24
  (81 shorter events, 1.8 us)
Async XLA Ops:
  7.2 135.9 %all-gather.3.cloned.1.call-start = ((), (), s32[]{:S(2)}) async-start(), calls=%async_computation.2 | async-start | bytes 2621440 | tf_op jit(solution)/shard_map/all_gather | solution.py:1487
  62.0 4.6 %copy-start.7 = (bf16[4,8,128,128]{3,2,1,0:T(8,128)(2,1)S(1)}, bf16[4,8,128,128]{3,2,1,0:T(8,128)(2,1)}, u32[]{:S(2)}) copy-start(bf16[4,8,128,128]{3,2,1,0:T(8,128)(2,1)} %get-tuple-element.35) | copy-start | bytes 3145732
  62.0 216.1 %reduce-scatter.2.cloned.1.call-start = ((), (), s32[]{:S(2)}) async-start(), calls=%async_computation.1 | async-start | bytes 2621440 | tf_op jit(solution)/shard_map/reduce_scatter | solution.py:1526
  63.7 4.0 %copy-start.15 = (s32[8]{0:T(128)S(1)}, s32[8]{0:T(128)}, u32[]{:S(2)}) copy-start(s32[8]{0:T(128)} %param.19) | copy-start | bytes 100
  67.5 9.7 %copy-start.9 = (bf16[3,1024,128]{1,2,0:T(8,128)(2,1)}, bf16[3,1024,128]{1,2,0:T(8,128)(2,1)S(1)}, u32[]{:S(2)}) copy-start(bf16[3,1024,128]{1,2,0:T(8,128)(2,1)S(1)} %copy.109) | copy-start | bytes 2359300
  67.7 5.9 %copy-start.1 = (bf16[2,1024,1024]{2,1,0:T(8,128)(2,1)S(1)}, bf16[2,1024,1024]{2,1,0:T(8,128)(2,1)}, u32[]{:S(2)}) copy-start(bf16[2,1024,1024]{2,1,0:T(8,128)(2,1)} %get-tuple-element.33) | copy-start | bytes 12582916
  86.5 32.6 %copy-start.13 = (s32[2]{0:T(128)S(1)}, s32[2]{0:T(128)}, u32[]{:S(2)}) copy-start(s32[2]{0:T(128)} %dynamic_slice.23.lengths) | copy-start | bytes 28
  86.5 32.7 %copy-start.6 = (bf16[2,128,1024]{2,1,0:T(8,128)(2,1)S(1)}, bf16[2,128,1024]{2,1,0:T(8,128)(2,1)}, u32[]{:S(2)}) copy-start(bf16[2,128,1024]{2,1,0:T(8,128)(2,1)} %cotangent.1) | copy-start | bytes 1572868
  143.9 75.6 %copy-start = (bf16[2,128,1024]{2,1,0:T(8,128)(2,1)S(1)}, bf16[2,128,1024]{2,1,0:T(8,128)(2,1)}, u32[]{:S(2)}) copy-start(bf16[2,128,1024]{2,1,0:T(8,128)(2,1)} %hidden.3) | copy-start | bytes 1572868
  234.8 6.1 %copy-start.2 = (bf16[2,1024,128]{2,1,0:T(8,128)(2,1)S(1)}, bf16[2,1024,128]{2,1,0:T(8,128)(2,1)}, u32[]{:S(2)}) copy-start(bf16[2,1024,128]{2,1,0:T(8,128)(2,1)} %get-tuple-element.36.attention) | copy-start | bytes 1572868
  243.9 28.0 %copy-start.14 = (f32[1,512]{1,0:T(1,128)S(1)}, f32[1,512]{1,0:T(1,128)}, u32[]{:S(2)}) copy-start(f32[1,512]{1,0:T(1,128)} %get-tuple-element.46) | copy-start | bytes 6148
  244.3 28.7 %copy-start.12 = (f32[8,1024]{1,0:T(8,128)S(1)}, f32[8,1024]{1,0:T(8,128)}, u32[]{:S(2)}) copy-start(f32[8,1024]{1,0:T(8,128)} %get-tuple-element.45) | copy-start | bytes 98308
  244.3 28.6 %copy-start.8 = (f32[2,128,1024]{2,1,0:T(8,128)S(1)}, f32[2,128,1024]{2,1,0:T(8,128)}, u32[]{:S(2)}) copy-start(f32[2,128,1024]{2,1,0:T(8,128)} %get-tuple-element.38) | copy-start | bytes 3145732
  269.9 3.0 copy-start.5
  269.9 4.0 %copy-start.3 = (bf16[2,1024,384]{2,1,0:T(8,128)(2,1)S(1)}, bf16[2,1024,384]{2,1,0:T(8,128)(2,1)}, u32[]{:S(2)}) copy-start(bf16[2,1024,384]{2,1,0:T(8,128)(2,1)} %attend_back.1) | copy-start | bytes 4718596
  269.9 3.9 %copy-start.10 = (bf16[3,1024,128]{1,2,0:T(8,128)(2,1)S(1)}, bf16[3,1024,128]{1,2,0:T(8,128)(2,1)}, u32[]{:S(2)}) copy-start(bf16[3,1024,128]{1,2,0:T(8,128)(2,1)} %copy-done.9) | copy-start | bytes 2359300
  319.3 20.8 %copy-start.11 = (f32[2,4,128,128]{3,2,1,0:T(8,128)S(1)}, f32[2,4,128,128]{3,2,1,0:T(8,128)}, u32[]{:S(2)}) copy-start(f32[2,4,128,128]{3,2,1,0:T(8,128)} %get-tuple-element.47) | copy-start | bytes 1572868
  319.3 24.7 %copy-start.4 = (f32[2,128,1024]{2,1,0:T(8,128)S(1)}, f32[2,128,1024]{2,1,0:T(8,128)}, u32[]{:S(2)}) copy-start(f32[2,128,1024]{2,1,0:T(8,128)} %get-tuple-element.44) | copy-start | bytes 3145732
Sparse Core Ops, SparseCore 0:
  62.2 46.7 all-gather.2
  219.5 42.5 reduce-scatter.1

commit v3 on v2

--- a/solution.py
+++ b/solution.py
@@ -482,44 +482,6 @@
     return [{"wide": pair}, {"wide": ax}, {"wide": ay}]
 
 
-def gather_body(count, *refs):
-    srcs, dsts = refs[:count], refs[count : 2 * count]
-    send, recv, local = refs[2 * count :]
-    greet(wide_square(square_places()))
-    parts = [
-        SquareGather(srcs[i], dsts[i], send.at[i], recv.at[i], local.at[i]) for i in range(count)
-    ]
-    for part in parts:
-        part.start()
-    for part in parts:
-        part.first()
-    for part in parts:
-        part.second()
-    for part in parts:
-        part.third()
-    for part in parts:
-        part.finish()
-
-
-def square_gather(*arrays):
-    count = len(arrays)
-    width = arrays[0].shape[-1]
-    shape = jax.ShapeDtypeStruct((2, 8 * BLK, width), arrays[0].dtype)
-    return pl.pallas_call(
-        functools.partial(gather_body, count),
-        out_shape=[shape] * count,
-        in_specs=[vmem()] * count,
-        out_specs=[hbm()] * count,
-        scratch_shapes=[
-            pltpu.SemaphoreType.DMA((count, SquareGather.SENDS)),
-            pltpu.SemaphoreType.DMA((count, SquareGather.SENDS)),
-            pltpu.SemaphoreType.DMA((count,)),
-        ],
-        compiler_params=pltpu.CompilerParams(collective_id=count, has_side_effects=True),
-        name="square_gather" + str(count),
-    )(*arrays)
-
-
 def add_rows(dst, first, second, third=None):
     step = 16
 
@@ -618,53 +580,60 @@
             copy.wait_send()
 
 
-def scatter_scratch(count, width):
-    return [
-        pltpu.VMEM((count, 4, 2, BLK, width), BF),
-        pltpu.VMEM((count, 4, 2, BLK, width), BF),
-        pltpu.VMEM((count, 3, BLK, width), BF),
-        pltpu.VMEM((count, 3, BLK, width), BF),
-        pltpu.SemaphoreType.DMA((count, SquareScatter.SENDS)),
-        pltpu.SemaphoreType.DMA((count, SquareScatter.SENDS)),
-    ]
-
-
-def scatter_parts(srcs, outs, scratch):
-    return [
-        SquareScatter(srcs[i], outs[i], *[buffer.at[i] for buffer in scratch])
-        for i in range(len(srcs))
-    ]
-
-
-def scatter_body(count, *refs):
-    srcs, outs = refs[:count], refs[count : 2 * count]
-    greet(wide_square(square_places()))
-    parts = scatter_parts(srcs, outs, refs[2 * count :])
-    for part in parts:
-        part.start()
-    for part in parts:
-        part.first()
-    for part in parts:
-        part.middle()
-    for part in parts:
-        part.own_sums()
-    for part in parts:
-        part.finish()
-
-
-def square_scatter(*arrays):
-    count = len(arrays)
-    width = arrays[0].shape[-1]
-    shape = jax.ShapeDtypeStruct((2, BLK, width), F32)
-    return pl.pallas_call(
-        functools.partial(scatter_body, count),
-        out_shape=[shape] * count,
-        in_specs=[vmem()] * count,
-        out_specs=[vmem()] * count,
-        scratch_shapes=scatter_scratch(count, width),
-        compiler_params=pltpu.CompilerParams(collective_id=4 + count, has_side_effects=True),
-        name="square_scatter" + str(count),
-    )(*arrays)
+class LineGather:
+    def __init__(self, depth, pieces, send, recv):
+        self.depth, self.pieces, self.send, self.recv = depth, pieces, send, recv
+        self.layer = lax.axis_index("tp")
+
+    def copies(self, step, up):
+        index = self.layer - step + 1 if up else self.layer + step - 1
+        goal = {"tp": self.layer + 1 if up else self.layer - 1}
+        side = 0 if up else 1
+        made = []
+        for number, (own, buffer) in enumerate(self.pieces):
+            source = own if step == 1 else buffer.at[index]
+            made.append(
+                remote(
+                    source,
+                    buffer.at[index],
+                    self.send.at[side, number, step - 1],
+                    self.recv.at[side, number, step - 1],
+                    goal,
+                )
+            )
+        return made
+
+    def each(self, step, act):
+        layer = self.layer
+
+        @pl.when((layer < self.depth - 1) & (layer - step + 1 >= 0))
+        def _():
+            for copy in self.copies(step, True):
+                act(copy)
+
+        @pl.when((layer > 0) & (layer + step - 1 < self.depth))
+        def _():
+            for copy in self.copies(step, False):
+                act(copy)
+
+    def start(self, step):
+        self.each(step, lambda copy: copy.start())
+
+    def sent(self, step):
+        self.each(step, lambda copy: copy.wait_send())
+
+    def arrive(self, step):
+        layer = self.layer
+
+        @pl.when(layer - step >= 0)
+        def _():
+            for copy in self.copies(step, True):
+                copy.wait_recv()
+
+        @pl.when(layer + step < self.depth)
+        def _():
+            for copy in self.copies(step, False):
+                copy.wait_recv()
 
 
 def wide_others(own):
@@ -702,62 +671,8 @@
     gather = SquareGather(hidden, hidden_all, send, recv, local.at[0])
     gather.start()
 
-    def up_copies(step):
-        index = layer - step + 1
-        sem = step - 1
-        src_w = attn_w if step == 1 else attn_z.at[index]
-        src_v = vec if step == 1 else vec_z.at[index]
-        up = {"tp": layer + 1}
-        return (
-            remote(src_w, attn_z.at[index], z_send.at[0, sem], z_recv.at[0, sem], up),
-            remote(src_v, vec_z.at[index], z_send.at[1, sem], z_recv.at[1, sem], up),
-        )
-
-    def down_copies(step):
-        index = layer + step - 1
-        sem = step - 1
-        src_w = attn_w if step == 1 else attn_z.at[index]
-        src_v = vec if step == 1 else vec_z.at[index]
-        down = {"tp": layer - 1}
-        return (
-            remote(src_w, attn_z.at[index], z_send.at[2, sem], z_recv.at[2, sem], down),
-            remote(src_v, vec_z.at[index], z_send.at[3, sem], z_recv.at[3, sem], down),
-        )
-
-    def z_start(step):
-        @pl.when((layer < depth - 1) & (layer - step + 1 >= 0))
-        def _():
-            for copy in up_copies(step):
-                copy.start()
-
-        @pl.when((layer > 0) & (layer + step - 1 < depth))
-        def _():
-            for copy in down_copies(step):
-                copy.start()
-
-    def z_arrive(step):
-        @pl.when(layer - step >= 0)
-        def _():
-            for copy in up_copies(step):
-                copy.wait_recv()
-
-        @pl.when(layer + step < depth)
-        def _():
-            for copy in down_copies(step):
-                copy.wait_recv()
-
-    def z_sent(step):
-        @pl.when((layer < depth - 1) & (layer - step + 1 >= 0))
-        def _():
-            for copy in up_copies(step):
-                copy.wait_send()
-
-        @pl.when((layer > 0) & (layer + step - 1 < depth))
-        def _():
-            for copy in down_copies(step):
-                copy.wait_send()
-
-    z_start(1)
+    line = LineGather(depth, [(attn_w, attn_z), (vec, vec_z)], z_send, z_recv)
+    line.start(1)
     own_z = [
         pltpu.make_async_copy(attn_w, attn_z.at[layer], own_sems.at[0]),
         pltpu.make_async_copy(vec, vec_z.at[layer], own_sems.at[1]),
@@ -781,17 +696,17 @@
         )
     for copy in ffn_copies:
         copy.start()
-    z_arrive(1)
+    line.arrive(1)
     if depth > 2:
-        z_start(2)
+        line.start(2)
     gather.second()
     if depth > 2:
-        z_arrive(2)
+        line.arrive(2)
     if depth > 3:
-        z_start(3)
+        line.start(3)
     gather.third()
     if depth > 3:
-        z_arrive(3)
+        line.arrive(3)
     for copy in own_z:
         copy.wait()
     per_layer = 8 // depth
@@ -827,7 +742,7 @@
     attn_own.wait()
     vec_own.wait()
     for step in range(1, depth):
-        z_sent(step)
+        line.sent(step)
 
 
 def first_exchange(depth, hidden, attn_w, ffn_w, vec):
@@ -849,8 +764,8 @@
             dma((SquareGather.SENDS,)),
             dma((SquareGather.SENDS,)),
             dma((1,)),
-            dma((4, depth - 1)),
-            dma((4, depth - 1)),
+            dma((2, 2, depth - 1)),
+            dma((2, 2, depth - 1)),
             dma((7,)),
             dma((7,)),
             dma((7,)),
@@ -864,332 +779,251 @@
     )(hidden, attn_w, ffn_w, vec)
 
 
-def last_body(
+def head_bias(length, slope, rows):
+    place = lax.broadcasted_iota(jnp.int32, (rows, QB), 0)
+    bias = slope * place.astype(F32)
+    return jnp.where(place < length, bias, NEG)
+
+
+QB = 256
+
+
+def dot_nt(first, second):
+    return lax.dot_general(first, second, (((1,), (1,)), ((), ())), preferred_element_type=F32)
+
+
+def dot_nn(first, second):
+    return lax.dot_general(first, second, (((1,), (0,)), ((), ())), preferred_element_type=F32)
+
+
+def later_key(size):
+    key_place = lax.broadcasted_iota(jnp.int32, (size, size), 0)
+    query_place = lax.broadcasted_iota(jnp.int32, (size, size), 1)
+    return key_place > query_place
+
+
+def slot_scores(key, query, bias, step):
+    extent = (step + 1) * QB
+    scores = dot_nt(key[:extent], query) * (0.125 * LOG2E) + bias[:extent]
+    edge = jnp.where(later_key(QB), NEG, scores[extent - QB :])
+    return edge if step == 0 else jnp.concatenate([scores[: extent - QB], edge], 0)
+
+
+def attend_slot(slot, length, slopes, qkv, out, totals, bias):
+    rows = qkv.shape[1]
+    for head in range(2):
+        lanes = pl.ds(head * HEAD, HEAD)
+        bias[...] = head_bias(length, slopes[head], rows)
+        key = qkv[slot, :, pl.ds(2 * HEAD + head * HEAD, HEAD)]
+        value_t = qkv[slot, :, pl.ds(4 * HEAD + head * HEAD, HEAD)].T
+        for step in range(rows // QB):
+            here = pl.ds(step * QB, QB)
+            scores = slot_scores(key, qkv[slot, here, lanes], bias, step)
+            highest = jnp.max(scores, axis=0, keepdims=True)
+            weights = jnp.exp2(scores - highest)
+            total = jnp.sum(weights, axis=0, keepdims=True)
+            mixed = dot_nn(value_t[:, : (step + 1) * QB], weights.astype(BF)) / total
+            out[slot, here, lanes] = mixed.T.astype(BF)
+            totals[slot, pl.ds(head, 1), here] = highest + jnp.log2(total)
+
+
+def attend_slot_back(
+    slot, length, slopes, qkv, attention, grad, totals, out, bias, key_sum, value_sum
+):
+    rows = qkv.shape[1]
+    for head in range(2):
+        lanes = pl.ds(head * HEAD, HEAD)
+        key_lanes = pl.ds(2 * HEAD + head * HEAD, HEAD)
+        value_lanes = pl.ds(4 * HEAD + head * HEAD, HEAD)
+        bias[...] = head_bias(length, slopes[head], rows)
+        key = qkv[slot, :, key_lanes]
+        value = qkv[slot, :, value_lanes]
+        key_t = key.T
+        key_sum[...] = jnp.zeros_like(key_sum)
+        value_sum[...] = jnp.zeros_like(value_sum)
+        for step in range(rows // QB):
+            here = pl.ds(step * QB, QB)
+            extent = (step + 1) * QB
+            query = qkv[slot, here, lanes]
+            grad_rows = grad[slot, here, lanes]
+            product = grad_rows.astype(F32) * attention[slot, here, lanes].astype(F32)
+            delta = jnp.sum(product.T, axis=0, keepdims=True)
+            scores = slot_scores(key, query, bias, step)
+            probs = jnp.exp2(scores - totals[slot, pl.ds(head, 1), here])
+            grad_probs = dot_nt(value[:extent], grad_rows)
+            grad_scores = (probs * (grad_probs - delta)).astype(BF)
+            span = pl.ds(0, extent)
+            value_sum[span] += dot_nn(probs.astype(BF), grad_rows)
+            key_sum[span] += dot_nn(grad_scores, query)
+            grad_query = dot_nn(key_t[:, :extent], grad_scores)
+            out[slot, here, lanes] = (grad_query.T * 0.125).astype(BF)
+        out[slot, :, key_lanes] = (key_sum[...] * 0.125).astype(BF)
+        out[slot, :, value_lanes] = value_sum[...].astype(BF)
+
+
+def weight_loads(attn_all, qkv_w, dense_w, sems):
+    loads = []
+    for blk in range(8):
+        rows = pl.ds(blk * BLK, BLK)
+        for kind in range(3):
+            lanes = pl.ds(kind * BLK, BLK)
+            loads.append(
+                pltpu.make_async_copy(attn_all.at[kind, blk], qkv_w.at[rows, lanes], sems.at[kind, blk])
+            )
+        loads.append(pltpu.make_async_copy(attn_all.at[3, blk], dense_w.at[:, rows], sems.at[3, blk]))
+    return loads
+
+
+def front_body(
     depth,
-    shares,
-    attn_g,
-    ffn_g,
-    rows_out,
-    attn_out,
-    ffn_out,
-    attn_in,
-    attn_z,
+    lengths,
+    slopes,
+    hidden_all,
+    attn_all,
+    ffn_all,
+    vectors,
+    qkv_b,
+    down_own,
+    normed,
+    qkv,
+    attention,
+    totals,
+    branch,
+    down_all,
+    ffn_z,
+    share,
+    qkv_w,
+    dense_w,
+    bias,
     from_pair,
     summed,
     from_x,
     from_y,
     s_send,
     s_recv,
-    a_send,
-    a_recv,
-    z_send,
-    z_recv,
-    f_send,
-    f_recv,
-    own_sems,
+    g_send,
+    g_recv,
+    l_send,
+    l_recv,
+    local,
+    w_sems,
 ):
-    own, pair, ax, ay, dg = square_places()
+    width = hidden_all.shape[-1]
     layer = lax.axis_index("tp")
-    per_layer = 8 // depth
-    greet(wide_others(own) + [{"tp": (layer + step) % depth} for step in range(1, depth)])
-    scatter = scatter_parts(
-        [shares], [rows_out], (from_pair, summed, from_x, from_y, s_send, s_recv)
-    )[0]
-    scatter.start()
-    attn_copies = []
-    for step in range(1, 8):
-        there = (own + step) % 8
-        attn_copies.append(
-            remote(
-                attn_g.at[there],
-                attn_in.at[own],
-                a_send.at[step - 1],
-                a_recv.at[step - 1],
-                {"wide": there},
-            )
-        )
-    for copy in attn_copies:
-        copy.start()
-    own_copy = pltpu.make_async_copy(attn_g.at[own], attn_in.at[own], own_sems.at[0])
-    own_copy.start()
-    scatter.first()
-
-    def onward(index):
-        goal = index // per_layer
-        piece = index % per_layer
-        return remote(
-            attn_in.at[index],
-            attn_z.at[layer, piece],
-            z_send.at[index],
-            z_recv.at[layer, piece],
-            {"tp": goal},
-        )
-
-    def forward(index):
-        @pl.when(index // per_layer != layer)
+    loads = weight_loads(attn_all, qkv_w, dense_w, w_sems)
+    for load in loads:
+        load.start()
+    greet(wide_square(square_places()) + line_others(depth))
+    gather = SquareGather(down_own, down_all, g_send, g_recv, local.at[0])
+    gather.start()
+    line = LineGather(depth, [(ffn_all, ffn_z)], l_send, l_recv)
+    line.start(1)
+    own_z = pltpu.make_async_copy(ffn_all, ffn_z.at[layer], local.at[1])
+    own_z.start()
+    scatter = SquareScatter(share, branch, from_pair, summed, from_x, from_y, s_send, s_recv)
+    for load in loads:
+        load.wait()
+    step = 32
+
+    def one_slot(slot, carry):
+        def block(index, carry):
+            def norm_part(part, carry):
+                rows = pl.ds(pl.multiple_of(index * QB + part * step, step), step)
+                hat, _inverse = norm_stats(hidden_all[slot, rows].astype(F32))
+                normed[slot, rows] = (hat * vectors[0:1] + vectors[1:2]).astype(BF)
+                return carry
+
+            lax.fori_loop(0, QB // step, norm_part, 0)
+            rows = pl.ds(pl.multiple_of(index * QB, QB), QB)
+            qkv[slot, rows] = (dot_nn(normed[slot, rows], qkv_w[...]) + qkv_b[...]).astype(BF)
+            return carry
+
+        lax.fori_loop(0, 8 * BLK // QB, block, 0)
+        attend_slot(slot, lengths[slot], slopes, qkv, attention, totals, bias)
+
+        @pl.when(slot == 0)
         def _():
-            onward(index).start()
-
-    own_copy.wait()
-    forward(own)
-    for step in range(1, 8):
-        attn_copies[step - 1].wait_recv()
-        forward((own + 8 - step) % 8)
-    ffn_own = pltpu.make_async_copy(ffn_g.at[own], ffn_out.at[own], own_sems.at[1])
-    ffn_own.start()
-    ffn_copies = []
-    for step in range(1, 8):
-        there = (own + step) % 8
-        ffn_copies.append(
-            remote(
-                ffn_g.at[there],
-                ffn_out.at[own],
-                f_send.at[step - 1],
-                f_recv.at[step - 1],
-                {"wide": there},
-            )
-        )
+            gather.first()
+
+        return carry
+
+    lax.fori_loop(0, 2, one_slot, 0)
+
+    def compute(index, carry):
+        rows = pl.ds(pl.multiple_of(relation(index) * BLK, BLK), BLK)
+        values = attention[:, rows].reshape(2 * BLK, 2 * HEAD)
+        share[:, rows] = dot_nn(values, dense_w[...]).astype(BF).reshape(2, BLK, width)
+        return carry
+
+    for number, chip in enumerate((0, 1, 2, 3)):
+        start = (6, 2, 4, 0)[number]
+        lax.fori_loop(start, start + 2, compute, 0)
+        scatter.pairs[chip].start()
+    gather.second()
+    scatter.near(0)
+    scatter.near(1)
+    scatter.near(2)
+    line.arrive(1)
+    line.start(2)
+    gather.third()
+    scatter.near(3)
+    line.arrive(2)
+    line.start(3)
     scatter.middle()
-    for copy in ffn_copies:
-        copy.start()
-    scatter.own_sums()
+    gather.finish()
     scatter.finish()
-    for step in range(1, depth):
-        source = (layer + step) % depth
-        for piece in range(per_layer):
-            remote(
-                attn_in.at[piece],
-                attn_z.at[source, piece],
-                z_send.at[piece],
-                z_recv.at[source, piece],
-                {"tp": source},
-            ).wait_recv()
-    for piece in range(per_layer):
-        for kind in range(4):
-            total = attn_in[layer * per_layer + piece, kind].astype(F32)
-            for step in range(1, depth):
-                total = total + attn_z[(layer + step) % depth, piece, kind].astype(F32)
-            attn_out[piece, kind] = total
-    for copy in attn_copies:
-        copy.wait_send()
-    for index in range(8):
-        @pl.when(index // per_layer != layer)
-        def _(index=index):
-            onward(index).wait_send()
-
-    for copy in ffn_copies:
-        copy.wait_recv()
-    for copy in ffn_copies:
-        copy.wait_send()
-    ffn_own.wait()
-
-
-def last_exchange(depth, shares, attn_g, ffn_g):
-    width = shares.shape[-1]
+    own_z.wait()
+    line.arrive(3)
+    for number in range(1, depth):
+        line.sent(number)
+
+
+def line_others(depth):
+    layer = lax.axis_index("tp")
+    return [{"tp": (layer + step) % depth} for step in range(1, depth)]
+
+
+def front(depth, lengths, slopes, hidden_all, attn_all, ffn_all, vectors, qkv_b, down_own):
+    width = hidden_all.shape[-1]
     dma = pltpu.SemaphoreType.DMA
-    per_layer = 8 // depth
+    smem = pl.BlockSpec(memory_space=pltpu.SMEM)
+    tokens = jax.ShapeDtypeStruct((2, 8 * BLK, width), BF)
     return pl.pallas_call(
-        functools.partial(last_body, depth),
+        functools.partial(front_body, depth),
         out_shape=[
+            tokens,
+            jax.ShapeDtypeStruct((2, 8 * BLK, 6 * HEAD), BF),
+            jax.ShapeDtypeStruct((2, 8 * BLK, 2 * HEAD), BF),
+            jax.ShapeDtypeStruct((2, 2, 8 * BLK), F32),
             jax.ShapeDtypeStruct((2, BLK, width), F32),
-            jax.ShapeDtypeStruct((per_layer, 4, BLK, BLK), F32),
-            jax.ShapeDtypeStruct((8, 2, BLK, BLK), BF),
+            tokens,
+            jax.ShapeDtypeStruct((depth,) + ffn_all.shape, BF),
         ],
-        in_specs=[vmem()] * 3,
-        out_specs=[vmem()] * 3,
+        in_specs=[smem, smem, vmem(), hbm()] + [vmem()] * 4,
+        out_specs=[vmem()] * 5 + [hbm()] * 2,
         scratch_shapes=[
-            pltpu.VMEM((8, 4, BLK, BLK), BF),
-            pltpu.VMEM((depth, per_layer, 4, BLK, BLK), BF),
+            pltpu.VMEM((2, 8 * BLK, width), BF),
+            pltpu.VMEM((width, 6 * HEAD), BF),
+            pltpu.VMEM((2 * HEAD, width), BF),
+            pltpu.VMEM((8 * BLK, QB), F32),
         ]
-        + scatter_scratch(1, width)
+        + single_scratch(width)
         + [
-            dma((7,)),
-            dma((7,)),
-            dma((8,)),
-            dma((depth, per_layer)),
-            dma((7,)),
-            dma((7,)),
+            dma((SquareGather.SENDS,)),
+            dma((SquareGather.SENDS,)),
+            dma((2, 1, depth - 1)),
+            dma((2, 1, depth - 1)),
             dma((2,)),
+            dma((4, 8)),
         ],
-        compiler_params=pltpu.CompilerParams(collective_id=11, has_side_effects=True),
-        name="last_exchange",
-    )(shares, attn_g, ffn_g)
-
-
-def sums_body(depth, parts, gathered, send, recv, local):
-    own = lax.axis_index("wide")
-    layer = lax.axis_index("tp")
-    others = []
-    for up in range(depth):
-        for step in range(8):
-            if up or step:
-                others.append(((own + step) % 8, (layer + up) % depth))
-    greet([{"wide": wide, "tp": tp} for wide, tp in others])
-    keep = pltpu.make_async_copy(parts.at[own], gathered.at[own, layer], local.at[0])
-    keep.start()
-    copies = [
-        remote(
-            parts.at[wide],
-            gathered.at[own, layer],
-            send.at[index],
-            recv.at[index],
-            {"wide": wide, "tp": tp},
-        )
-        for index, (wide, tp) in enumerate(others)
-    ]
-    for copy in copies:
-        copy.start()
-    for copy in copies:
-        copy.wait_recv()
-    for copy in copies:
-        copy.wait_send()
-    keep.wait()
-
-
-def share_sums(depth, parts):
-    dma = pltpu.SemaphoreType.DMA
-    return pl.pallas_call(
-        functools.partial(sums_body, depth),
-        out_shape=jax.ShapeDtypeStruct((8, depth) + parts.shape[1:], F32),
-        in_specs=[vmem()],
-        out_specs=vmem(),
-        scratch_shapes=[dma((8 * depth - 1,)), dma((8 * depth - 1,)), dma((1,))],
-        compiler_params=pltpu.CompilerParams(collective_id=12, has_side_effects=True),
-        name="share_sums",
-    )(parts)
-
-
-def head_bias(length, slope, rows):
-    place = lax.broadcasted_iota(jnp.int32, (rows, QB), 0)
-    bias = slope * place.astype(F32)
-    return jnp.where(place < length, bias, NEG)
-
-
-QB = 256
-
-
-def dot_nt(first, second):
-    return lax.dot_general(first, second, (((1,), (1,)), ((), ())), preferred_element_type=F32)
-
-
-def dot_nn(first, second):
-    return lax.dot_general(first, second, (((1,), (0,)), ((), ())), preferred_element_type=F32)
-
-
-def later_key(size):
-    key_place = lax.broadcasted_iota(jnp.int32, (size, size), 0)
-    query_place = lax.broadcasted_iota(jnp.int32, (size, size), 1)
-    return key_place > query_place
-
-
-def attend_body(lengths, slopes, qkv, out, totals, bias):
-    slot = pl.program_id(0)
-    rows = qkv.shape[1]
-    length = lengths[slot]
-    scale = 0.125 * LOG2E
-    for head in range(2):
-        lanes = pl.ds(head * HEAD, HEAD)
-        bias[...] = head_bias(length, slopes[head], rows)
-        key = qkv[0, :, pl.ds(2 * HEAD + head * HEAD, HEAD)]
-        value = qkv[0, :, pl.ds(4 * HEAD + head * HEAD, HEAD)]
-        value_t = value.T
-        for step in range(rows // QB):
-            here = pl.ds(step * QB, QB)
-            extent = (step + 1) * QB
-            query = qkv[0, here, lanes]
-            scores = dot_nt(key[:extent], query) * scale + bias[:extent]
-            low_part = jnp.where(later_key(QB), NEG, scores[extent - QB :])
-            scores = low_part if step == 0 else jnp.concatenate([scores[: extent - QB], low_part], 0)
-            highest = jnp.max(scores, axis=0, keepdims=True)
-            weights = jnp.exp2(scores - highest)
-            total = jnp.sum(weights, axis=0, keepdims=True)
-            mixed = dot_nn(value_t[:, :extent], weights.astype(BF)) / total
-            out[0, here, lanes] = mixed.T.astype(BF)
-            totals[0, pl.ds(head, 1), here] = highest + jnp.log2(total)
-
-
-def attend(lengths, slopes, qkv):
-    slots, rows, _width = qkv.shape
-    return pl.pallas_call(
-        attend_body,
-        grid=(slots,),
-        out_shape=[
-            jax.ShapeDtypeStruct((slots, rows, 2 * HEAD), BF),
-            jax.ShapeDtypeStruct((slots, 2, rows), F32),
-        ],
-        in_specs=[
-            pl.BlockSpec(memory_space=pltpu.SMEM),
-            pl.BlockSpec(memory_space=pltpu.SMEM),
-            pl.BlockSpec((1, rows, 6 * HEAD), lambda s: (s, 0, 0)),
-        ],
-        out_specs=[
-            pl.BlockSpec((1, rows, 2 * HEAD), lambda s: (s, 0, 0)),
-            pl.BlockSpec((1, 2, rows), lambda s: (s, 0, 0)),
-        ],
-        scratch_shapes=[pltpu.VMEM((rows, QB), F32)],
-        name="attend",
-    )(lengths, slopes, qkv)
-
-
-def attend_back_body(lengths, slopes, qkv, attention, grad, totals, out, bias, key_sum, value_sum):
-    slot = pl.program_id(0)
-    rows = qkv.shape[1]
-    length = lengths[slot]
-    scale = 0.125 * LOG2E
-    for head in range(2):
-        lanes = pl.ds(head * HEAD, HEAD)
-        key_lanes = pl.ds(2 * HEAD + head * HEAD, HEAD)
-        value_lanes = pl.ds(4 * HEAD + head * HEAD, HEAD)
-        bias[...] = head_bias(length, slopes[head], rows)
-        key = qkv[0, :, key_lanes]
-        value = qkv[0, :, value_lanes]
-        key_t = key.T
-        key_sum[...] = jnp.zeros_like(key_sum)
-        value_sum[...] = jnp.zeros_like(value_sum)
-        for step in range(rows // QB):
-            here = pl.ds(step * QB, QB)
-            extent = (step + 1) * QB
-            query = qkv[0, here, lanes]
-            grad_rows = grad[0, here, lanes]
-            product = grad_rows.astype(F32) * attention[0, here, lanes].astype(F32)
-            delta = jnp.sum(product.T, axis=0, keepdims=True)
-            scores = dot_nt(key[:extent], query) * scale + bias[:extent]
-            low_part = jnp.where(later_key(QB), NEG, scores[extent - QB :])
-            scores = low_part if step == 0 else jnp.concatenate([scores[: extent - QB], low_part], 0)
-            probs = jnp.exp2(scores - totals[0, pl.ds(head, 1), here])
-            grad_probs = dot_nt(value[:extent], grad_rows)
-            grad_scores = (probs * (grad_probs - delta)).astype(BF)
-            span = pl.ds(0, extent)
-            value_sum[span] += dot_nn(probs.astype(BF), grad_rows)
-            key_sum[span] += dot_nn(grad_scores, query)
-            grad_query = dot_nn(key_t[:, :extent], grad_scores)
-            out[0, here, lanes] = (grad_query.T * 0.125).astype(BF)
-        out[0, :, key_lanes] = (key_sum[...] * 0.125).astype(BF)
-        out[0, :, value_lanes] = value_sum[...].astype(BF)
-
-
-def attend_back(lengths, slopes, qkv, attention, grad, totals):
-    slots, rows, _width = qkv.shape
-    return pl.pallas_call(
-        attend_back_body,
-        grid=(slots,),
-        out_shape=jax.ShapeDtypeStruct((slots, rows, 6 * HEAD), BF),
-        in_specs=[
-            pl.BlockSpec(memory_space=pltpu.SMEM),
-            pl.BlockSpec(memory_space=pltpu.SMEM),
-            pl.BlockSpec((1, rows, 6 * HEAD), lambda s: (s, 0, 0)),
-            pl.BlockSpec((1, rows, 2 * HEAD), lambda s: (s, 0, 0)),
-            pl.BlockSpec((1, rows, 2 * HEAD), lambda s: (s, 0, 0)),
-            pl.BlockSpec((1, 2, rows), lambda s: (s, 0, 0)),
-        ],
-        out_specs=pl.BlockSpec((1, rows, 6 * HEAD), lambda s: (s, 0, 0)),
-        scratch_shapes=[
-            pltpu.VMEM((rows, QB), F32),
-            pltpu.VMEM((rows, HEAD), F32),
-            pltpu.VMEM((rows, HEAD), F32),
-        ],
-        name="attend_back",
-    )(lengths, slopes, qkv, attention, grad, totals)
+        compiler_params=pltpu.CompilerParams(
+            collective_id=11, has_side_effects=True, vmem_limit_bytes=VMEM_MAX
+        ),
+        name="front",
+    )(lengths, slopes, hidden_all, attn_all, ffn_all, vectors, qkv_b, down_own)
+
+
+VMEM_MAX = 62 * 1024 * 1024
 
 
 def norm_stats(values):
@@ -1239,7 +1073,7 @@
     residual,
     grad_resid,
     sums,
-    ffn_g,
+    ffn_sum,
     grad_up_b,
     second_all,
     second_share,
@@ -1249,6 +1083,8 @@
     pre_t,
     own_rows,
     grad_second,
+    ffn_g,
+    ffn_in,
     from_pair,
     summed,
     from_x,
@@ -1261,8 +1097,11 @@
     h_recv,
     local,
     w_sems,
+    z_send,
+    z_recv,
 ):
     width = hidden.shape[-1]
+    layer = lax.axis_index("tp")
     units = depth * BLK
     loads = []
     for up in range(depth):
@@ -1277,7 +1116,7 @@
             )
     for load in loads:
         load.start()
-    greet(wide_square(square_places()))
+    greet(wide_square(square_places()) + line_others(depth))
     step = 32
 
     def norm_part(index, carry):
@@ -1345,14 +1184,33 @@
             total = total + dot_nn(left[rows, pl.ds(8 * BLK, 8 * BLK)], right[1])
             total = total.astype(BF)
             for blk in range(8):
-                ffn_g[up, blk, kind] = total[:, blk * BLK : (blk + 1) * BLK]
+                ffn_g[kind, up, blk] = total[:, blk * BLK : (blk + 1) * BLK]
             return carry
 
         lax.fori_loop(0, depth, one, 0)
 
+    def line_copies(kind):
+        made = []
+        for up in range(1, depth):
+            goal = (layer + up) % depth
+            made.append(
+                remote(
+                    ffn_g.at[kind, goal],
+                    ffn_in.at[kind, up - 1],
+                    z_send.at[kind, up - 1],
+                    z_recv.at[kind, up - 1],
+                    {"tp": goal},
+                )
+            )
+        return made
+
     weight_grads(pre_t, second_all, 0)
+    for copy in line_copies(0):
+        copy.start()
     scatter.middle()
     weight_grads(act_t, down_all, 1)
+    for copy in line_copies(1):
+        copy.start()
     scatter.finish()
     gather.sent()
 
@@ -1378,6 +1236,20 @@
     again.first()
     again.second()
     again.third()
+    for kind in range(2):
+        for copy in line_copies(kind):
+            copy.wait_recv()
+
+        def add_block(blk, carry, kind=kind):
+            total = ffn_g[kind, layer, blk].astype(F32)
+            for up in range(depth - 1):
+                total = total + ffn_in[kind, up, blk].astype(F32)
+            ffn_sum[blk, kind] = total.astype(BF)
+            return carry
+
+        lax.fori_loop(0, 8, add_block, 0)
+        for copy in line_copies(kind):
+            copy.wait_send()
     again.finish()
 
 
@@ -1395,7 +1267,7 @@
             rows,
             rows,
             jax.ShapeDtypeStruct((8, width), F32),
-            jax.ShapeDtypeStruct((depth, 8, 2, BLK, BLK), BF),
+            jax.ShapeDtypeStruct((8, 2, BLK, BLK), BF),
             jax.ShapeDtypeStruct((1, units), F32),
         ],
         in_specs=[vmem()] * 7 + [hbm()],
@@ -1409,6 +1281,8 @@
             pltpu.VMEM((units, 16 * BLK), BF),
             pltpu.VMEM((2, BLK, width), BF),
             pltpu.VMEM((2, BLK, width), F32),
+            pltpu.VMEM((2, depth, 8, BLK, BLK), BF),
+            pltpu.VMEM((2, depth - 1, 8, BLK, BLK), BF),
         ]
         + single_scratch(width)
         + [
@@ -1418,9 +1292,11 @@
             dma((SquareGather.SENDS,)),
             dma((2,)),
             dma((2, 8 * depth)),
+            dma((2, depth - 1)),
+            dma((2, depth - 1)),
         ],
         compiler_params=pltpu.CompilerParams(
-            collective_id=13, has_side_effects=True, vmem_limit_bytes=62 * 1024 * 1024
+            collective_id=13, has_side_effects=True, vmem_limit_bytes=VMEM_MAX
         ),
         name="middle",
     )(hidden, branch, vectors, up_b, cotangent, valid, down_all, ffn_z)
@@ -1435,6 +1311,386 @@
         pltpu.SemaphoreType.DMA((SquareScatter.SENDS,)),
         pltpu.SemaphoreType.DMA((SquareScatter.SENDS,)),
     ]
+
+
+class WideExchange:
+    def __init__(self, source, target, send, recv):
+        own = lax.axis_index("wide")
+        self.copies = [
+            remote(
+                source((own + step) % 8),
+                target(own),
+                send.at[step - 1],
+                recv.at[step - 1],
+                {"wide": (own + step) % 8},
+            )
+            for step in range(1, 8)
+        ]
+
+    def start(self):
+        for copy in self.copies:
+            copy.start()
+
+    def arrive(self):
+        for copy in self.copies:
+            copy.wait_recv()
+
+    def sent(self):
+        for copy in self.copies:
+            copy.wait_send()
+
+
+def back_body(
+    depth,
+    lengths,
+    slopes,
+    hidden,
+    residual,
+    grad_resid,
+    valid,
+    vectors,
+    branch_all,
+    attn_all,
+    qkv,
+    attention,
+    totals,
+    normed,
+    down_share,
+    mid_sums,
+    grad_up_b,
+    ffn_sum,
+    output,
+    grad_in,
+    vec_sums,
+    unit_sums,
+    grad_q,
+    grad_k,
+    grad_v,
+    grad_d,
+    grad_up,
+    grad_down,
+    grad_att,
+    grad_qkv,
+    share,
+    qkv_w,
+    dense_w,
+    bias,
+    key_sum,
+    value_sum,
+    down_out,
+    grad_normed,
+    attn_g,
+    attn_in,
+    attn_z,
+    ffn_in,
+    parts,
+    gathered,
+    d_pair,
+    d_summed,
+    d_x,
+    d_y,
+    d_send,
+    d_recv,
+    n_pair,
+    n_summed,
+    n_x,
+    n_y,
+    n_send,
+    n_recv,
+    w_sems,
+    f_send,
+    f_recv,
+    a_send,
+    a_recv,
+    z_send,
+    z_recv,
+    v_send,
+    v_recv,
+):
+    own = lax.axis_index("wide")
+    layer = lax.axis_index("tp")
+    per_layer = 8 // depth
+    width = hidden.shape[-1]
+    step = 32
+    others = [
+        ((own + side) % 8, (layer + up) % depth)
+        for up in range(depth)
+        for side in range(8)
+        if up or side
+    ]
+    loads = weight_loads(attn_all, qkv_w, dense_w, w_sems)
+    for load in loads:
+        load.start()
+    greet([{"wide": wide, "tp": tp} for wide, tp in others])
+    down = SquareScatter(down_share, down_out, d_pair, d_summed, d_x, d_y, d_send, d_recv)
+    down.start()
+    ffn = WideExchange(lambda dev: ffn_sum.at[dev], lambda dev: ffn_in.at[dev], f_send, f_recv)
+    ffn.start()
+    for load in loads:
+        load.wait()
+
+    def att_block(index, carry):
+        slot = index // 4
+        rows = pl.ds(pl.multiple_of((index % 4) * QB, QB), QB)
+        grad_att[slot, rows] = dot_nt(branch_all[slot, rows], dense_w[...]).astype(BF)
+        return carry
+
+    lax.fori_loop(0, 8, att_block, 0)
+    for chip in range(3):
+        down.near(chip)
+    dense_part = dot_nn(attention[0].T, branch_all[0]) + dot_nn(attention[1].T, branch_all[1])
+    dense_part = dense_part.astype(BF)
+    for blk in range(8):
+        attn_g[blk, 3] = dense_part[:, blk * BLK : (blk + 1) * BLK]
+    kinds = (pl.ds(3, 1), pl.ds(0, 3))
+    exchanges = [
+        WideExchange(
+            lambda dev, kind=kind: attn_g.at[dev, kind],
+            lambda dev, kind=kind: attn_in.at[dev, kind],
+            a_send.at[group],
+            a_recv.at[group],
+        )
+        for group, kind in enumerate(kinds)
+    ]
+
+    def onward(group, index, source):
+        return remote(
+            source.at[index, kinds[group]],
+            attn_z.at[layer, index % per_layer, kinds[group]],
+            z_send.at[group, index],
+            z_recv.at[group, layer, index % per_layer],
+            {"tp": index // per_layer},
+        )
+
+    def forward(group, index, source):
+        @pl.when(index // per_layer != layer)
+        def _():
+            onward(group, index, source).start()
+
+    def forward_all(group):
+        for number in range(1, 8):
+            exchanges[group].copies[number - 1].wait_recv()
+            forward(group, (own + 8 - number) % 8, attn_in)
+
+    exchanges[0].start()
+    forward(0, own, attn_g)
+
+    def slot_back(slot, carry):
+        attend_slot_back(
+            slot,
+            lengths[slot],
+            slopes,
+            qkv,
+            attention,
+            grad_att,
+            totals,
+            grad_qkv,
+            bias,
+            key_sum,
+            value_sum,
+        )
+
+        @pl.when(slot == 0)
+        def _():
+            forward_all(0)
+            down.middle()
+
+        return carry
+
+    lax.fori_loop(0, 2, slot_back, 0)
+
+    weight_part = dot_nn(grad_qkv[0].T, normed[0]) + dot_nn(grad_qkv[1].T, normed[1])
+    weight_part = weight_part.astype(BF)
+    for kind in range(3):
+        for blk in range(8):
+            attn_g[blk, kind] = weight_part[
+                kind * BLK : (kind + 1) * BLK, blk * BLK : (blk + 1) * BLK
+            ]
+    exchanges[1].start()
+    forward(1, own, attn_g)
+    scatter = SquareScatter(share, grad_normed, n_pair, n_summed, n_x, n_y, n_send, n_recv)
+
+    def compute(index, carry):
+        rows = pl.ds(pl.multiple_of(relation(index) * BLK, BLK), BLK)
+        values = grad_qkv[:, rows].reshape(2 * BLK, 6 * HEAD)
+        share[:, rows] = dot_nt(values, qkv_w[...]).astype(BF).reshape(2, BLK, width)
+        return carry
+
+    for chip in range(4):
+        start = (6, 2, 4, 0)[chip]
+        lax.fori_loop(start, start + 2, compute, 0)
+        scatter.pairs[chip].start()
+        if chip:
+            scatter.near(chip - 1)
+    head_sum = jnp.sum(grad_qkv[0].astype(F32), axis=0, keepdims=True)
+    head_sum = head_sum + jnp.sum(grad_qkv[1].astype(F32), axis=0, keepdims=True)
+    down.near(3)
+    down.finish()
+
+    def out_part(index, carry):
+        rows = pl.ds(pl.multiple_of(index * step, step), step)
+        for slot in range(2):
+            total = residual[slot, rows] + down_out[slot, rows] + vectors[5:6]
+            output[slot, rows] = (valid[slot, rows][:, :1] * total).astype(BF)
+        return carry
+
+    lax.fori_loop(0, BLK // step, out_part, 0)
+    forward_all(1)
+    scatter.near(3)
+    ffn.arrive()
+    ffn_in[own] = ffn_sum[own]
+    for blk in range(8):
+        lanes = slice(blk * BLK, (blk + 1) * BLK)
+        grad_up[:, lanes] = ffn_in[blk, 0].astype(F32).T
+        grad_down[lanes] = ffn_in[blk, 1].astype(F32)
+    scatter.middle()
+    for blk in range(8):
+        lanes = slice(blk * BLK, (blk + 1) * BLK)
+        for place in range(4):
+            parts[blk, pl.ds(2 + place, 1)] = mid_sums[place : place + 1, lanes]
+        for place in range(depth):
+            parts[blk, pl.ds(6 + place, 1)] = grad_up_b[:, place * BLK : (place + 1) * BLK]
+        parts[blk, pl.ds(6 + depth, 1)] = head_sum[:, : 2 * HEAD]
+        parts[blk, pl.ds(7 + depth, 1)] = head_sum[:, 4 * HEAD :]
+    scatter.finish()
+
+    def back_part(index, carry):
+        gain_sum, shift_sum = carry
+        rows = pl.ds(pl.multiple_of(index * step, step), step)
+        for slot in range(2):
+            hat, inverse = norm_stats(hidden[slot, rows].astype(F32))
+            grad = grad_normed[slot, rows]
+            total = grad_resid[slot, rows] + norm_back_rows(grad, hat, inverse, vectors[0:1])
+            grad_in[slot, rows] = total.astype(BF)
+            gain_sum = gain_sum + jnp.sum(grad * hat, axis=0, keepdims=True)
+            shift_sum = shift_sum + jnp.sum(grad, axis=0, keepdims=True)
+        return gain_sum, shift_sum
+
+    zero = jnp.zeros((1, width), F32)
+    gain_sum, shift_sum = lax.fori_loop(0, BLK // step, back_part, (zero, zero))
+    for blk in range(8):
+        lanes = slice(blk * BLK, (blk + 1) * BLK)
+        parts[blk, pl.ds(0, 1)] = gain_sum[:, lanes]
+        parts[blk, pl.ds(1, 1)] = shift_sum[:, lanes]
+    sum_copies = [
+        remote(
+            parts.at[wide],
+            gathered.at[own, layer],
+            v_send.at[index],
+            v_recv.at[index],
+            {"wide": wide, "tp": tp},
+        )
+        for index, (wide, tp) in enumerate(others)
+    ]
+    for copy in sum_copies:
+        copy.start()
+    gathered[own, layer] = parts[own]
+
+    for group in range(2):
+        for up in range(1, depth):
+            source = (layer + up) % depth
+            for piece in range(per_layer):
+                remote(
+                    attn_in.at[piece, kinds[group]],
+                    attn_z.at[source, piece, kinds[group]],
+                    z_send.at[group, piece],
+                    z_recv.at[group, source, piece],
+                    {"tp": source},
+                ).wait_recv()
+    attn_in[own] = attn_g[own]
+    for piece in range(per_layer):
+        for kind, target in enumerate((grad_q, grad_k, grad_v, grad_d)):
+            total = attn_in[layer * per_layer + piece, kind].astype(F32)
+            for up in range(1, depth):
+                total = total + attn_z[(layer + up) % depth, piece, kind].astype(F32)
+            lanes = slice(piece * BLK, (piece + 1) * BLK)
+            if kind < 3:
+                target[:, lanes] = total.T
+            else:
+                target[lanes] = total
+    for copy in sum_copies:
+        copy.wait_recv()
+
+    def unit_part(dev, carry):
+        total = gathered[dev, 0]
+        for up in range(1, depth):
+            total = total + gathered[dev, up]
+        unit_sums[dev] = total
+        return carry + total
+
+    vec_sums[...] = lax.fori_loop(0, 8, unit_part, jnp.zeros((16, BLK), F32))
+    for copy in sum_copies:
+        copy.wait_send()
+    ffn.sent()
+    for group in range(2):
+        exchanges[group].sent()
+        for index in range(8):
+
+            @pl.when(index // per_layer != layer)
+            def _(index=index, group=group):
+                onward(group, index, attn_in).wait_send()
+
+
+def back(depth, *operands):
+    width = operands[2].shape[-1]
+    dma = pltpu.SemaphoreType.DMA
+    smem = pl.BlockSpec(memory_space=pltpu.SMEM)
+    per_layer = 8 // depth
+    rows = jax.ShapeDtypeStruct((2, BLK, width), BF)
+    square = jax.ShapeDtypeStruct((BLK, per_layer * BLK), F32)
+    peers = 8 * depth - 1
+    return pl.pallas_call(
+        functools.partial(back_body, depth),
+        out_shape=[
+            rows,
+            rows,
+            jax.ShapeDtypeStruct((16, BLK), F32),
+            jax.ShapeDtypeStruct((8, 16, BLK), F32),
+            square,
+            square,
+            square,
+            jax.ShapeDtypeStruct((per_layer * BLK, BLK), F32),
+            jax.ShapeDtypeStruct((BLK, 8 * BLK), F32),
+            jax.ShapeDtypeStruct((8 * BLK, BLK), F32),
+        ],
+        in_specs=[smem, smem] + [vmem()] * 6 + [hbm()] + [vmem()] * 8,
+        out_specs=[vmem()] * 10,
+        scratch_shapes=[
+            pltpu.VMEM((2, 8 * BLK, 2 * HEAD), BF),
+            pltpu.VMEM((2, 8 * BLK, 6 * HEAD), BF),
+            pltpu.VMEM((2, 8 * BLK, width), BF),
+            pltpu.VMEM((width, 6 * HEAD), BF),
+            pltpu.VMEM((2 * HEAD, width), BF),
+            pltpu.VMEM((8 * BLK, QB), F32),
+            pltpu.VMEM((8 * BLK, HEAD), F32),
+            pltpu.VMEM((8 * BLK, HEAD), F32),
+            pltpu.VMEM((2, BLK, width), F32),
+            pltpu.VMEM((2, BLK, width), F32),
+            pltpu.VMEM((8, 4, BLK, BLK), BF),
+            pltpu.VMEM((8, 4, BLK, BLK), BF),
+            pltpu.VMEM((depth, per_layer, 4, BLK, BLK), BF),
+            pltpu.VMEM((8, 2, BLK, BLK), BF),
+            pltpu.VMEM((8, 16, BLK), F32),
+            pltpu.VMEM((8, depth, 16, BLK), F32),
+        ]
+        + single_scratch(width)
+        + single_scratch(width)
+        + [
+            dma((4, 8)),
+            dma((7,)),
+            dma((7,)),
+            dma((2, 7)),
+            dma((2, 7)),
+            dma((2, 8)),
+            dma((2, depth, per_layer)),
+            dma((peers,)),
+            dma((peers,)),
+        ],
+        compiler_params=pltpu.CompilerParams(
+            collective_id=12, has_side_effects=True, vmem_limit_bytes=VMEM_MAX
+        ),
+        name="back",
+    )(*operands)
 
 
 def square_device(
@@ -1484,10 +1740,7 @@
         [pre_gain, pre_shift, mid_gain, mid_shift, b_dense, b_down, b_up.reshape(-1), head_row]
     ).astype(F32)
     hidden_all, attn_all, ffn_all, vec_all = first_exchange(depth, hidden_in, attn_w, ffn_w, vec)
-    ffn_z = lax.all_gather(ffn_all, "tp", axis=0, tiled=False)
-
     vectors = vec_all[:, 0].transpose(1, 0, 2).reshape(8, width)
-    gain_one, shift_one = vectors[0], vectors[1]
     up_b = vec_all[:, :, 6].reshape(8, depth, heads_dev, 4 * 8).transpose(1, 2, 0, 3)
     up_b = lax.dynamic_index_in_dim(up_b.reshape(depth, 8, BLK), own, 1, False).reshape(-1)
     span = heads_dev * 8
@@ -1498,92 +1751,86 @@
         return lax.dynamic_index_in_dim(full, own, 0, False)
 
     qkv_b = jnp.concatenate([head_vector(0), jnp.zeros((2 * HEAD,), F32), head_vector(1)])
-    qkv_w = attn_all[:3].reshape(3, width, BLK).transpose(1, 0, 2).reshape(width, 3 * BLK)
-    dense_w = attn_all[3].transpose(1, 0, 2).reshape(BLK, width)
-    normed = norm_stats(hidden_all.astype(F32))[0] * gain_one + shift_one
-    normed = normed.astype(BF)
-    qkv = (row_product(normed, qkv_w) + qkv_b).astype(BF)
-    attention, totals = attend(own_lengths, slopes, qkv)
-    branch = square_scatter(row_product(attention, dense_w).astype(BF))[0]
-
-    hidden = hidden_in.astype(F32)
     places = own * BLK + jnp.arange(BLK, dtype=jnp.int32)
     validity = (places[None, :] < own_lengths[:, None]).astype(F32)[:, :, None]
-    grad_output = validity * cotangent.astype(F32)
-    down_all = square_gather(grad_output.astype(BF))[0]
-    branch_all, down_share, residual, grad_resid, mid_sums, ffn_g, grad_up_b = middle(
+    down_own = (validity * cotangent.astype(F32)).astype(BF)
+    valid = jnp.broadcast_to(validity, (2, BLK, BLK))
+    normed, qkv, attention, totals, branch, down_all, ffn_z = front(
+        depth,
+        own_lengths,
+        slopes,
+        hidden_all,
+        attn_all,
+        ffn_all,
+        vectors,
+        qkv_b.reshape(1, -1),
+        down_own,
+    )
+    branch_all, down_share, residual, grad_resid, mid_sums, ffn_sum, grad_up_b = middle(
         depth,
         hidden_in,
         branch,
         vectors,
         up_b.reshape(1, -1),
         cotangent,
-        jnp.broadcast_to(validity, (2, BLK, BLK)),
+        valid,
         down_all,
         ffn_z,
     )
-    grad_up_b = grad_up_b[0]
-    ffn_g = lax.psum_scatter(ffn_g, "tp", scatter_dimension=0, tiled=False)
-    down_out = square_scatter(down_share)[0]
-    output = (validity * (residual + down_out + vectors[5])).astype(BF)
-    grad_attention = times_transposed(branch_all, dense_w).astype(BF)
-    grad_dense = inner_rows(attention, branch_all).astype(BF)
-    grad_qkv = attend_back(own_lengths, slopes, qkv, attention, grad_attention, totals)
-    normed_share = times_transposed(grad_qkv, qkv_w).astype(BF)
-    grad_qkv_w = inner_rows(normed, grad_qkv).astype(BF)
-    grad_qkv_b = jnp.sum(flatten_rows(grad_qkv), axis=0, dtype=F32)
-    attn_g = jnp.concatenate(
-        [
-            grad_qkv_w.reshape(8, BLK, 3, BLK).transpose(0, 2, 1, 3),
-            grad_dense.reshape(BLK, 8, BLK).transpose(1, 0, 2)[:, None],
-        ],
-        1,
-    )
-    grad_normed, attn_sum, ffn_sum = last_exchange(depth, normed_share, attn_g, ffn_g)
-
-    hat_one, inverse_one = norm_stats(hidden)
-    grad_in = (grad_resid + norm_back_rows(grad_normed, hat_one, inverse_one, gain_one)).astype(BF)
-
-    def token_sum(values):
-        return jnp.sum(values, axis=(0, 1))
-
-    parts = jnp.concatenate(
-        [jnp.stack([token_sum(grad_normed * hat_one), token_sum(grad_normed)]), mid_sums[:4]]
-    )
-    parts = parts.reshape(6, 8, BLK).transpose(1, 0, 2)
-    own_sums = jnp.concatenate([grad_up_b, grad_qkv_b[: 2 * HEAD], grad_qkv_b[4 * HEAD :]])
-    own_sums = jnp.broadcast_to(own_sums.reshape(1, -1, BLK), (8, depth + 2, BLK))
-    pad = jnp.zeros((8, 16 - 8 - depth, BLK), F32)
-    sums = share_sums(depth, jnp.concatenate([parts, own_sums, pad], 1))
-    vec_sums = jnp.sum(sums[:, :, :6], axis=(0, 1))
-    unit_sums = jnp.sum(sums[:, :, 6 : 8 + depth], axis=1)
-    up_sum = unit_sums[:, :depth].transpose(1, 0, 2).reshape(2 * HEAD // 8, 8 * depth * BLK // 16)
-    head_sums = unit_sums[:, depth:].transpose(1, 0, 2).reshape(2, 16, HEAD)
+    (
+        output,
+        grad_in,
+        vec_sums,
+        unit_sums,
+        grad_q,
+        grad_k,
+        grad_v,
+        grad_d,
+        grad_up,
+        grad_down,
+    ) = back(
+        depth,
+        own_lengths,
+        slopes,
+        hidden_in,
+        residual,
+        grad_resid,
+        valid,
+        vectors,
+        branch_all,
+        attn_all,
+        qkv,
+        attention,
+        totals,
+        normed,
+        down_share,
+        mid_sums,
+        grad_up_b,
+        ffn_sum,
+    )
+    up_sum = unit_sums[:, 6 : 6 + depth].transpose(1, 0, 2).reshape(16, 2 * depth * HEAD // 2)
+    head_sums = unit_sums[:, 6 + depth : 8 + depth].transpose(1, 0, 2).reshape(2, 16, HEAD)
 
     def own_block(tensor, size):
         return lax.dynamic_slice(tensor, (layer * heads_dev, own * size), (heads_dev, size))
 
-    def side_by_side(blocks):
-        return blocks.transpose(1, 0, 2).reshape(BLK, -1)
-
-    ffn_sum = ffn_sum.astype(F32)
     return (
         output,
         grad_in,
         vec_sums[0],
         vec_sums[1],
-        side_by_side(attn_sum[:, 0]),
-        side_by_side(attn_sum[:, 1]),
-        side_by_side(attn_sum[:, 2]),
+        grad_q,
+        grad_k,
+        grad_v,
         own_block(head_sums[0], 8),
         own_block(head_sums[1], 8),
-        attn_sum[:, 3].reshape(per_layer * BLK, BLK),
+        grad_d,
         vec_sums[2],
         vec_sums[3],
         vec_sums[4],
-        ffn_sum[:, 0].reshape(8 * BLK, BLK).T,
+        grad_up,
         own_block(up_sum, 4 * 8),
-        ffn_sum[:, 1].reshape(8 * BLK, BLK),
+        grad_down,
         vec_sums[5],
     )
 

time: 354 us -> 307 us (0.87)
  matrix products: 24.8 us -> 0 us
  other arithmetic: 22.7 us -> 5.61 us
  between operations: 14.6 us -> 0.87 us
  local copies, waits for them, and re-layouts: 24.3 us -> 31.7 us
    dot_general x6 -> x0, matrix products: 24.8 us -> none  [the longest x2 8.52 us: times_transposed(): lax.dot_general(first_op, second_op, (((first_op.ndim - 1,), (1,)), ((),...]
    reduce_sum x7 -> x0, other arithmetic: 11.9 us -> none  [the longest x2 4.19 us: norm_stats(): spread = jnp.mean(centred * centred, axis=-1, keepdims=True)]
    unnamed x39 -> x20, local copies, waits for them, and re-layouts: 6.32 us -> 16.7 us
    pallas_call x1, Pallas kernels: 75.5 us -> 81.2 us  [middle(): pl.pallas_call(functools.partial(middle_body, depth), out_shape=[tokens,...]
    pallas_call x7 -> x2, Pallas kernels: 148 us -> 144 us  [the longest x1 82.1 us: back(): pl.pallas_call(functools.partial(back_body, depth), out_shape=[rows, rows...]
  transfers between devices with their start and end apart: 2 -> 0, of which waited for: 0 -> 0; matrix products, arithmetic and copies ran while one was open for 13% -> 0% of each run, Pallas kernels for 27% -> 0%
where the time goes in v3:
time: 307 us; the launch traced here: 306 us
  Pallas kernels  268 us (87%)
  local copies, waits for them, and re-layouts  31.7 us (10%)
  other arithmetic  5.61 us (2%)
    pallas_call x1, Pallas kernels, back(): pl.pallas_call(functools.partial(back_body, depth), out_shape=[rows, rows...  82.1 us
    pallas_call x1, Pallas kernels, middle(): pl.pallas_call(functools.partial(middle_body, depth), out_shape=[tokens,...  81.2 us
    pallas_call x1, Pallas kernels, front(): pl.pallas_call(functools.partial(front_body, depth), out_shape=[tokens, j...  61.9 us
    pallas_call x1, Pallas kernels, first_exchange(): pl.pallas_call(functools.partial(first_body, depth), out_shape=[jax.Shape...  43.1 us
    unnamed x20, local copies, waits for them, and re-layouts  16.7 us

profile of v3, /device:TPU:0, one launch (start us, length us, event | category | flops | bytes accessed | tf_op | source)
XLA Modules:
  0.0 306.5 jit_solution(2074458304451152286)
XLA Ops:
  0.7 0.0 copy-start.3
  0.7 0.0 copy-start
  0.7 1.2 copy.43
  1.9 0.2 copy.44
  2.1 1.8 pad_maximum_fusion.ffn_w
  3.9 0.9 copy.37
  4.8 0.1 copy.38
  4.9 1.0 copy.39
  5.9 0.1 copy.40
  6.0 1.0 copy.41
  7.0 0.1 copy.42
  7.1 1.6 pad_maximum_fusion.1.attn_w
  8.7 0.8 reshape.113
  9.5 0.8 reshape.114
  10.2 0.1 maximum_bitcast_fusion
  10.3 0.8 stack_reshape.11
  11.1 0.8 stack.55
  11.8 0.6 convert_element_type.20.vec
  12.4 43.1 %first_exchange.1 = (bf16[2,1024,1024]{2,1,0:T(8,128)(2,1)}, bf16[4,8,128,128]{3,2,1,0:T(8,128)(2,1)}, bf16[2,8,128,128]{3,2,1,0:T(8,128)(2,1)}, f32[8,4,8,128]{3,2,1,0:T(8,128)}) custom-call(bf16[2,128,1024]{2,1,0:T(8,128)(2,1)} %hidden.5, bf16[2,4,128,128]{3,2,1,0:T(8,128)(2,1)} %pad_maximum_fusion.1.attn_w, ...), custom_call_target="tpu_custom_call" | custom-call | tf_op jit(solution)/shard_map/first_exchange/pallas_call | solution.py:751
  55.5 1.1 slice_reduce_fusion.2
  56.6 0.1 reshape_squeeze.9
  56.8 0.1 reshape.116
  56.9 0.1 reshape_squeeze.10
  57.0 0.1 reshape.117
  57.1 0.6 reshape.118.qkv_b
  57.7 0.0 copy-done.3
  57.7 0.1 dynamic_slice.23.lengths
  57.8 0.0 copy-start.2
  57.8 0.1 compare_convert_fusion
  57.8 0.0 copy-done
  57.9 0.9 multiply_convert_fusion.down_own
  58.8 0.5 exponential_multiply_fusion.slopes
  59.3 1.4 slice_bitcast_fusion.vectors
  60.7 0.0 copy-done.2
  60.7 61.9 %front.1 = (bf16[2,1024,1024]{2,1,0:T(8,128)(2,1)}, bf16[2,1024,384]{2,1,0:T(8,128)(2,1)}, bf16[2,1024,128]{2,1,0:T(8,128)(2,1)}, f32[2,2,1024]{2,1,0:T(2,128)},...) custom-call(s32[2]{0:T(128)} %copy-done.2, ...), custom_call_target="tpu_custom_call" | custom-call | tf_op jit(solution)/shard_map/front/pallas_call | solution.py:991
  122.6 1.0 slice_reduce_fusion
  123.6 0.1 reshape_squeeze.11
  123.7 0.1 reshape.119
  123.8 0.6 dynamic-slice_bitcast_fusion.up_b
  124.4 0.8 broadcast_in_dim.16.valid
  125.2 81.2 %middle.1 = (bf16[2,1024,1024]{2,1,0:T(8,128)(2,1)}, bf16[2,1024,1024]{2,1,0:T(8,128)(2,1)}, f32[2,128,1024]{2,1,0:T(8,128)}, f32[2,128,1024]{2,1,0:T(8,128)}, f...) custom-call(bf16[2,128,1024]{2,1,0:T(8,128)(2,1)} %hidden.5, ...), custom_call_target="tpu_custom_call" | custom-call | tf_op jit(solution)/shard_map/middle/pallas_call | solution.py:1262
  206.4 82.1 %back.1 = (bf16[2,128,1024]{2,1,0:T(8,128)(2,1)}, bf16[2,128,1024]{2,1,0:T(8,128)(2,1)}, f32[16,128]{1,0:T(8,128)}, f32[8,16,128]{2,1,0:T(8,128)}, f32[128,256]{...) custom-call(s32[2]{0:T(128)} %copy-done.2, ...), custom_call_target="tpu_custom_call" | custom-call | tf_op jit(solution)/shard_map/back/pallas_call | solution.py:1642
  288.5 0.0 copy-start.1
  288.5 0.9 slice_bitcast_fusion.1
  289.4 0.7 dynamic_slice.29
  290.1 0.8 slice_bitcast_fusion.2
  290.9 0.1 squeeze.41
  291.0 0.7 dynamic_slice.27
  291.6 0.1 squeeze.42
  291.7 0.7 dynamic_slice.28
  292.3 1.4 slice_bitcast_fusion.3
  293.8 1.9 copy.59
  295.6 1.9 copy.60
  297.5 1.6 copy.61
  299.1 1.6 copy.62
  300.6 1.6 copy.63
  302.2 1.6 copy.64
  303.8 1.9 copy.65
  305.7 0.0 copy-done.1
  305.7 0.8 copy.66
  (11 shorter events, 0.1 us)
Async XLA Ops:
  0.7 57.0 %copy-start.3 = (s32[8]{0:T(128)S(1)}, s32[8]{0:T(128)}, u32[]{:S(2)}) copy-start(s32[8]{0:T(128)} %param.19) | copy-start | bytes 100
  0.7 57.2 %copy-start = (bf16[2,128,1024]{2,1,0:T(8,128)(2,1)S(1)}, bf16[2,128,1024]{2,1,0:T(8,128)(2,1)}, u32[]{:S(2)}) copy-start(bf16[2,128,1024]{2,1,0:T(8,128)(2,1)} %cotangent.1) | copy-start | bytes 1572868
  57.8 2.9 copy-start.2
  288.5 17.2 %copy-start.1 = (f32[1024,128]{1,0:T(8,128)S(1)}, f32[1024,128]{1,0:T(8,128)}, u32[]{:S(2)}) copy-start(f32[1024,128]{1,0:T(8,128)} %get-tuple-element.117) | copy-start | bytes 1572868

commit v4 on v0

--- a/solution.py
+++ b/solution.py
@@ -1,11 +1,15 @@
+import functools
 import math
 
 import jax
 import jax.numpy as jnp
 from jax import lax
+from jax.experimental import pallas as pl
+from jax.experimental.pallas import tpu as pltpu
 from jax.sharding import PartitionSpec as P
 
 HEAD = 64
+MESH = pl.DeviceIdType.MESH
 
 
 def norm_rows(values, gain_vec, shift_vec):
@@ -363,9 +367,1360 @@
     )
 
 
+BF = jnp.bfloat16
+F32 = jnp.float32
+LOG2E = 1.4426950408889634
+NEG = -1e30
+BLK = 128
+
+
+def hbm():
+    return pl.BlockSpec(memory_space=pl.ANY)
+
+
+def vmem():
+    return pl.BlockSpec(memory_space=pltpu.VMEM)
+
+
+def square_places():
+    own = lax.axis_index("wide")
+    core = own % 2
+    col = (own // 2) % 2
+    row = own // 4
+    pair = own + 1 - 2 * core
+    along_x = own + 2 - 4 * col
+    along_y = own + 4 - 8 * row
+    return own, pair, along_x, along_y, along_x + along_y - own
+
+
+def greet(targets):
+    barrier = pltpu.get_barrier_semaphore()
+    for target in targets:
+        pl.semaphore_signal(barrier, inc=1, device_id=target, device_id_type=MESH)
+    pl.semaphore_wait(barrier, len(targets))
+
+
+def remote(src, dst, send_sem, recv_sem, target):
+    return pltpu.make_async_remote_copy(
+        src_ref=src,
+        dst_ref=dst,
+        send_sem=send_sem,
+        recv_sem=recv_sem,
+        device_id=target,
+        device_id_type=MESH,
+    )
+
+
+class SquareGather:
+    SENDS = 13
+
+    def __init__(self, src, dst, send, recv, local):
+        own, pair, ax, ay, dg = square_places()
+
+        def place(slot, dev):
+            return dst.at[slot, pl.ds(pl.multiple_of(dev * BLK, BLK), BLK)]
+
+        def both(dev):
+            return dst.at[:, pl.ds(pl.multiple_of(dev * BLK, BLK), BLK)]
+
+        to_x, to_y, to_p = {"wide": ax}, {"wide": ay}, {"wide": pair}
+        self.local = pltpu.make_async_copy(src, both(own), local)
+        copies = {}
+        copies["x0"] = remote(src.at[0], place(0, own), send.at[0], recv.at[0], to_x)
+        copies["x1"] = remote(src.at[1], place(1, own), send.at[1], recv.at[1], to_x)
+        copies["y0"] = remote(src.at[0], place(0, own), send.at[2], recv.at[2], to_y)
+        copies["y1"] = remote(src.at[1], place(1, own), send.at[3], recv.at[3], to_y)
+        copies["d0"] = remote(place(0, ay), place(0, ay), send.at[4], recv.at[4], to_x)
+        copies["d1"] = remote(place(1, ax), place(1, ax), send.at[5], recv.at[5], to_y)
+        copies["p"] = remote(src, both(own), send.at[6], recv.at[6], to_p)
+        for index, (name, slot, dev) in enumerate(
+            (("x0", 0, ax), ("x1", 1, ax), ("y0", 0, ay), ("y1", 1, ay), ("d0", 0, dg), ("d1", 1, dg))
+        ):
+            copies["p" + name] = remote(
+                place(slot, dev), place(slot, dev), send.at[7 + index], recv.at[7 + index], to_p
+            )
+        self.copies = copies
+
+    def start(self):
+        for name in ("y0", "x1", "x0", "y1", "p"):
+            self.copies[name].start()
+        self.local.start()
+
+    def pass_on(self, arrived, sends):
+        self.copies[arrived].wait_recv()
+        for name in sends:
+            self.copies[name].start()
+
+    def first(self):
+        self.pass_on("y0", ("d0", "py0"))
+        self.pass_on("x1", ("d1", "px1"))
+
+    def second(self):
+        self.pass_on("x0", ("px0",))
+        self.pass_on("y1", ("py1",))
+
+    def third(self):
+        self.pass_on("d0", ("pd0",))
+        self.pass_on("d1", ("pd1",))
+
+    def arrive(self, *names):
+        for name in names:
+            self.copies[name].wait_recv()
+
+    def sent(self):
+        for copy in self.copies.values():
+            copy.wait_send()
+
+    def finish(self):
+        self.arrive("p", "px0", "px1", "py0", "py1", "pd0", "pd1")
+        self.sent()
+        self.local.wait()
+
+
+def wide_square(own_places):
+    _own, pair, ax, ay, _dg = own_places
+    return [{"wide": pair}, {"wide": ax}, {"wide": ay}]
+
+
+def add_rows(dst, first, second, third=None):
+    step = 16
+
+    def body(index, carry):
+        rows = pl.ds(pl.multiple_of(index * step, step), step)
+        total = first[rows].astype(F32) + second[rows].astype(F32)
+        if third is not None:
+            total = total + third[rows].astype(F32)
+        dst[rows] = total.astype(dst.dtype)
+        return carry
+
+    lax.fori_loop(0, BLK // step, body, 0)
+
+
+class SquareScatter:
+    SENDS = 10
+
+    def __init__(self, src, out, summed, from_x, from_y, send, recv):
+        own, pair, ax, ay, dg = square_places()
+        shift = pair - own
+        to_x, to_y, to_p = {"wide": ax}, {"wide": ay}, {"wide": pair}
+        self.src, self.out = src, out
+        self.summed, self.from_x, self.from_y = summed, from_x, from_y
+        self.dests = (dg, ax, ay, own)
+        self.pairs = []
+        for chip in range(4):
+            rows = pl.ds(pl.multiple_of((self.dests[chip] + shift) * BLK, BLK), BLK)
+            self.pairs.append(
+                remote(src.at[:, rows], summed.at[chip], send.at[chip], recv.at[chip], to_p)
+            )
+        self.dx = remote(summed.at[0, 0], from_x.at[0], send.at[4], recv.at[4], to_x)
+        self.dy = remote(summed.at[0, 1], from_y.at[0], send.at[5], recv.at[5], to_y)
+        self.xx = remote(summed.at[1, 0], from_x.at[1], send.at[6], recv.at[6], to_x)
+        self.yy = remote(summed.at[2, 1], from_y.at[1], send.at[7], recv.at[7], to_y)
+        self.ty = remote(summed.at[2, 0], from_y.at[2], send.at[8], recv.at[8], to_y)
+        self.tx = remote(summed.at[1, 1], from_x.at[2], send.at[9], recv.at[9], to_x)
+
+    def block(self, slot, chip):
+        rows = pl.ds(pl.multiple_of(self.dests[chip] * BLK, BLK), BLK)
+        return self.src.at[slot, rows]
+
+    def pair_sum(self, chip, slot, third=None):
+        add_rows(
+            self.summed.at[chip, slot],
+            self.block(slot, chip),
+            self.summed.at[chip, slot],
+            third,
+        )
+
+    def near(self, chip):
+        self.pairs[chip].wait_recv()
+        if chip == 0:
+            self.pair_sum(0, 0)
+            self.dx.start()
+            self.pair_sum(0, 1)
+            self.dy.start()
+        elif chip == 1:
+            self.pair_sum(1, 0)
+            self.xx.start()
+        elif chip == 2:
+            self.pair_sum(2, 1)
+            self.yy.start()
+        else:
+            self.pair_sum(3, 0)
+            self.pair_sum(3, 1)
+
+    def middle(self):
+        self.dx.wait_recv()
+        self.pair_sum(2, 0, self.from_x.at[0])
+        self.ty.start()
+        self.dy.wait_recv()
+        self.pair_sum(1, 1, self.from_y.at[0])
+        self.tx.start()
+
+    def start(self):
+        for chip in range(4):
+            self.pairs[chip].start()
+
+    def first(self):
+        for chip in range(3):
+            self.near(chip)
+
+    def own_sums(self):
+        self.near(3)
+
+    def finish(self):
+        self.xx.wait_recv()
+        self.ty.wait_recv()
+        add_rows(self.out.at[0], self.summed.at[3, 0], self.from_x.at[1], self.from_y.at[2])
+        self.yy.wait_recv()
+        self.tx.wait_recv()
+        add_rows(self.out.at[1], self.summed.at[3, 1], self.from_y.at[1], self.from_x.at[2])
+        for copy in self.pairs:
+            copy.wait_send()
+        for copy in (self.dx, self.dy, self.xx, self.yy, self.ty, self.tx):
+            copy.wait_send()
+
+
+class LineGather:
+    def __init__(self, depth, pieces, send, recv):
+        self.depth, self.pieces, self.send, self.recv = depth, pieces, send, recv
+        self.layer = lax.axis_index("tp")
+
+    def copies(self, step, up):
+        index = self.layer - step + 1 if up else self.layer + step - 1
+        goal = {"tp": self.layer + 1 if up else self.layer - 1}
+        side = 0 if up else 1
+        made = []
+        for number, (own, place) in enumerate(self.pieces):
+            source = own if step == 1 else place(index)
+            made.append(
+                remote(
+                    source,
+                    place(index),
+                    self.send.at[side, number, step - 1],
+                    self.recv.at[side, number, step - 1],
+                    goal,
+                )
+            )
+        return made
+
+    def each(self, step, act):
+        layer = self.layer
+
+        @pl.when((layer < self.depth - 1) & (layer - step + 1 >= 0))
+        def _():
+            for copy in self.copies(step, True):
+                act(copy)
+
+        @pl.when((layer > 0) & (layer + step - 1 < self.depth))
+        def _():
+            for copy in self.copies(step, False):
+                act(copy)
+
+    def start(self, step):
+        self.each(step, lambda copy: copy.start())
+
+    def sent(self, step):
+        self.each(step, lambda copy: copy.wait_send())
+
+    def arrive(self, step):
+        layer = self.layer
+
+        @pl.when(layer - step >= 0)
+        def _():
+            for copy in self.copies(step, True):
+                copy.wait_recv()
+
+        @pl.when(layer + step < self.depth)
+        def _():
+            for copy in self.copies(step, False):
+                copy.wait_recv()
+
+
+def wide_others(own):
+    return [{"wide": (own + step) % 8} for step in range(1, 8)]
+
+
+def head_bias(length, slope, rows):
+    place = lax.broadcasted_iota(jnp.int32, (rows, QB), 0)
+    return jnp.where(place < length, slope * place.astype(F32), NEG)
+
+
+QB = 256
+
+
+def dot_nt(first, second):
+    return lax.dot_general(first, second, (((1,), (1,)), ((), ())), preferred_element_type=F32)
+
+
+def dot_nn(first, second):
+    return lax.dot_general(first, second, (((1,), (0,)), ((), ())), preferred_element_type=F32)
+
+
+def later_key(size):
+    key_place = lax.broadcasted_iota(jnp.int32, (size, size), 0)
+    query_place = lax.broadcasted_iota(jnp.int32, (size, size), 1)
+    return key_place > query_place
+
+
+def slot_scores(key, query, bias, step):
+    extent = (step + 1) * QB
+    scores = dot_nt(key[:extent], query) * (0.125 * LOG2E) + bias[:extent]
+    edge = jnp.where(later_key(QB), NEG, scores[extent - QB :])
+    return edge if step == 0 else jnp.concatenate([scores[: extent - QB], edge], 0)
+
+
+def attend_slot(slot, length, slopes, qkv, out, totals, bias):
+    rows = qkv.shape[1]
+    for head in range(2):
+        lanes = pl.ds(head * HEAD, HEAD)
+        bias[...] = head_bias(length, slopes[head], rows)
+        key = qkv[slot, :, pl.ds(2 * HEAD + head * HEAD, HEAD)]
+        value_t = qkv[slot, :, pl.ds(4 * HEAD + head * HEAD, HEAD)].T
+        for step in range(rows // QB):
+            here = pl.ds(step * QB, QB)
+            scores = slot_scores(key, qkv[slot, here, lanes], bias, step)
+            highest = jnp.max(scores, axis=0, keepdims=True)
+            weights = jnp.exp2(scores - highest)
+            total = jnp.sum(weights, axis=0, keepdims=True)
+            mixed = dot_nn(value_t[:, : (step + 1) * QB], weights.astype(BF)) / total
+            out[slot, here, lanes] = mixed.T.astype(BF)
+            totals[slot, pl.ds(head, 1), here] = highest + jnp.log2(total)
+
+
+def attend_slot_back(
+    slot, length, slopes, qkv, attention, grad, totals, out, bias, key_sum, value_sum
+):
+    rows = qkv.shape[1]
+    for head in range(2):
+        lanes = pl.ds(head * HEAD, HEAD)
+        key_lanes = pl.ds(2 * HEAD + head * HEAD, HEAD)
+        value_lanes = pl.ds(4 * HEAD + head * HEAD, HEAD)
+        bias[...] = head_bias(length, slopes[head], rows)
+        key = qkv[slot, :, key_lanes]
+        value = qkv[slot, :, value_lanes]
+        key_t = key.T
+        key_sum[...] = jnp.zeros_like(key_sum)
+        value_sum[...] = jnp.zeros_like(value_sum)
+        for step in range(rows // QB):
+            here = pl.ds(step * QB, QB)
+            extent = (step + 1) * QB
+            query = qkv[slot, here, lanes]
+            grad_rows = grad[slot, here, lanes]
+            product = grad_rows.astype(F32) * attention[slot, here, lanes].astype(F32)
+            delta = jnp.sum(product.T, axis=0, keepdims=True)
+            scores = slot_scores(key, query, bias, step)
+            probs = jnp.exp2(scores - totals[slot, pl.ds(head, 1), here])
+            grad_probs = dot_nt(value[:extent], grad_rows)
+            grad_scores = (probs * (grad_probs - delta)).astype(BF)
+            span = pl.ds(0, extent)
+            value_sum[span] += dot_nn(probs.astype(BF), grad_rows)
+            key_sum[span] += dot_nn(grad_scores, query)
+            grad_query = dot_nn(key_t[:, :extent], grad_scores)
+            out[slot, here, lanes] = (grad_query.T * 0.125).astype(BF)
+        out[slot, :, key_lanes] = (key_sum[...] * 0.125).astype(BF)
+        out[slot, :, value_lanes] = value_sum[...].astype(BF)
+
+
+def line_others(depth):
+    layer = lax.axis_index("tp")
+    return [{"tp": (layer + step) % depth} for step in range(1, depth)]
+
+
+VMEM_MAX = 67043328
+
+
+def norm_stats(values):
+    middle = jnp.mean(values, axis=-1, keepdims=True)
+    centred = values - middle
+    spread = jnp.mean(centred * centred, axis=-1, keepdims=True)
+    inverse = lax.rsqrt(spread + 1e-05)
+    return centred * inverse, inverse
+
+
+def norm_back_rows(grad, hat, inverse, gain):
+    scaled = grad * gain
+    first = jnp.mean(scaled, axis=-1, keepdims=True)
+    second = jnp.mean(scaled * hat, axis=-1, keepdims=True)
+    return (scaled - first - hat * second) * inverse
+
+
+def gelu_parts(values):
+    root = math.sqrt(2 / math.pi)
+    squared = values * values
+    inner = jnp.tanh(root * values * (1.0 + 0.044715 * squared))
+    half = 0.5 * (1.0 + inner)
+    slope = half + 0.5 * values * (1.0 - inner * inner) * root * (1.0 + 3 * 0.044715 * squared)
+    return values * half, slope
+
+
+def relation(index):
+    own = lax.axis_index("wide")
+    core = (own + index) % 2
+    col = (own // 2 + index // 2) % 2
+    row = (own // 4 + index // 4) % 2
+    return row * 4 + col * 2 + core
+
+
+class WideExchange:
+    def __init__(self, source, target, send, recv):
+        own = lax.axis_index("wide")
+        self.copies = [
+            remote(
+                source((own + step) % 8),
+                target(own),
+                send.at[step - 1],
+                recv.at[step - 1],
+                {"wide": (own + step) % 8},
+            )
+            for step in range(1, 8)
+        ]
+
+    def start(self):
+        for copy in self.copies:
+            copy.start()
+
+    def arrive(self):
+        for copy in self.copies:
+            copy.wait_recv()
+
+    def sent(self):
+        for copy in self.copies:
+            copy.wait_send()
+
+
+def layer_body(
+    depth,
+    lengths,
+    hidden,
+    cotangent,
+    w_query,
+    w_key,
+    w_value,
+    w_dense,
+    w_up,
+    w_down,
+    pre_gain,
+    pre_shift,
+    mid_gain,
+    mid_shift,
+    b_dense,
+    b_down,
+    b_up,
+    b_query,
+    b_value,
+    output,
+    grad_in,
+    attn_sum,
+    ffn_x,
+    vec_sums,
+    unit_sums,
+    hidden_all,
+    normed,
+    down_all,
+    branch_all,
+    second_share,
+    down_share,
+    qkv,
+    attention,
+    grad_att,
+    act_t,
+    pre_t,
+    totals,
+    bias,
+    key_sum,
+    value_sum,
+    qkv_w,
+    dense_w,
+    up_t,
+    down_t,
+    up_w,
+    down_w,
+    z_qkv,
+    z_dense,
+    z_vec,
+    vec_wide,
+    vec_line,
+    vec_wide_all,
+    vec_line_all,
+    vectors,
+    up_bias,
+    qkv_bias,
+    own_rows,
+    down_own,
+    residual,
+    grad_second,
+    grad_resid,
+    down_out,
+    sums,
+    up_sum,
+    ffn_g,
+    ffn_in,
+    ffn_sum,
+    attn_g,
+    attn_in,
+    attn_z,
+    parts,
+    gathered,
+    a_summed,
+    a_x,
+    a_y,
+    b_summed,
+    b_x,
+    b_y,
+    gather_send,
+    gather_recv,
+    gather_local,
+    scatter_send,
+    scatter_recv,
+    line_send,
+    line_recv,
+    ffn_line_send,
+    ffn_line_recv,
+    wide_send,
+    wide_recv,
+    grad_line_send,
+    grad_line_recv,
+    onward_send,
+    onward_recv,
+    sum_send,
+    sum_recv,
+    own_sems,
+):
+    own = lax.axis_index("wide")
+    layer = lax.axis_index("tp")
+    per_layer = 8 // depth
+    width = hidden.shape[-1]
+    step = 32
+    steps = BLK // step
+    others = [
+        ((own + side) % 8, (layer + up) % depth)
+        for up in range(depth)
+        for side in range(8)
+        if up or side
+    ]
+    own_lanes = pl.ds(pl.multiple_of(own * BLK, BLK), BLK)
+
+    for place, ref in enumerate((pre_gain, pre_shift, mid_gain, mid_shift, b_dense, b_down)):
+        vec_wide[pl.ds(place, 1)] = ref[...].astype(F32)
+    vec_line[...] = jnp.zeros_like(vec_line)
+    vec_line[0 : b_up.shape[0], 0 : b_up.shape[1]] = b_up[...].astype(F32)
+    vec_line[b_up.shape[0] :, 0:8] = b_query[...].astype(F32)
+    vec_line[b_up.shape[0] :, 8:16] = b_value[...].astype(F32)
+    first_row = own * BLK
+
+    def token_mask(slot, rows, count):
+        place = first_row + rows * count + lax.broadcasted_iota(jnp.int32, (count, BLK), 0)
+        inside = place < lengths[layer * 2 + slot]
+        return jnp.where(inside, 1.0, 0.0).astype(F32)[:, :1]
+
+    def down_part(index, carry):
+        rows = pl.ds(pl.multiple_of(index * step, step), step)
+        for slot in range(2):
+            values = token_mask(slot, index, step) * cotangent[slot, rows].astype(F32)
+            down_own[slot, rows] = values.astype(BF)
+        return carry
+
+    lax.fori_loop(0, steps, down_part, 0)
+    greet([{"wide": wide, "tp": tp} for wide, tp in others])
+
+    def gather_of(number, src, dst):
+        return SquareGather(
+            src, dst, gather_send.at[number], gather_recv.at[number], gather_local.at[number]
+        )
+
+    def wide_of(number, source, target):
+        return WideExchange(source, target, wide_send.at[number], wide_recv.at[number])
+
+    gains = wide_of(0, lambda dev: vec_wide, lambda dev: vec_wide_all.at[dev])
+    gains.start()
+    hid = gather_of(0, hidden, hidden_all)
+    hid.start()
+    line = LineGather(
+        depth,
+        [
+            (w_query, lambda at: z_qkv.at[at, 0]),
+            (w_key, lambda at: z_qkv.at[at, 1]),
+            (w_value, lambda at: z_qkv.at[at, 2]),
+            (w_dense, lambda at: z_dense.at[at]),
+            (vec_line, lambda at: z_vec.at[at]),
+        ],
+        line_send,
+        line_recv,
+    )
+    line.start(1)
+    own_copies = [
+        pltpu.make_async_copy(ref, place(layer), own_sems.at[number])
+        for number, (ref, place) in enumerate(line.pieces)
+    ]
+    for copy in own_copies:
+        copy.start()
+    vec_wide_all[own] = vec_wide[...]
+    gains.arrive()
+    for dev in range(8):
+        vectors[:, dev * BLK : (dev + 1) * BLK] = vec_wide_all[dev]
+
+    def norm_block(index, carry):
+        base = relation(index) * BLK
+
+        def norm_part(part, carry):
+            rows = pl.ds(pl.multiple_of(base + part * step, step), step)
+            for slot in range(2):
+                hat, _inverse = norm_stats(hidden_all[slot, rows].astype(F32))
+                normed[slot, rows] = (hat * vectors[0:1] + vectors[1:2]).astype(BF)
+            return carry
+
+        return lax.fori_loop(0, steps, norm_part, carry)
+
+    hid.arrive("p")
+    hid.local.wait()
+    lax.fori_loop(0, 2, norm_block, 0)
+    hid.first()
+    line.arrive(1)
+    line.start(2)
+    hid.second()
+    line.arrive(2)
+    line.start(3)
+    hid.arrive("px0", "px1", "py0", "py1")
+    lax.fori_loop(2, 6, norm_block, 0)
+    hid.third()
+    line.arrive(3)
+    for copy in own_copies:
+        copy.wait()
+
+    def goal_lanes(dev):
+        return pl.ds(pl.multiple_of((dev % per_layer) * BLK, BLK), BLK)
+
+    heads = wide_of(
+        1,
+        lambda dev: z_qkv.at[dev // per_layer, :, :, goal_lanes(dev)],
+        lambda dev: attn_in.at[dev, pl.ds(0, 3)],
+    )
+    dense = wide_of(
+        2,
+        lambda dev: z_dense.at[dev // per_layer, goal_lanes(dev)],
+        lambda dev: dense_w.at[:, own_lanes],
+    )
+    biases = wide_of(3, lambda dev: z_vec, lambda dev: vec_line_all.at[dev])
+    ups = wide_of(
+        4,
+        lambda dev: w_up.at[:, pl.ds(pl.multiple_of(dev * BLK, BLK), BLK)],
+        lambda dev: up_t.at[own_lanes],
+    )
+    downs = wide_of(
+        5,
+        lambda dev: w_down.at[pl.ds(pl.multiple_of(dev * BLK, BLK), BLK)],
+        lambda dev: down_t.at[:, own_lanes],
+    )
+    arrivals = (biases, heads, dense, ups, downs)
+    for exchange in arrivals:
+        exchange.start()
+    gd = gather_of(1, down_own, down_all)
+    gd.start()
+    own_copies = [
+        pltpu.make_async_copy(z_qkv.at[own // per_layer, :, :, goal_lanes(own)], attn_in.at[own, pl.ds(0, 3)], own_sems.at[5]),
+        pltpu.make_async_copy(z_dense.at[own // per_layer, goal_lanes(own)], dense_w.at[:, own_lanes], own_sems.at[6]),
+        pltpu.make_async_copy(w_up.at[:, own_lanes], up_t.at[own_lanes], own_sems.at[7]),
+        pltpu.make_async_copy(w_down.at[own_lanes], down_t.at[:, own_lanes], own_sems.at[8]),
+    ]
+    for copy in own_copies:
+        copy.start()
+    vec_line_all[own] = z_vec[...]
+    hid.arrive("pd0", "pd1")
+    lax.fori_loop(6, 8, norm_block, 0)
+    biases.arrive()
+    head_layer = own // per_layer
+    piece = own % per_layer
+    unit_row = own // 2
+    for dev in range(8):
+        for head in range(2):
+            lanes = slice(head * HEAD + dev * 8, head * HEAD + dev * 8 + 8)
+            row = pl.ds(b_up.shape[0] + 2 * piece + head, 1)
+            values = vec_line_all[dev, head_layer, row]
+            qkv_bias[:, lanes] = values[:, 0:8]
+            lanes = slice(4 * HEAD + lanes.start, 4 * HEAD + lanes.stop)
+            qkv_bias[:, lanes] = values[:, 8:16]
+    qkv_bias[:, 2 * HEAD : 4 * HEAD] = jnp.zeros((1, 2 * HEAD), F32)
+    for up in range(depth):
+        for part in range(4):
+            values = vec_line_all[4 * (own % 2) + part, up, pl.ds(unit_row, 1)]
+            up_bias[:, up * BLK + part * 32 : up * BLK + part * 32 + 32] = values[:, 0:32]
+    heads.arrive()
+    for copy in own_copies:
+        copy.wait()
+    for dev in range(8):
+        for kind in range(3):
+            qkv_w[dev * BLK : (dev + 1) * BLK, kind * BLK : (kind + 1) * BLK] = attn_in[dev, kind]
+
+    ffn_line = LineGather(
+        depth,
+        [
+            (up_t, lambda at: up_w.at[:, pl.ds(pl.multiple_of(at * BLK, BLK), BLK)]),
+            (down_t, lambda at: down_w.at[pl.ds(pl.multiple_of(at * BLK, BLK), BLK)]),
+        ],
+        ffn_line_send,
+        ffn_line_recv,
+    )
+    slopes = [
+        jnp.exp2(-0.5 * (jnp.full((1, 1), 2 * own + head, jnp.int32).astype(F32) + 1.0)) * LOG2E
+        for head in range(2)
+    ]
+
+    def one_slot(slot, carry):
+        def block(index, carry):
+            rows = pl.ds(pl.multiple_of(index * QB, QB), QB)
+            qkv[slot, rows] = (dot_nn(normed[slot, rows], qkv_w[...]) + qkv_bias[...]).astype(BF)
+            return carry
+
+        lax.fori_loop(0, 8 * BLK // QB, block, 0)
+        attend_slot(slot, lengths[layer * 2 + slot], slopes, qkv, attention, totals, bias)
+
+        @pl.when(slot == 0)
+        def _():
+            ups.arrive()
+            downs.arrive()
+            ffn_line.start(1)
+
+        return carry
+
+    lax.fori_loop(0, 2, one_slot, 0)
+    own_copies = [
+        pltpu.make_async_copy(ref, place(layer), own_sems.at[9 + number])
+        for number, (ref, place) in enumerate(ffn_line.pieces)
+    ]
+    for copy in own_copies:
+        copy.start()
+    hid.sent()
+    dense.arrive()
+    share = branch_all
+
+    def dense_block(index, carry):
+        rows = pl.ds(pl.multiple_of(relation(index) * BLK, BLK), BLK)
+        values = attention[:, rows].reshape(2 * BLK, 2 * HEAD)
+        share[:, rows] = dot_nn(values, dense_w[...]).astype(BF).reshape(2, BLK, width)
+        return carry
+
+    def scatter_of(number, src, out, buffers):
+        return SquareScatter(src, out, *buffers, scatter_send.at[number], scatter_recv.at[number])
+
+    scatter = scatter_of(0, share, residual, (a_summed, a_x, a_y))
+    for chip in range(4):
+        start = (6, 2, 4, 0)[chip]
+        lax.fori_loop(start, start + 2, dense_block, 0)
+        scatter.pairs[chip].start()
+        if chip:
+            scatter.near(chip - 1)
+    gd.first()
+    ffn_line.arrive(1)
+    ffn_line.start(2)
+    scatter.near(3)
+    gd.second()
+    scatter.middle()
+    gd.third()
+    ffn_line.arrive(2)
+    ffn_line.start(3)
+    scatter.finish()
+
+    def second_part(index, carry):
+        rows = pl.ds(pl.multiple_of(index * step, step), step)
+        for slot in range(2):
+            values = hidden[slot, rows].astype(F32) + residual[slot, rows] + vectors[4:5]
+            residual[slot, rows] = values
+            hat, _inverse = norm_stats(values)
+            own_rows[slot, rows] = (hat * vectors[2:3] + vectors[3:4]).astype(BF)
+        return carry
+
+    lax.fori_loop(0, steps, second_part, 0)
+    second_all = hidden_all
+    gather = gather_of(2, own_rows, second_all)
+    gather.start()
+    scatter = scatter_of(1, second_share, grad_second, (a_summed, a_x, a_y))
+    gd.arrive("p", "px0", "px1", "py0", "py1", "pd0", "pd1")
+    gd.local.wait()
+    for copy in own_copies:
+        copy.wait()
+    ffn_line.arrive(3)
+
+    def compute(index, carry):
+        source = relation(index)
+        rows = pl.ds(pl.multiple_of(source * BLK, BLK), BLK)
+        values = second_all[:, rows].reshape(2 * BLK, width)
+        act_value, act_slope = gelu_parts(dot_nn(values, up_w[...]) + up_bias[...])
+        activated = act_value.astype(BF)
+        grad_rows = down_all[:, rows].reshape(2 * BLK, width)
+        grad_pre = (dot_nt(grad_rows, down_w[...]) * act_slope).astype(BF)
+        second_share[:, rows] = dot_nt(grad_pre, up_w[...]).astype(BF).reshape(2, BLK, width)
+        down_share[:, rows] = dot_nn(activated, down_w[...]).astype(BF).reshape(2, BLK, width)
+        up_sum[...] += jnp.sum(grad_pre.astype(F32), axis=0, keepdims=True)
+        for slot in range(2):
+            lanes = pl.ds(pl.multiple_of(slot * 8 * BLK + source * BLK, BLK), BLK)
+            part = slice(slot * BLK, (slot + 1) * BLK)
+            act_t[:, lanes] = activated[part].T
+            pre_t[:, lanes] = grad_pre[part].T
+        return carry
+
+    up_sum[...] = jnp.zeros_like(up_sum)
+    gather.arrive("p")
+    gather.local.wait()
+    lax.fori_loop(0, 2, compute, 0)
+    scatter.pairs[3].start()
+    gather.first()
+    gather.second()
+    gather.arrive("px0", "px1", "py0", "py1")
+    lax.fori_loop(2, 4, compute, 0)
+    scatter.pairs[1].start()
+    scatter.near(3)
+    lax.fori_loop(4, 6, compute, 0)
+    scatter.pairs[2].start()
+    gather.third()
+    scatter.near(1)
+    gather.arrive("pd0", "pd1")
+    lax.fori_loop(6, 8, compute, 0)
+    scatter.pairs[0].start()
+    scatter.near(2)
+    scatter.near(0)
+
+    def weight_grads(left, right, kind):
+        def one(up, carry):
+            rows = pl.ds(pl.multiple_of(up * BLK, BLK), BLK)
+            total = dot_nn(left[rows, pl.ds(0, 8 * BLK)], right[0])
+            total = total + dot_nn(left[rows, pl.ds(8 * BLK, 8 * BLK)], right[1])
+            total = total.astype(BF)
+            for blk in range(8):
+                ffn_g[kind, up, blk] = total[:, blk * BLK : (blk + 1) * BLK]
+            return carry
+
+        lax.fori_loop(0, depth, one, 0)
+
+    def line_copies(kind):
+        return [
+            remote(
+                ffn_g.at[kind, (layer + up) % depth],
+                ffn_in.at[kind, up - 1],
+                grad_line_send.at[kind, up - 1],
+                grad_line_recv.at[kind, up - 1],
+                {"tp": (layer + up) % depth},
+            )
+            for up in range(1, depth)
+        ]
+
+    def line_sums(kind):
+        for copy in line_copies(kind):
+            copy.wait_recv()
+
+        def add_block(blk, carry):
+            total = ffn_g[kind, layer, blk].astype(F32)
+            for up in range(depth - 1):
+                total = total + ffn_in[kind, up, blk].astype(F32)
+            ffn_sum[blk, kind] = total.astype(BF)
+            return carry
+
+        lax.fori_loop(0, 8, add_block, 0)
+
+    weight_grads(pre_t, second_all, 0)
+    for copy in line_copies(0):
+        copy.start()
+    scatter.middle()
+    weight_grads(act_t, down_all, 1)
+    for copy in line_copies(1):
+        copy.start()
+    scatter.finish()
+    gather.sent()
+    sums[...] = jnp.zeros_like(sums)
+
+    def back_part(index, carry):
+        rows = pl.ds(pl.multiple_of(index * step, step), step)
+        for slot in range(2):
+            hat, inverse = norm_stats(residual[slot, rows])
+            grad = grad_second[slot, rows]
+            grad_out = token_mask(slot, index, step) * cotangent[slot, rows].astype(F32)
+            total = grad_out + norm_back_rows(grad, hat, inverse, vectors[2:3])
+            grad_resid[slot, rows] = total
+            own_rows[slot, rows] = total.astype(BF)
+            for place, value in enumerate((total, grad * hat, grad, grad_out)):
+                sums[pl.ds(place, 1)] += jnp.sum(value, axis=0, keepdims=True)
+        return carry
+
+    lax.fori_loop(0, steps, back_part, 0)
+    again = gather_of(3, own_rows, branch_all)
+    again.start()
+    down = scatter_of(2, down_share, down_out, (b_summed, b_x, b_y))
+    down.start()
+
+    def att_block(index, carry):
+        rows = pl.ds(pl.multiple_of(relation(index) * BLK, BLK), BLK)
+        values = branch_all[:, rows].reshape(2 * BLK, width)
+        grad_att[:, rows] = dot_nt(values, dense_w[...]).astype(BF).reshape(2, BLK, 2 * HEAD)
+        return carry
+
+    again.arrive("p")
+    again.local.wait()
+    lax.fori_loop(0, 2, att_block, 0)
+    again.first()
+    down.near(0)
+    again.second()
+    again.arrive("px0", "px1", "py0", "py1")
+    down.near(1)
+    down.near(2)
+    lax.fori_loop(2, 6, att_block, 0)
+    again.third()
+    again.arrive("pd0", "pd1")
+    lax.fori_loop(6, 8, att_block, 0)
+
+    dense_part = dot_nn(attention[0].T, branch_all[0]) + dot_nn(attention[1].T, branch_all[1])
+    dense_part = dense_part.astype(BF)
+    for blk in range(8):
+        attn_g[blk, 3] = dense_part[:, blk * BLK : (blk + 1) * BLK]
+    kinds = (pl.ds(3, 1), pl.ds(0, 3))
+    exchanges = [
+        wide_of(
+            6 + group,
+            lambda dev, kind=kind: attn_g.at[dev, kind],
+            lambda dev, kind=kind: attn_in.at[dev, kind],
+        )
+        for group, kind in enumerate(kinds)
+    ]
+
+    def onward(group, index, source):
+        return remote(
+            source.at[index, kinds[group]],
+            attn_z.at[layer, index % per_layer, kinds[group]],
+            onward_send.at[group, index],
+            onward_recv.at[group, layer, index % per_layer],
+            {"tp": index // per_layer},
+        )
+
+    def forward(group, index, source):
+        @pl.when(index // per_layer != layer)
+        def _():
+            onward(group, index, source).start()
+
+    def forward_all(group):
+        for number in range(1, 8):
+            exchanges[group].copies[number - 1].wait_recv()
+            forward(group, (own + 8 - number) % 8, attn_in)
+
+    exchanges[0].start()
+    forward(0, own, attn_g)
+    ffn = wide_of(8, lambda dev: ffn_sum.at[dev], lambda dev: ffn_x.at[dev])
+
+    def slot_back(slot, carry):
+        attend_slot_back(
+            slot,
+            lengths[layer * 2 + slot],
+            slopes,
+            qkv,
+            attention,
+            grad_att,
+            totals,
+            qkv,
+            bias,
+            key_sum,
+            value_sum,
+        )
+
+        @pl.when(slot == 0)
+        def _():
+            forward_all(0)
+            down.middle()
+            line_sums(0)
+
+        return carry
+
+    lax.fori_loop(0, 2, slot_back, 0)
+    grad_qkv = qkv
+    weight_part = dot_nn(grad_qkv[0].T, normed[0]) + dot_nn(grad_qkv[1].T, normed[1])
+    weight_part = weight_part.astype(BF)
+    for kind in range(3):
+        for blk in range(8):
+            attn_g[blk, kind] = weight_part[
+                kind * BLK : (kind + 1) * BLK, blk * BLK : (blk + 1) * BLK
+            ]
+    exchanges[1].start()
+    forward(1, own, attn_g)
+    share = second_share
+    grad_normed = grad_second
+    scatter = scatter_of(3, share, grad_normed, (a_summed, a_x, a_y))
+
+    def normed_block(index, carry):
+        rows = pl.ds(pl.multiple_of(relation(index) * BLK, BLK), BLK)
+        values = grad_qkv[:, rows].reshape(2 * BLK, 6 * HEAD)
+        share[:, rows] = dot_nt(values, qkv_w[...]).astype(BF).reshape(2, BLK, width)
+        return carry
+
+    for chip in range(4):
+        start = (6, 2, 4, 0)[chip]
+        lax.fori_loop(start, start + 2, normed_block, 0)
+        scatter.pairs[chip].start()
+        if chip:
+            scatter.near(chip - 1)
+    line_sums(1)
+    ffn.start()
+    head_sum = jnp.sum(grad_qkv[0].astype(F32), axis=0, keepdims=True)
+    head_sum = head_sum + jnp.sum(grad_qkv[1].astype(F32), axis=0, keepdims=True)
+    down.near(3)
+    down.finish()
+
+    def out_part(index, carry):
+        rows = pl.ds(pl.multiple_of(index * step, step), step)
+        for slot in range(2):
+            total = residual[slot, rows] + down_out[slot, rows] + vectors[5:6]
+            output[slot, rows] = (token_mask(slot, index, step) * total).astype(BF)
+        return carry
+
+    lax.fori_loop(0, steps, out_part, 0)
+    forward_all(1)
+    scatter.near(3)
+    scatter.middle()
+    for blk in range(8):
+        lanes = slice(blk * BLK, (blk + 1) * BLK)
+        for place in range(4):
+            parts[blk, pl.ds(2 + place, 1)] = sums[place : place + 1, lanes]
+        for place in range(depth):
+            parts[blk, pl.ds(6 + place, 1)] = up_sum[:, place * BLK : (place + 1) * BLK]
+        parts[blk, pl.ds(6 + depth, 1)] = head_sum[:, : 2 * HEAD]
+        parts[blk, pl.ds(7 + depth, 1)] = head_sum[:, 4 * HEAD :]
+    scatter.finish()
+
+    def last_part(index, carry):
+        gain_sum, shift_sum = carry
+        rows = pl.ds(pl.multiple_of(index * step, step), step)
+        for slot in range(2):
+            hat, inverse = norm_stats(hidden[slot, rows].astype(F32))
+            grad = grad_normed[slot, rows]
+            total = grad_resid[slot, rows] + norm_back_rows(grad, hat, inverse, vectors[0:1])
+            grad_in[slot, rows] = total.astype(BF)
+            gain_sum = gain_sum + jnp.sum(grad * hat, axis=0, keepdims=True)
+            shift_sum = shift_sum + jnp.sum(grad, axis=0, keepdims=True)
+        return gain_sum, shift_sum
+
+    zero = jnp.zeros((1, width), F32)
+    gain_sum, shift_sum = lax.fori_loop(0, steps, last_part, (zero, zero))
+    for blk in range(8):
+        lanes = slice(blk * BLK, (blk + 1) * BLK)
+        parts[blk, pl.ds(0, 1)] = gain_sum[:, lanes]
+        parts[blk, pl.ds(1, 1)] = shift_sum[:, lanes]
+    sum_copies = [
+        remote(
+            parts.at[wide],
+            gathered.at[own, layer],
+            sum_send.at[index],
+            sum_recv.at[index],
+            {"wide": wide, "tp": tp},
+        )
+        for index, (wide, tp) in enumerate(others)
+    ]
+    for copy in sum_copies:
+        copy.start()
+    gathered[own, layer] = parts[own]
+    for group in range(2):
+        for up in range(1, depth):
+            source = (layer + up) % depth
+            for number in range(per_layer):
+                remote(
+                    attn_in.at[number, kinds[group]],
+                    attn_z.at[source, number, kinds[group]],
+                    onward_send.at[group, number],
+                    onward_recv.at[group, source, number],
+                    {"tp": source},
+                ).wait_recv()
+    attn_in[own] = attn_g[own]
+    for number in range(per_layer):
+        for kind in range(4):
+            total = attn_in[layer * per_layer + number, kind].astype(F32)
+            for up in range(1, depth):
+                total = total + attn_z[(layer + up) % depth, number, kind].astype(F32)
+            attn_sum[number, kind] = total
+    ffn_x[own] = ffn_sum[own]
+    ffn.arrive()
+    for copy in sum_copies:
+        copy.wait_recv()
+
+    def unit_part(dev, carry):
+        total = gathered[dev, 0]
+        for up in range(1, depth):
+            total = total + gathered[dev, up]
+        unit_sums[dev] = total
+        return carry + total
+
+    vec_sums[...] = lax.fori_loop(0, 8, unit_part, jnp.zeros((16, BLK), F32))
+
+    for copy in sum_copies:
+        copy.wait_send()
+    for exchange in (gains, ffn) + arrivals + tuple(exchanges):
+        exchange.sent()
+    for number in range(1, depth):
+        line.sent(number)
+        ffn_line.sent(number)
+    for kind in range(2):
+        for copy in line_copies(kind):
+            copy.wait_send()
+    gd.sent()
+    again.sent()
+    for group in range(2):
+        for index in range(8):
+
+            @pl.when(index // per_layer != layer)
+            def _(index=index, group=group):
+                onward(group, index, attn_in).wait_send()
+
+
+def layer_pass(depth, lengths, hidden, cotangent, *weights):
+    width = hidden.shape[-1]
+    units = depth * BLK
+    per_layer = 8 // depth
+    dma = pltpu.SemaphoreType.DMA
+    rows = jax.ShapeDtypeStruct((2, BLK, width), BF)
+    tokens = pltpu.VMEM((2, 8 * BLK, width), BF)
+    own_f32 = pltpu.VMEM((2, BLK, width), F32)
+    own_bf = pltpu.VMEM((2, BLK, width), BF)
+    line_vec = (8, BLK)
+    peers = 8 * depth - 1
+    vectors = [part.reshape(1, BLK) for part in weights[6:12]]
+    operands = (hidden, cotangent) + weights[:6] + tuple(vectors) + weights[12:]
+    return pl.pallas_call(
+        functools.partial(layer_body, depth),
+        out_shape=[
+            rows,
+            rows,
+            jax.ShapeDtypeStruct((per_layer, 4, BLK, BLK), F32),
+            jax.ShapeDtypeStruct((8, 2, BLK, BLK), BF),
+            jax.ShapeDtypeStruct((16, BLK), F32),
+            jax.ShapeDtypeStruct((8, 16, BLK), F32),
+        ],
+        in_specs=[pl.BlockSpec(memory_space=pltpu.SMEM)] + [vmem()] * len(operands),
+        out_specs=[vmem()] * 6,
+        scratch_shapes=[tokens] * 6
+        + [
+            pltpu.VMEM((2, 8 * BLK, 6 * HEAD), BF),
+            pltpu.VMEM((2, 8 * BLK, 2 * HEAD), BF),
+            pltpu.VMEM((2, 8 * BLK, 2 * HEAD), BF),
+            pltpu.VMEM((units, 16 * BLK), BF),
+            pltpu.VMEM((units, 16 * BLK), BF),
+            pltpu.VMEM((2, 2, 8 * BLK), F32),
+            pltpu.VMEM((8 * BLK, QB), F32),
+            pltpu.VMEM((8 * BLK, HEAD), F32),
+            pltpu.VMEM((8 * BLK, HEAD), F32),
+            pltpu.VMEM((width, 6 * HEAD), BF),
+            pltpu.VMEM((2 * HEAD, width), BF),
+            pltpu.VMEM((width, BLK), BF),
+            pltpu.VMEM((BLK, width), BF),
+            pltpu.VMEM((width, units), BF),
+            pltpu.VMEM((units, width), BF),
+            pltpu.VMEM((depth, 3, BLK, per_layer * BLK), BF),
+            pltpu.VMEM((depth, per_layer * BLK, BLK), BF),
+            pltpu.VMEM((depth,) + line_vec, F32),
+            pltpu.VMEM((8, BLK), F32),
+            pltpu.VMEM(line_vec, F32),
+            pltpu.VMEM((8, 8, BLK), F32),
+            pltpu.VMEM((8, depth) + line_vec, F32),
+            pltpu.VMEM((8, width), F32),
+            pltpu.VMEM((1, units), F32),
+            pltpu.VMEM((1, 6 * HEAD), F32),
+            own_bf,
+            own_bf,
+            own_f32,
+            own_f32,
+            own_f32,
+            own_f32,
+            pltpu.VMEM((8, width), F32),
+            pltpu.VMEM((1, units), F32),
+            pltpu.VMEM((2, depth, 8, BLK, BLK), BF),
+            pltpu.VMEM((2, depth - 1, 8, BLK, BLK), BF),
+            pltpu.VMEM((8, 2, BLK, BLK), BF),
+            pltpu.VMEM((8, 4, BLK, BLK), BF),
+            pltpu.VMEM((8, 4, BLK, BLK), BF),
+            pltpu.VMEM((depth, per_layer, 4, BLK, BLK), BF),
+            pltpu.VMEM((8, 16, BLK), F32),
+            pltpu.VMEM((8, depth, 16, BLK), F32),
+        ]
+        + [
+            pltpu.VMEM((4, 2, BLK, width), BF),
+            pltpu.VMEM((3, BLK, width), BF),
+            pltpu.VMEM((3, BLK, width), BF),
+        ]
+        * 2
+        + [
+            dma((4, SquareGather.SENDS)),
+            dma((4, SquareGather.SENDS)),
+            dma((4,)),
+            dma((4, SquareScatter.SENDS)),
+            dma((4, SquareScatter.SENDS)),
+            dma((2, 5, depth - 1)),
+            dma((2, 5, depth - 1)),
+            dma((2, 2, depth - 1)),
+            dma((2, 2, depth - 1)),
+            dma((9, 7)),
+            dma((9, 7)),
+            dma((2, depth - 1)),
+            dma((2, depth - 1)),
+            dma((2, 8)),
+            dma((2, depth, per_layer)),
+            dma((peers,)),
+            dma((peers,)),
+            dma((11,)),
+        ],
+        compiler_params=pltpu.CompilerParams(
+            collective_id=1, has_side_effects=True, vmem_limit_bytes=VMEM_MAX
+        ),
+        name="layer",
+    )(lengths, *operands)
+
+
+def write_body(
+    depth,
+    output_in,
+    grad_in_in,
+    attn_sum,
+    ffn_x,
+    vec_in,
+    unit_sums,
+    output,
+    grad_in,
+    grad_q,
+    grad_k,
+    grad_v,
+    grad_d,
+    grad_up,
+    grad_down,
+    up_b,
+    query_b,
+    value_b,
+    vec_sums,
+):
+    own = lax.axis_index("wide")
+    layer = lax.axis_index("tp")
+    per_layer = 8 // depth
+    output[...] = output_in[...]
+    grad_in[...] = grad_in_in[...]
+    for number in range(per_layer):
+        lanes = slice(number * BLK, (number + 1) * BLK)
+        for kind, target in enumerate((grad_q, grad_k, grad_v)):
+            target[:, lanes] = attn_sum[number, kind].T
+        grad_d[lanes] = attn_sum[number, 3]
+    for blk in range(8):
+        lanes = slice(blk * BLK, (blk + 1) * BLK)
+        grad_up[:, lanes] = ffn_x[blk, 0].astype(F32).T
+        grad_down[lanes] = ffn_x[blk, 1].astype(F32)
+    for row in range(up_b.shape[0]):
+        unit = unit_sums[2 * row + own // 4, pl.ds(6 + layer, 1)]
+        moved = pltpu.roll(unit, (BLK - 32 * (own % 4)) % BLK, 1)
+        up_b[row : row + 1] = moved[:, :32]
+        shift = (BLK - ((row % 2) * HEAD + 8 * own)) % BLK
+        for place, target in enumerate((query_b, value_b)):
+            unit = unit_sums[per_layer * layer + row // 2, pl.ds(6 + depth + place, 1)]
+            target[row : row + 1] = pltpu.roll(unit, shift, 1)[:, :8]
+    vec_sums[...] = vec_in[...]
+
+
+def write_out(depth, *pieces):
+    per_layer = 8 // depth
+    width = pieces[0].shape[-1]
+    rows = jax.ShapeDtypeStruct(pieces[0].shape, BF)
+    square = jax.ShapeDtypeStruct((BLK, per_layer * BLK), F32)
+    head = jax.ShapeDtypeStruct((4, 8), F32)
+    return pl.pallas_call(
+        functools.partial(write_body, depth),
+        out_shape=[
+            rows,
+            rows,
+            square,
+            square,
+            square,
+            jax.ShapeDtypeStruct((per_layer * BLK, BLK), F32),
+            jax.ShapeDtypeStruct((BLK, width), F32),
+            jax.ShapeDtypeStruct((width, BLK), F32),
+            jax.ShapeDtypeStruct((4, 32), F32),
+            head,
+            head,
+            jax.ShapeDtypeStruct((16, BLK), F32),
+        ],
+        in_specs=[vmem()] * 6,
+        out_specs=[vmem()] * 12,
+        name="write_out",
+    )(*pieces)
+
+
+def square_device(
+    hidden_in,
+    lengths,
+    pre_gain,
+    pre_shift,
+    w_query,
+    w_key,
+    w_value,
+    b_query,
+    b_value,
+    w_dense,
+    b_dense,
+    mid_gain,
+    mid_shift,
+    w_up,
+    b_up,
+    w_down,
+    b_down,
+    cotangent,
+):
+    depth = lax.axis_size("tp")
+    pieces = layer_pass(
+        depth,
+        lengths,
+        hidden_in,
+        cotangent,
+        w_query,
+        w_key,
+        w_value,
+        w_dense,
+        w_up,
+        w_down,
+        pre_gain,
+        pre_shift,
+        mid_gain,
+        mid_shift,
+        b_dense,
+        b_down,
+        b_up,
+        b_query,
+        b_value,
+    )
+    (
+        output,
+        grad_in,
+        grad_q,
+        grad_k,
+        grad_v,
+        grad_d,
+        grad_up,
+        grad_down,
+        up_b,
+        query_b,
+        value_b,
+        vec_sums,
+    ) = write_out(depth, *pieces)
+    return (
+        output,
+        grad_in,
+        vec_sums[0],
+        vec_sums[1],
+        grad_q,
+        grad_k,
+        grad_v,
+        query_b,
+        value_b,
+        grad_d,
+        vec_sums[2],
+        vec_sums[3],
+        vec_sums[4],
+        grad_up,
+        up_b,
+        grad_down,
+        vec_sums[5],
+    )
+
+
 def solution(mesh):
+    square = mesh.shape["wide"] == 8 and mesh.shape["tp"] == 4
     return jax.shard_map(
-        per_device,
+        square_device if square else per_device,
         mesh=mesh,
         in_specs=(
             P("tp", "wide", None),

time: 1200 us -> 221 us (0.18)
  waiting for transfers between devices: 758 us -> 0 us
  Pallas kernels: 0 us -> 218 us
  blocking collectives: 172 us -> 0 us
  matrix products: 108 us -> 0 us
  local copies, waits for them, and re-layouts: 86.3 us -> 1.44 us
  other arithmetic: 54.7 us -> 0 us
  between operations: 16.1 us -> 0.68 us
    reduce_scatter x9 -> x0, waiting for transfers between devices: 350 us -> none  [the longest x1 60.6 us: per_device(): lax.psum_scatter(times_transposed(grad_pre, up_w), 'tp', scatter_dimensio...]
    all_gather x9 -> x0, waiting for transfers between devices: 304 us -> none  [the longest x2 70.8 us: attention_forward(): pairs_all = lax.all_gather(pairs, 'wide', axis=1, tiled=True)]
    pallas_call x0 -> x2, Pallas kernels: none -> 218 us  [the longest x1 215 us: layer_pass(): pl.pallas_call(functools.partial(layer_body, depth), out_shape=[rows, row...]
    all_gather x13 -> x0, blocking collectives: 120 us -> none  [the longest x1 12.5 us: per_device(): lax.all_gather(w_query, 'wide', axis=0, tiled=True)]
    dot_general x39 -> x0, matrix products: 108 us -> none  [the longest x9 29.7 us: row_product(): return jnp.dot(first_op, second_op, preferred_element_type=jnp.float32)]
    unnamed x24 -> x0, waiting for transfers between devices: 104 us -> none
    psum x1 -> x0, blocking collectives: 39.7 us -> none  [per_device(): lax.psum((grad_gain_one, grad_shift_one, grad_dense_b, grad_gain_two, gra...]
    reduce_sum x17 -> x0, other arithmetic: 27.4 us -> none  [the longest x4 9.96 us: forward_group(): jnp.sum(jnp.exp(masked - highest), axis=-1, keepdims=True)]
  transfers between devices with their start and end apart: 21 -> 0, of which waited for: 21 -> 0; matrix products, arithmetic and copies ran while one was open for 7% -> 0% of each run, Pallas kernels for 0% -> 0%
where the time goes in v4:
time: 221 us; the launch traced here: 220 us
  Pallas kernels  218 us (99%)
    pallas_call x1, Pallas kernels, layer_pass(): pl.pallas_call(functools.partial(layer_body, depth), out_shape=[rows, row...  215 us

profile of v4, /device:TPU:0, one launch (start us, length us, event | category | flops | bytes accessed | tf_op | source)
XLA Modules:
  0.0 220.4 jit_solution(9392468096820478170)
XLA Ops:
  0.7 215.1 %layer.1 = (bf16[2,128,1024]{2,1,0:T(8,128)(2,1)}, bf16[2,128,1024]{2,1,0:T(8,128)(2,1)}, f32[2,4,128,128]{3,2,1,0:T(8,128)}, bf16[8,2,128,128]{3,2,1,0:T(8,128)...) custom-call(s32[8]{0:T(128)} %lengths.1, bf16[2,128,1024]{2,1,0:T(8,128)(2,1)} %hidden.1, ...), custom_call_target="tpu_custom_call" | custom-call | tf_op jit(solution)/shard_map/layer/pallas_call | solution.py:1480
  215.8 3.2 %write_out.1 = (bf16[2,128,1024]{2,1,0:T(8,128)(2,1)}, bf16[2,128,1024]{2,1,0:T(8,128)(2,1)}, f32[128,256]{1,0:T(8,128)}, f32[128,256]{1,0:T(8,128)}, f32[128,25...) custom-call(bf16[2,128,1024]{2,1,0:T(8,128)(2,1)} %get-tuple-element, ...), custom_call_target="tpu_custom_call" | custom-call | tf_op jit(solution)/shard_map/write_out/pallas_call | solution.py:1621
  219.0 1.4 slice_bitcast_fusion

commit v5 on v4

--- a/solution.py
+++ b/solution.py
@@ -414,25 +414,19 @@
 class SquareGather:
     SENDS = 13
 
-    def __init__(self, src, dst, send, recv, local):
+    def __init__(self, src, place, both, send, recv, local=None):
         own, pair, ax, ay, dg = square_places()
-
-        def place(slot, dev):
-            return dst.at[slot, pl.ds(pl.multiple_of(dev * BLK, BLK), BLK)]
-
-        def both(dev):
-            return dst.at[:, pl.ds(pl.multiple_of(dev * BLK, BLK), BLK)]
-
+        first, second, whole = src
         to_x, to_y, to_p = {"wide": ax}, {"wide": ay}, {"wide": pair}
-        self.local = pltpu.make_async_copy(src, both(own), local)
+        self.local = None if local is None else pltpu.make_async_copy(whole, both(own), local)
         copies = {}
-        copies["x0"] = remote(src.at[0], place(0, own), send.at[0], recv.at[0], to_x)
-        copies["x1"] = remote(src.at[1], place(1, own), send.at[1], recv.at[1], to_x)
-        copies["y0"] = remote(src.at[0], place(0, own), send.at[2], recv.at[2], to_y)
-        copies["y1"] = remote(src.at[1], place(1, own), send.at[3], recv.at[3], to_y)
+        copies["x0"] = remote(first, place(0, own), send.at[0], recv.at[0], to_x)
+        copies["x1"] = remote(second, place(1, own), send.at[1], recv.at[1], to_x)
+        copies["y0"] = remote(first, place(0, own), send.at[2], recv.at[2], to_y)
+        copies["y1"] = remote(second, place(1, own), send.at[3], recv.at[3], to_y)
         copies["d0"] = remote(place(0, ay), place(0, ay), send.at[4], recv.at[4], to_x)
         copies["d1"] = remote(place(1, ax), place(1, ax), send.at[5], recv.at[5], to_y)
-        copies["p"] = remote(src, both(own), send.at[6], recv.at[6], to_p)
+        copies["p"] = remote(whole, both(own), send.at[6], recv.at[6], to_p)
         for index, (name, slot, dev) in enumerate(
             (("x0", 0, ax), ("x1", 1, ax), ("y0", 0, ay), ("y1", 1, ay), ("d0", 0, dg), ("d1", 1, dg))
         ):
@@ -444,7 +438,8 @@
     def start(self):
         for name in ("y0", "x1", "x0", "y1", "p"):
             self.copies[name].start()
-        self.local.start()
+        if self.local is not None:
+            self.local.start()
 
     def pass_on(self, arrived, sends):
         self.copies[arrived].wait_recv()
@@ -470,11 +465,6 @@
     def sent(self):
         for copy in self.copies.values():
             copy.wait_send()
-
-    def finish(self):
-        self.arrive("p", "px0", "px1", "py0", "py1", "pd0", "pd1")
-        self.sent()
-        self.local.wait()
 
 
 def wide_square(own_places):
@@ -499,37 +489,29 @@
 class SquareScatter:
     SENDS = 10
 
-    def __init__(self, src, out, summed, from_x, from_y, send, recv):
+    def __init__(self, both, half, out, summed_both, summed, from_x, from_y, send, recv):
         own, pair, ax, ay, dg = square_places()
         shift = pair - own
         to_x, to_y, to_p = {"wide": ax}, {"wide": ay}, {"wide": pair}
-        self.src, self.out = src, out
+        self.half, self.out = half, out
         self.summed, self.from_x, self.from_y = summed, from_x, from_y
         self.dests = (dg, ax, ay, own)
-        self.pairs = []
-        for chip in range(4):
-            rows = pl.ds(pl.multiple_of((self.dests[chip] + shift) * BLK, BLK), BLK)
-            self.pairs.append(
-                remote(src.at[:, rows], summed.at[chip], send.at[chip], recv.at[chip], to_p)
+        self.pairs = [
+            remote(
+                both(self.dests[chip] + shift), summed_both(chip), send.at[chip], recv.at[chip], to_p
             )
-        self.dx = remote(summed.at[0, 0], from_x.at[0], send.at[4], recv.at[4], to_x)
-        self.dy = remote(summed.at[0, 1], from_y.at[0], send.at[5], recv.at[5], to_y)
-        self.xx = remote(summed.at[1, 0], from_x.at[1], send.at[6], recv.at[6], to_x)
-        self.yy = remote(summed.at[2, 1], from_y.at[1], send.at[7], recv.at[7], to_y)
-        self.ty = remote(summed.at[2, 0], from_y.at[2], send.at[8], recv.at[8], to_y)
-        self.tx = remote(summed.at[1, 1], from_x.at[2], send.at[9], recv.at[9], to_x)
-
-    def block(self, slot, chip):
-        rows = pl.ds(pl.multiple_of(self.dests[chip] * BLK, BLK), BLK)
-        return self.src.at[slot, rows]
+            for chip in range(4)
+        ]
+        self.dx = remote(summed(0, 0), from_x(0), send.at[4], recv.at[4], to_x)
+        self.dy = remote(summed(0, 1), from_y(0), send.at[5], recv.at[5], to_y)
+        self.xx = remote(summed(1, 0), from_x(1), send.at[6], recv.at[6], to_x)
+        self.yy = remote(summed(2, 1), from_y(1), send.at[7], recv.at[7], to_y)
+        self.ty = remote(summed(2, 0), from_y(2), send.at[8], recv.at[8], to_y)
+        self.tx = remote(summed(1, 1), from_x(2), send.at[9], recv.at[9], to_x)
 
     def pair_sum(self, chip, slot, third=None):
-        add_rows(
-            self.summed.at[chip, slot],
-            self.block(slot, chip),
-            self.summed.at[chip, slot],
-            third,
-        )
+        place = self.summed(chip, slot)
+        add_rows(place, self.half(slot, self.dests[chip]), place, third)
 
     def near(self, chip):
         self.pairs[chip].wait_recv()
@@ -550,30 +532,23 @@
 
     def middle(self):
         self.dx.wait_recv()
-        self.pair_sum(2, 0, self.from_x.at[0])
+        self.pair_sum(2, 0, self.from_x(0))
         self.ty.start()
         self.dy.wait_recv()
-        self.pair_sum(1, 1, self.from_y.at[0])
+        self.pair_sum(1, 1, self.from_y(0))
         self.tx.start()
 
     def start(self):
         for chip in range(4):
             self.pairs[chip].start()
 
-    def first(self):
-        for chip in range(3):
-            self.near(chip)
-
-    def own_sums(self):
-        self.near(3)
-
     def finish(self):
         self.xx.wait_recv()
         self.ty.wait_recv()
-        add_rows(self.out.at[0], self.summed.at[3, 0], self.from_x.at[1], self.from_y.at[2])
+        add_rows(self.out.at[0], self.summed(3, 0), self.from_x(1), self.from_y(2))
         self.yy.wait_recv()
         self.tx.wait_recv()
-        add_rows(self.out.at[1], self.summed.at[3, 1], self.from_y.at[1], self.from_x.at[2])
+        add_rows(self.out.at[1], self.summed(3, 1), self.from_y(1), self.from_x(2))
         for copy in self.pairs:
             copy.wait_send()
         for copy in (self.dx, self.dy, self.xx, self.yy, self.ty, self.tx):
@@ -669,56 +644,54 @@
     return edge if step == 0 else jnp.concatenate([scores[: extent - QB], edge], 0)
 
 
-def attend_slot(slot, length, slopes, qkv, out, totals, bias):
+def attend_head(slot, head, length, slopes, qkv, out, totals, bias):
     rows = qkv.shape[1]
-    for head in range(2):
-        lanes = pl.ds(head * HEAD, HEAD)
-        bias[...] = head_bias(length, slopes[head], rows)
-        key = qkv[slot, :, pl.ds(2 * HEAD + head * HEAD, HEAD)]
-        value_t = qkv[slot, :, pl.ds(4 * HEAD + head * HEAD, HEAD)].T
-        for step in range(rows // QB):
-            here = pl.ds(step * QB, QB)
-            scores = slot_scores(key, qkv[slot, here, lanes], bias, step)
-            highest = jnp.max(scores, axis=0, keepdims=True)
-            weights = jnp.exp2(scores - highest)
-            total = jnp.sum(weights, axis=0, keepdims=True)
-            mixed = dot_nn(value_t[:, : (step + 1) * QB], weights.astype(BF)) / total
-            out[slot, here, lanes] = mixed.T.astype(BF)
-            totals[slot, pl.ds(head, 1), here] = highest + jnp.log2(total)
-
-
-def attend_slot_back(
-    slot, length, slopes, qkv, attention, grad, totals, out, bias, key_sum, value_sum
+    lanes = pl.ds(head * HEAD, HEAD)
+    bias[...] = head_bias(length, slopes[head], rows)
+    key = qkv[slot, :, pl.ds(2 * HEAD + head * HEAD, HEAD)]
+    value_t = qkv[slot, :, pl.ds(4 * HEAD + head * HEAD, HEAD)].T
+    for step in range(rows // QB):
+        here = pl.ds(step * QB, QB)
+        scores = slot_scores(key, qkv[slot, here, lanes], bias, step)
+        highest = jnp.max(scores, axis=0, keepdims=True)
+        weights = jnp.exp2(scores - highest)
+        total = jnp.sum(weights, axis=0, keepdims=True)
+        mixed = dot_nn(value_t[:, : (step + 1) * QB], weights.astype(BF)) / total
+        out[slot, here, lanes] = mixed.T.astype(BF)
+        totals[slot, pl.ds(head, 1), here] = highest + jnp.log2(total)
+
+
+def attend_head_back(
+    slot, head, length, slopes, qkv, attention, grad, totals, out, bias, key_sum, value_sum
 ):
     rows = qkv.shape[1]
-    for head in range(2):
-        lanes = pl.ds(head * HEAD, HEAD)
-        key_lanes = pl.ds(2 * HEAD + head * HEAD, HEAD)
-        value_lanes = pl.ds(4 * HEAD + head * HEAD, HEAD)
-        bias[...] = head_bias(length, slopes[head], rows)
-        key = qkv[slot, :, key_lanes]
-        value = qkv[slot, :, value_lanes]
-        key_t = key.T
-        key_sum[...] = jnp.zeros_like(key_sum)
-        value_sum[...] = jnp.zeros_like(value_sum)
-        for step in range(rows // QB):
-            here = pl.ds(step * QB, QB)
-            extent = (step + 1) * QB
-            query = qkv[slot, here, lanes]
-            grad_rows = grad[slot, here, lanes]
-            product = grad_rows.astype(F32) * attention[slot, here, lanes].astype(F32)
-            delta = jnp.sum(product.T, axis=0, keepdims=True)
-            scores = slot_scores(key, query, bias, step)
-            probs = jnp.exp2(scores - totals[slot, pl.ds(head, 1), here])
-            grad_probs = dot_nt(value[:extent], grad_rows)
-            grad_scores = (probs * (grad_probs - delta)).astype(BF)
-            span = pl.ds(0, extent)
-            value_sum[span] += dot_nn(probs.astype(BF), grad_rows)
-            key_sum[span] += dot_nn(grad_scores, query)
-            grad_query = dot_nn(key_t[:, :extent], grad_scores)
-            out[slot, here, lanes] = (grad_query.T * 0.125).astype(BF)
-        out[slot, :, key_lanes] = (key_sum[...] * 0.125).astype(BF)
-        out[slot, :, value_lanes] = value_sum[...].astype(BF)
+    lanes = pl.ds(head * HEAD, HEAD)
+    key_lanes = pl.ds(2 * HEAD + head * HEAD, HEAD)
+    value_lanes = pl.ds(4 * HEAD + head * HEAD, HEAD)
+    bias[...] = head_bias(length, slopes[head], rows)
+    key = qkv[slot, :, key_lanes]
+    value = qkv[slot, :, value_lanes]
+    key_t = key.T
+    key_sum[...] = jnp.zeros_like(key_sum)
+    value_sum[...] = jnp.zeros_like(value_sum)
+    for step in range(rows // QB):
+        here = pl.ds(step * QB, QB)
+        extent = (step + 1) * QB
+        query = qkv[slot, here, lanes]
+        grad_rows = grad[slot, here, lanes]
+        product = grad_rows.astype(F32) * attention[slot, here, lanes].astype(F32)
+        delta = jnp.sum(product.T, axis=0, keepdims=True)
+        scores = slot_scores(key, query, bias, step)
+        probs = jnp.exp2(scores - totals[slot, pl.ds(head, 1), here])
+        grad_probs = dot_nt(value[:extent], grad_rows)
+        grad_scores = (probs * (grad_probs - delta)).astype(BF)
+        span = pl.ds(0, extent)
+        value_sum[span] += dot_nn(probs.astype(BF), grad_rows)
+        key_sum[span] += dot_nn(grad_scores, query)
+        grad_query = dot_nn(key_t[:, :extent], grad_scores)
+        out[slot, here, lanes] = (grad_query.T * 0.125).astype(BF)
+    out[slot, :, key_lanes] = (key_sum[...] * 0.125).astype(BF)
+    out[slot, :, value_lanes] = value_sum[...].astype(BF)
 
 
 def line_others(depth):
@@ -811,13 +784,13 @@
     output,
     grad_in,
     attn_sum,
+    dense_sum,
     ffn_x,
     vec_sums,
     unit_sums,
     hidden_all,
     normed,
     down_all,
-    branch_all,
     second_share,
     down_share,
     qkv,
@@ -830,13 +803,14 @@
     key_sum,
     value_sum,
     qkv_w,
-    dense_w,
+    dense_all,
+    att_own,
+    att_grad_own,
     up_t,
     down_t,
     up_w,
     down_w,
     z_qkv,
-    z_dense,
     z_vec,
     vec_wide,
     vec_line,
@@ -859,6 +833,8 @@
     attn_g,
     attn_in,
     attn_z,
+    dense_out,
+    dense_in,
     parts,
     gathered,
     a_summed,
@@ -882,6 +858,8 @@
     grad_line_recv,
     onward_send,
     onward_recv,
+    dense_send,
+    dense_recv,
     sum_send,
     sum_recv,
     own_sems,
@@ -921,11 +899,19 @@
         return carry
 
     lax.fori_loop(0, steps, down_part, 0)
-    greet([{"wide": wide, "tp": tp} for wide, tp in others])
+    greet(wide_others(own) + line_others(depth))
+
+    def block_rows(dev):
+        return pl.ds(pl.multiple_of(dev * BLK, BLK), BLK)
 
     def gather_of(number, src, dst):
         return SquareGather(
-            src, dst, gather_send.at[number], gather_recv.at[number], gather_local.at[number]
+            (src.at[0], src.at[1], src),
+            lambda slot, dev: dst.at[slot, block_rows(dev)],
+            lambda dev: dst.at[:, block_rows(dev)],
+            gather_send.at[number],
+            gather_recv.at[number],
+            gather_local.at[number],
         )
 
     def wide_of(number, source, target):
@@ -941,7 +927,7 @@
             (w_query, lambda at: z_qkv.at[at, 0]),
             (w_key, lambda at: z_qkv.at[at, 1]),
             (w_value, lambda at: z_qkv.at[at, 2]),
-            (w_dense, lambda at: z_dense.at[at]),
+            (w_dense, lambda at: dense_all.at[own, at]),
             (vec_line, lambda at: z_vec.at[at]),
         ],
         line_send,
@@ -978,6 +964,20 @@
     line.arrive(1)
     line.start(2)
     hid.second()
+    ups = wide_of(
+        3, lambda dev: w_up.at[:, block_rows(dev)], lambda dev: up_t.at[block_rows(dev)]
+    )
+    downs = wide_of(
+        4, lambda dev: w_down.at[block_rows(dev)], lambda dev: down_t.at[:, block_rows(dev)]
+    )
+    unit_copies = [
+        pltpu.make_async_copy(w_up.at[:, own_lanes], up_t.at[own_lanes], own_sems.at[6]),
+        pltpu.make_async_copy(w_down.at[own_lanes], down_t.at[:, own_lanes], own_sems.at[7]),
+    ]
+    ups.start()
+    downs.start()
+    for copy in unit_copies:
+        copy.start()
     line.arrive(2)
     line.start(3)
     hid.arrive("px0", "px1", "py0", "py1")
@@ -993,34 +993,22 @@
     heads = wide_of(
         1,
         lambda dev: z_qkv.at[dev // per_layer, :, :, goal_lanes(dev)],
-        lambda dev: attn_in.at[dev, pl.ds(0, 3)],
-    )
-    dense = wide_of(
-        2,
-        lambda dev: z_dense.at[dev // per_layer, goal_lanes(dev)],
-        lambda dev: dense_w.at[:, own_lanes],
-    )
-    biases = wide_of(3, lambda dev: z_vec, lambda dev: vec_line_all.at[dev])
-    ups = wide_of(
-        4,
-        lambda dev: w_up.at[:, pl.ds(pl.multiple_of(dev * BLK, BLK), BLK)],
-        lambda dev: up_t.at[own_lanes],
-    )
-    downs = wide_of(
-        5,
-        lambda dev: w_down.at[pl.ds(pl.multiple_of(dev * BLK, BLK), BLK)],
-        lambda dev: down_t.at[:, own_lanes],
-    )
-    arrivals = (biases, heads, dense, ups, downs)
-    for exchange in arrivals:
-        exchange.start()
+        lambda dev: attn_in.at[dev],
+    )
+    biases = wide_of(2, lambda dev: z_vec, lambda dev: vec_line_all.at[dev])
+    dense = SquareGather(
+        (dense_all.at[own, pl.ds(0, 2)], dense_all.at[own, pl.ds(2, 2)], dense_all.at[own]),
+        lambda half, dev: dense_all.at[dev, pl.ds(2 * half, 2)],
+        lambda dev: dense_all.at[dev],
+        gather_send.at[3],
+        gather_recv.at[3],
+    )
+    biases.start()
+    heads.start()
+    dense.start()
     gd = gather_of(1, down_own, down_all)
-    gd.start()
     own_copies = [
-        pltpu.make_async_copy(z_qkv.at[own // per_layer, :, :, goal_lanes(own)], attn_in.at[own, pl.ds(0, 3)], own_sems.at[5]),
-        pltpu.make_async_copy(z_dense.at[own // per_layer, goal_lanes(own)], dense_w.at[:, own_lanes], own_sems.at[6]),
-        pltpu.make_async_copy(w_up.at[:, own_lanes], up_t.at[own_lanes], own_sems.at[7]),
-        pltpu.make_async_copy(w_down.at[own_lanes], down_t.at[:, own_lanes], own_sems.at[8]),
+        pltpu.make_async_copy(z_qkv.at[own // per_layer, :, :, goal_lanes(own)], attn_in.at[own], own_sems.at[5]),
     ]
     for copy in own_copies:
         copy.start()
@@ -1045,8 +1033,11 @@
             values = vec_line_all[4 * (own % 2) + part, up, pl.ds(unit_row, 1)]
             up_bias[:, up * BLK + part * 32 : up * BLK + part * 32 + 32] = values[:, 0:32]
     heads.arrive()
-    for copy in own_copies:
+    hid.sent()
+    for copy in own_copies + unit_copies:
         copy.wait()
+    ups.arrive()
+    downs.arrive()
     for dev in range(8):
         for kind in range(3):
             qkv_w[dev * BLK : (dev + 1) * BLK, kind * BLK : (kind + 1) * BLK] = attn_in[dev, kind]
@@ -1060,10 +1051,29 @@
         ffn_line_send,
         ffn_line_recv,
     )
+    ffn_line.start(1)
+    unit_copies = [
+        pltpu.make_async_copy(ref, place(layer), own_sems.at[8 + number])
+        for number, (ref, place) in enumerate(ffn_line.pieces)
+    ]
+    for copy in unit_copies:
+        copy.start()
     slopes = [
         jnp.exp2(-0.5 * (jnp.full((1, 1), 2 * own + head, jnp.int32).astype(F32) + 1.0)) * LOG2E
         for head in range(2)
     ]
+
+    def att_exchange(slot):
+        return wide_of(
+            7 + slot,
+            lambda dev: attention.at[slot, block_rows(dev)],
+            lambda dev: att_own.at[slot, :, block_rows(dev)],
+        )
+
+    def att_local(slot):
+        return pltpu.make_async_copy(
+            attention.at[slot, block_rows(own)], att_own.at[slot, :, block_rows(own)], own_sems.at[10 + slot]
+        )
 
     def one_slot(slot, carry):
         def block(index, carry):
@@ -1072,53 +1082,55 @@
             return carry
 
         lax.fori_loop(0, 8 * BLK // QB, block, 0)
-        attend_slot(slot, lengths[layer * 2 + slot], slopes, qkv, attention, totals, bias)
+        length = lengths[layer * 2 + slot]
+        attend_head(slot, 0, length, slopes, qkv, attention, totals, bias)
 
         @pl.when(slot == 0)
         def _():
-            ups.arrive()
-            downs.arrive()
-            ffn_line.start(1)
+            dense.first()
+            dense.second()
+
+        attend_head(slot, 1, length, slopes, qkv, attention, totals, bias)
+        att_exchange(slot).start()
+        att_local(slot).start()
+
+        @pl.when(slot == 0)
+        def _():
+            ffn_line.arrive(1)
+            ffn_line.start(2)
+            dense.third()
+            gd.start()
 
         return carry
 
     lax.fori_loop(0, 2, one_slot, 0)
-    own_copies = [
-        pltpu.make_async_copy(ref, place(layer), own_sems.at[9 + number])
-        for number, (ref, place) in enumerate(ffn_line.pieces)
-    ]
-    for copy in own_copies:
-        copy.start()
-    hid.sent()
-    dense.arrive()
-    share = branch_all
-
-    def dense_block(index, carry):
-        rows = pl.ds(pl.multiple_of(relation(index) * BLK, BLK), BLK)
-        values = attention[:, rows].reshape(2 * BLK, 2 * HEAD)
-        share[:, rows] = dot_nn(values, dense_w[...]).astype(BF).reshape(2, BLK, width)
-        return carry
-
-    def scatter_of(number, src, out, buffers):
-        return SquareScatter(src, out, *buffers, scatter_send.at[number], scatter_recv.at[number])
-
-    scatter = scatter_of(0, share, residual, (a_summed, a_x, a_y))
-    for chip in range(4):
-        start = (6, 2, 4, 0)[chip]
-        lax.fori_loop(start, start + 2, dense_block, 0)
-        scatter.pairs[chip].start()
-        if chip:
-            scatter.near(chip - 1)
     gd.first()
-    ffn_line.arrive(1)
-    ffn_line.start(2)
-    scatter.near(3)
     gd.second()
-    scatter.middle()
-    gd.third()
     ffn_line.arrive(2)
     ffn_line.start(3)
-    scatter.finish()
+    dense.arrive("p", "px0", "px1", "py0", "py1", "pd0", "pd1")
+    for slot in range(2):
+        att_exchange(slot).arrive()
+        att_local(slot).wait()
+
+    for part in range(4):
+        columns = [dense_all[2 * part + side].reshape(width, BLK) for side in range(2)]
+        product = dot_nn(att_own[...].reshape(2 * BLK, width), jnp.concatenate(columns, 1))
+        residual[:, :, part * QB : (part + 1) * QB] = product.reshape(2, BLK, QB)
+
+    def scatter_of(number, share, out, buffers):
+        summed, from_x, from_y = buffers
+        return SquareScatter(
+            lambda dev: share.at[:, block_rows(dev)],
+            lambda slot, dev: share.at[slot, block_rows(dev)],
+            out,
+            lambda chip: summed.at[chip],
+            lambda chip, slot: summed.at[chip, slot],
+            lambda place: from_x.at[place],
+            lambda place: from_y.at[place],
+            scatter_send.at[number],
+            scatter_recv.at[number],
+        )
 
     def second_part(index, carry):
         rows = pl.ds(pl.multiple_of(index * step, step), step)
@@ -1133,10 +1145,10 @@
     second_all = hidden_all
     gather = gather_of(2, own_rows, second_all)
     gather.start()
-    scatter = scatter_of(1, second_share, grad_second, (a_summed, a_x, a_y))
-    gd.arrive("p", "px0", "px1", "py0", "py1", "pd0", "pd1")
+    scatter = scatter_of(0, second_share, grad_second, (a_summed, a_x, a_y))
+    gd.arrive("p")
     gd.local.wait()
-    for copy in own_copies:
+    for copy in unit_copies:
         copy.wait()
     ffn_line.arrive(3)
 
@@ -1164,7 +1176,9 @@
     lax.fori_loop(0, 2, compute, 0)
     scatter.pairs[3].start()
     gather.first()
+    gd.third()
     gather.second()
+    gd.arrive("px0", "px1", "py0", "py1")
     gather.arrive("px0", "px1", "py0", "py1")
     lax.fori_loop(2, 4, compute, 0)
     scatter.pairs[1].start()
@@ -1173,6 +1187,7 @@
     scatter.pairs[2].start()
     gather.third()
     scatter.near(1)
+    gd.arrive("pd0", "pd1")
     gather.arrive("pd0", "pd1")
     lax.fori_loop(6, 8, compute, 0)
     scatter.pairs[0].start()
@@ -1241,88 +1256,116 @@
         return carry
 
     lax.fori_loop(0, steps, back_part, 0)
-    again = gather_of(3, own_rows, branch_all)
-    again.start()
-    down = scatter_of(2, down_share, down_out, (b_summed, b_x, b_y))
+    for at in range(depth):
+        columns = jnp.concatenate([dense_all[dev, at] for dev in range(8)], 1)
+        product = dot_nt(own_rows[...].reshape(2 * BLK, width), columns).astype(BF)
+        att_grad_own[:, :, at * QB : (at + 1) * QB] = product.reshape(2, BLK, QB)
+
+    def att_back(slot):
+        return wide_of(
+            9 + slot,
+            lambda dev: att_grad_own.at[slot, :, block_rows(dev)],
+            lambda dev: grad_att.at[slot, block_rows(dev)],
+        )
+
+    def att_back_local(slot):
+        return pltpu.make_async_copy(
+            att_grad_own.at[slot, :, block_rows(own)], grad_att.at[slot, block_rows(own)], own_sems.at[12 + slot]
+        )
+
+    for slot in range(2):
+        att_back(slot).start()
+        att_back_local(slot).start()
+    down = scatter_of(1, down_share, down_out, (b_summed, b_x, b_y))
     down.start()
 
-    def att_block(index, carry):
-        rows = pl.ds(pl.multiple_of(relation(index) * BLK, BLK), BLK)
-        values = branch_all[:, rows].reshape(2 * BLK, width)
-        grad_att[:, rows] = dot_nt(values, dense_w[...]).astype(BF).reshape(2, BLK, 2 * HEAD)
-        return carry
-
-    again.arrive("p")
-    again.local.wait()
-    lax.fori_loop(0, 2, att_block, 0)
-    again.first()
-    down.near(0)
-    again.second()
-    again.arrive("px0", "px1", "py0", "py1")
-    down.near(1)
-    down.near(2)
-    lax.fori_loop(2, 6, att_block, 0)
-    again.third()
-    again.arrive("pd0", "pd1")
-    lax.fori_loop(6, 8, att_block, 0)
-
-    dense_part = dot_nn(attention[0].T, branch_all[0]) + dot_nn(attention[1].T, branch_all[1])
-    dense_part = dense_part.astype(BF)
-    for blk in range(8):
-        attn_g[blk, 3] = dense_part[:, blk * BLK : (blk + 1) * BLK]
-    kinds = (pl.ds(3, 1), pl.ds(0, 3))
-    exchanges = [
-        wide_of(
-            6 + group,
-            lambda dev, kind=kind: attn_g.at[dev, kind],
-            lambda dev, kind=kind: attn_in.at[dev, kind],
-        )
-        for group, kind in enumerate(kinds)
-    ]
-
-    def onward(group, index, source):
-        return remote(
-            source.at[index, kinds[group]],
-            attn_z.at[layer, index % per_layer, kinds[group]],
-            onward_send.at[group, index],
-            onward_recv.at[group, layer, index % per_layer],
-            {"tp": index // per_layer},
-        )
-
-    def forward(group, index, source):
-        @pl.when(index // per_layer != layer)
-        def _():
-            onward(group, index, source).start()
-
-    def forward_all(group):
-        for number in range(1, 8):
-            exchanges[group].copies[number - 1].wait_recv()
-            forward(group, (own + 8 - number) % 8, attn_in)
-
-    exchanges[0].start()
-    forward(0, own, attn_g)
-    ffn = wide_of(8, lambda dev: ffn_sum.at[dev], lambda dev: ffn_x.at[dev])
+    half_lanes = pl.ds(0, width // 2)
+    sum_lanes = pl.ds(width // 2, width // 2)
+    for part in range(4):
+        rows = slice(part * QB, (part + 1) * QB)
+        left = own_rows[:, :, rows].reshape(2 * BLK, QB).T
+        for half in range(2):
+            lanes = slice(half * width // 2, (half + 1) * width // 2)
+            product = dot_nn(left, att_own[:, :, lanes].reshape(2 * BLK, width // 2))
+            second_all[half, rows, half_lanes] = product.astype(BF)
+    dense_back = SquareScatter(
+        lambda dev: second_all.at[:, block_rows(dev), half_lanes],
+        lambda half, dev: second_all.at[half, block_rows(dev), half_lanes],
+        dense_out,
+        lambda chip: second_all.at[:, pl.ds(chip * BLK, BLK), sum_lanes],
+        lambda chip, half: second_all.at[half, pl.ds(chip * BLK, BLK), sum_lanes],
+        lambda place: second_all.at[0, pl.ds((4 + place) * BLK, BLK), sum_lanes],
+        lambda place: second_all.at[1, pl.ds((4 + place) * BLK, BLK), sum_lanes],
+        scatter_send.at[3],
+        scatter_recv.at[3],
+    )
+
+    def dense_piece(at):
+        return dense_out.at[at // 2, :, pl.ds(pl.multiple_of((at % 2) * QB, QB), QB)]
+
+    def dense_copies():
+        return [
+            remote(
+                dense_piece((layer + up) % depth),
+                dense_in.at[up - 1],
+                dense_send.at[up - 1],
+                dense_recv.at[up - 1],
+                {"tp": (layer + up) % depth},
+            )
+            for up in range(1, depth)
+        ]
+
+    att_back(0).arrive()
+    att_back_local(0).wait()
+    dense_back.start()
+    for chip in range(3):
+        down.near(chip)
+    for chip in range(3):
+        dense_back.near(chip)
+
+    def ffn_exchange(kind):
+        return wide_of(5 + kind, lambda dev: ffn_sum.at[dev, kind], lambda dev: ffn_x.at[dev, kind])
 
     def slot_back(slot, carry):
-        attend_slot_back(
-            slot,
-            lengths[layer * 2 + slot],
-            slopes,
-            qkv,
-            attention,
-            grad_att,
-            totals,
-            qkv,
-            bias,
-            key_sum,
-            value_sum,
-        )
+        def one_head(head):
+            attend_head_back(
+                slot,
+                head,
+                lengths[layer * 2 + slot],
+                slopes,
+                qkv,
+                attention,
+                grad_att,
+                totals,
+                qkv,
+                bias,
+                key_sum,
+                value_sum,
+            )
+
+        one_head(0)
 
         @pl.when(slot == 0)
         def _():
-            forward_all(0)
+            down.near(3)
             down.middle()
+            dense_back.near(3)
+
+        @pl.when(slot == 1)
+        def _():
+            dense_back.finish()
+            for copy in dense_copies():
+                copy.start()
             line_sums(0)
+            ffn_exchange(0).start()
+
+        one_head(1)
+
+        @pl.when(slot == 0)
+        def _():
+            dense_back.middle()
+            att_back(1).arrive()
+            att_back_local(1).wait()
 
         return carry
 
@@ -1335,11 +1378,27 @@
             attn_g[blk, kind] = weight_part[
                 kind * BLK : (kind + 1) * BLK, blk * BLK : (blk + 1) * BLK
             ]
-    exchanges[1].start()
-    forward(1, own, attn_g)
+    exchange = wide_of(11, lambda dev: attn_g.at[dev], lambda dev: attn_in.at[dev])
+
+    def onward(index, source):
+        return remote(
+            source.at[index],
+            attn_z.at[layer, index % per_layer],
+            onward_send.at[index],
+            onward_recv.at[layer, index % per_layer],
+            {"tp": index // per_layer},
+        )
+
+    def forward(index, source):
+        @pl.when(index // per_layer != layer)
+        def _():
+            onward(index, source).start()
+
+    exchange.start()
+    forward(own, attn_g)
     share = second_share
     grad_normed = grad_second
-    scatter = scatter_of(3, share, grad_normed, (a_summed, a_x, a_y))
+    scatter = scatter_of(2, share, grad_normed, (a_summed, a_x, a_y))
 
     def normed_block(index, carry):
         rows = pl.ds(pl.multiple_of(relation(index) * BLK, BLK), BLK)
@@ -1354,10 +1413,9 @@
         if chip:
             scatter.near(chip - 1)
     line_sums(1)
-    ffn.start()
+    ffn_exchange(1).start()
     head_sum = jnp.sum(grad_qkv[0].astype(F32), axis=0, keepdims=True)
     head_sum = head_sum + jnp.sum(grad_qkv[1].astype(F32), axis=0, keepdims=True)
-    down.near(3)
     down.finish()
 
     def out_part(index, carry):
@@ -1368,7 +1426,9 @@
         return carry
 
     lax.fori_loop(0, steps, out_part, 0)
-    forward_all(1)
+    for number in range(1, 8):
+        exchange.copies[number - 1].wait_recv()
+        forward((own + 8 - number) % 8, attn_in)
     scatter.near(3)
     scatter.middle()
     for blk in range(8):
@@ -1412,26 +1472,32 @@
     for copy in sum_copies:
         copy.start()
     gathered[own, layer] = parts[own]
-    for group in range(2):
-        for up in range(1, depth):
-            source = (layer + up) % depth
-            for number in range(per_layer):
-                remote(
-                    attn_in.at[number, kinds[group]],
-                    attn_z.at[source, number, kinds[group]],
-                    onward_send.at[group, number],
-                    onward_recv.at[group, source, number],
-                    {"tp": source},
-                ).wait_recv()
+    for up in range(1, depth):
+        source = (layer + up) % depth
+        for number in range(per_layer):
+            remote(
+                attn_in.at[number],
+                attn_z.at[source, number],
+                onward_send.at[number],
+                onward_recv.at[source, number],
+                {"tp": source},
+            ).wait_recv()
     attn_in[own] = attn_g[own]
     for number in range(per_layer):
-        for kind in range(4):
+        for kind in range(3):
             total = attn_in[layer * per_layer + number, kind].astype(F32)
             for up in range(1, depth):
                 total = total + attn_z[(layer + up) % depth, number, kind].astype(F32)
             attn_sum[number, kind] = total
+    for copy in dense_copies():
+        copy.wait_recv()
+    total = dense_out[layer // 2, :, pl.ds(pl.multiple_of((layer % 2) * QB, QB), QB)].astype(F32)
+    for up in range(1, depth):
+        total = total + dense_in[up - 1].astype(F32)
+    dense_sum[...] = total
     ffn_x[own] = ffn_sum[own]
-    ffn.arrive()
+    for kind in range(2):
+        ffn_exchange(kind).arrive()
     for copy in sum_copies:
         copy.wait_recv()
 
@@ -1446,22 +1512,27 @@
 
     for copy in sum_copies:
         copy.wait_send()
-    for exchange in (gains, ffn) + arrivals + tuple(exchanges):
-        exchange.sent()
+    for slot in range(2):
+        att_exchange(slot).sent()
+        att_back(slot).sent()
+        ffn_exchange(slot).sent()
+    for sends in (gains, biases, heads, ups, downs, exchange):
+        sends.sent()
     for number in range(1, depth):
         line.sent(number)
         ffn_line.sent(number)
     for kind in range(2):
         for copy in line_copies(kind):
             copy.wait_send()
+    for copy in dense_copies():
+        copy.wait_send()
     gd.sent()
-    again.sent()
-    for group in range(2):
-        for index in range(8):
-
-            @pl.when(index // per_layer != layer)
-            def _(index=index, group=group):
-                onward(group, index, attn_in).wait_send()
+    dense.sent()
+    for index in range(8):
+
+        @pl.when(index // per_layer != layer)
+        def _(index=index):
+            onward(index, attn_in).wait_send()
 
 
 def layer_pass(depth, lengths, hidden, cotangent, *weights):
@@ -1482,14 +1553,15 @@
         out_shape=[
             rows,
             rows,
-            jax.ShapeDtypeStruct((per_layer, 4, BLK, BLK), F32),
+            jax.ShapeDtypeStruct((per_layer, 3, BLK, BLK), F32),
+            jax.ShapeDtypeStruct((BLK, per_layer * BLK), F32),
             jax.ShapeDtypeStruct((8, 2, BLK, BLK), BF),
             jax.ShapeDtypeStruct((16, BLK), F32),
             jax.ShapeDtypeStruct((8, 16, BLK), F32),
         ],
         in_specs=[pl.BlockSpec(memory_space=pltpu.SMEM)] + [vmem()] * len(operands),
-        out_specs=[vmem()] * 6,
-        scratch_shapes=[tokens] * 6
+        out_specs=[vmem()] * 7,
+        scratch_shapes=[tokens] * 5
         + [
             pltpu.VMEM((2, 8 * BLK, 6 * HEAD), BF),
             pltpu.VMEM((2, 8 * BLK, 2 * HEAD), BF),
@@ -1501,13 +1573,14 @@
             pltpu.VMEM((8 * BLK, HEAD), F32),
             pltpu.VMEM((8 * BLK, HEAD), F32),
             pltpu.VMEM((width, 6 * HEAD), BF),
-            pltpu.VMEM((2 * HEAD, width), BF),
+            pltpu.VMEM((8, depth, per_layer * BLK, BLK), BF),
+            own_bf,
+            own_bf,
             pltpu.VMEM((width, BLK), BF),
             pltpu.VMEM((BLK, width), BF),
             pltpu.VMEM((width, units), BF),
             pltpu.VMEM((units, width), BF),
             pltpu.VMEM((depth, 3, BLK, per_layer * BLK), BF),
-            pltpu.VMEM((depth, per_layer * BLK, BLK), BF),
             pltpu.VMEM((depth,) + line_vec, F32),
             pltpu.VMEM((8, BLK), F32),
             pltpu.VMEM(line_vec, F32),
@@ -1527,9 +1600,11 @@
             pltpu.VMEM((2, depth, 8, BLK, BLK), BF),
             pltpu.VMEM((2, depth - 1, 8, BLK, BLK), BF),
             pltpu.VMEM((8, 2, BLK, BLK), BF),
-            pltpu.VMEM((8, 4, BLK, BLK), BF),
-            pltpu.VMEM((8, 4, BLK, BLK), BF),
-            pltpu.VMEM((depth, per_layer, 4, BLK, BLK), BF),
+            pltpu.VMEM((8, 3, BLK, BLK), BF),
+            pltpu.VMEM((8, 3, BLK, BLK), BF),
+            pltpu.VMEM((depth, per_layer, 3, BLK, BLK), BF),
+            pltpu.VMEM((2, BLK, width // 2), BF),
+            pltpu.VMEM((depth - 1, BLK, per_layer * BLK), BF),
             pltpu.VMEM((8, 16, BLK), F32),
             pltpu.VMEM((8, depth, 16, BLK), F32),
         ]
@@ -1549,15 +1624,17 @@
             dma((2, 5, depth - 1)),
             dma((2, 2, depth - 1)),
             dma((2, 2, depth - 1)),
-            dma((9, 7)),
-            dma((9, 7)),
+            dma((12, 7)),
+            dma((12, 7)),
             dma((2, depth - 1)),
             dma((2, depth - 1)),
-            dma((2, 8)),
-            dma((2, depth, per_layer)),
+            dma((8,)),
+            dma((depth, per_layer)),
+            dma((depth - 1,)),
+            dma((depth - 1,)),
             dma((peers,)),
             dma((peers,)),
-            dma((11,)),
+            dma((14,)),
         ],
         compiler_params=pltpu.CompilerParams(
             collective_id=1, has_side_effects=True, vmem_limit_bytes=VMEM_MAX
@@ -1571,6 +1648,7 @@
     output_in,
     grad_in_in,
     attn_sum,
+    dense_sum,
     ffn_x,
     vec_in,
     unit_sums,
@@ -1585,7 +1663,7 @@
     up_b,
     query_b,
     value_b,
-    vec_sums,
+    *vec_rows,
 ):
     own = lax.axis_index("wide")
     layer = lax.axis_index("tp")
@@ -1596,7 +1674,7 @@
         lanes = slice(number * BLK, (number + 1) * BLK)
         for kind, target in enumerate((grad_q, grad_k, grad_v)):
             target[:, lanes] = attn_sum[number, kind].T
-        grad_d[lanes] = attn_sum[number, 3]
+    grad_d[...] = dense_sum[...].T
     for blk in range(8):
         lanes = slice(blk * BLK, (blk + 1) * BLK)
         grad_up[:, lanes] = ffn_x[blk, 0].astype(F32).T
@@ -1609,7 +1687,8 @@
         for place, target in enumerate((query_b, value_b)):
             unit = unit_sums[per_layer * layer + row // 2, pl.ds(6 + depth + place, 1)]
             target[row : row + 1] = pltpu.roll(unit, shift, 1)[:, :8]
-    vec_sums[...] = vec_in[...]
+    for place, target in enumerate(vec_rows):
+        target[...] = vec_in[pl.ds(place, 1)]
 
 
 def write_out(depth, *pieces):
@@ -1632,10 +1711,10 @@
             jax.ShapeDtypeStruct((4, 32), F32),
             head,
             head,
-            jax.ShapeDtypeStruct((16, BLK), F32),
-        ],
-        in_specs=[vmem()] * 6,
-        out_specs=[vmem()] * 12,
+        ]
+        + [jax.ShapeDtypeStruct((1, BLK), F32)] * 6,
+        in_specs=[vmem()] * 7,
+        out_specs=[vmem()] * 17,
         name="write_out",
     )(*pieces)
 
@@ -1694,8 +1773,9 @@
         up_b,
         query_b,
         value_b,
-        vec_sums,
+        *vec_rows,
     ) = write_out(depth, *pieces)
+    vec_sums = [row.reshape(BLK) for row in vec_rows]
     return (
         output,
         grad_in,

time: 221 us -> 210 us (0.950)
  Pallas kernels: 218 us -> 209 us
    pallas_call x1, Pallas kernels: 215 us -> 206 us  [layer_pass(): pl.pallas_call(functools.partial(layer_body, depth), out_shape=[rows, row...]
where the time goes in v5:
time: 210 us
  Pallas kernels  209 us (100%)
    pallas_call x1, Pallas kernels, layer_pass(): pl.pallas_call(functools.partial(layer_body, depth), out_shape=[rows, row...  206 us

profile of v5, /device:TPU:0, one launch (start us, length us, event | category | flops | bytes accessed | tf_op | source)
XLA Modules:
  0.0 209.8 jit_solution(8064167526307943280)
XLA Ops:
  0.7 205.7 %layer.1 = (bf16[2,128,1024]{2,1,0:T(8,128)(2,1)}, bf16[2,128,1024]{2,1,0:T(8,128)(2,1)}, f32[2,3,128,128]{3,2,1,0:T(8,128)}, f32[128,256]{1,0:T(8,128)}, bf16[8...) custom-call(s32[8]{0:T(128)} %lengths.1, bf16[2,128,1024]{2,1,0:T(8,128)(2,1)} %hidden.1, ...), custom_call_target="tpu_custom_call" | custom-call | tf_op jit(solution)/shard_map/layer/pallas_call | solution.py:1551
  206.4 3.2 %write_out.1 = (bf16[2,128,1024]{2,1,0:T(8,128)(2,1)}, bf16[2,128,1024]{2,1,0:T(8,128)(2,1)}, f32[128,256]{1,0:T(8,128)}, f32[128,256]{1,0:T(8,128)}, f32[128,25...) custom-call(bf16[2,128,1024]{2,1,0:T(8,128)(2,1)} %get-tuple-element, ...), custom_call_target="tpu_custom_call" | custom-call | tf_op jit(solution)/shard_map/write_out/pallas_call | solution.py:1700

commit v6 on v5

--- a/solution.py
+++ b/solution.py
@@ -435,11 +435,19 @@
             )
         self.copies = copies
 
-    def start(self):
-        for name in ("y0", "x1", "x0", "y1", "p"):
+    def start_half(self):
+        for name in ("y0", "x1"):
+            self.copies[name].start()
+
+    def start_rest(self):
+        for name in ("x0", "y1", "p"):
             self.copies[name].start()
         if self.local is not None:
             self.local.start()
+
+    def start(self):
+        self.start_half()
+        self.start_rest()
 
     def pass_on(self, arrived, sends):
         self.copies[arrived].wait_recv()
@@ -732,6 +740,16 @@
     col = (own // 2 + index // 2) % 2
     row = (own // 4 + index // 4) % 2
     return row * 4 + col * 2 + core
+
+
+def pair_of(dev):
+    col, row = (dev // 2) % 2, dev // 4
+    return 2 * ((col + row) % 2 + 2 * (dev % 2)) + row
+
+
+def dev_of(pair):
+    at, row = pair // 2, pair % 2
+    return 4 * row + 2 * ((at + row) % 2) + at // 2
 
 
 class WideExchange:
@@ -810,7 +828,7 @@
     down_t,
     up_w,
     down_w,
-    z_qkv,
+    qkv_all,
     z_vec,
     vec_wide,
     vec_line,
@@ -860,6 +878,10 @@
     onward_recv,
     dense_send,
     dense_recv,
+    head_send,
+    head_recv,
+    spread_send,
+    spread_recv,
     sum_send,
     sum_recv,
     own_sems,
@@ -919,14 +941,91 @@
 
     gains = wide_of(0, lambda dev: vec_wide, lambda dev: vec_wide_all.at[dev])
     gains.start()
+
+    mine = pair_of(own)
+    origin, piece = mine // per_layer, mine % per_layer
+    head_refs = (w_query, w_key, w_value)
+
+    def head_copies(number):
+        goal = dev_of(layer * per_layer + number)
+        copies = [
+            remote(
+                ref.at[:, pl.ds(number * BLK, BLK)],
+                qkv_all.at[kind, own],
+                head_send.at[number, kind],
+                head_recv.at[own, kind],
+                {"wide": goal},
+            )
+            for kind, ref in enumerate(head_refs)
+        ]
+        return goal, copies
+
+    def head_local(kind):
+        return pltpu.make_async_copy(
+            head_refs[kind].at[:, block_rows(piece)], qkv_all.at[kind, own], own_sems.at[2 + kind]
+        )
+
+    for number in range(per_layer):
+        goal, copies = head_copies(number)
+
+        @pl.when(goal != own)
+        def _(copies=copies):
+            for copy in copies:
+                copy.start()
+
+    @pl.when(layer == origin)
+    def _():
+        for kind in range(3):
+            head_local(kind).start()
+
+    def spread(kind, up):
+        side = 0 if up else 1
+        return remote(
+            qkv_all.at[kind],
+            qkv_all.at[kind],
+            spread_send.at[side, kind],
+            spread_recv.at[side, kind],
+            {"tp": layer + 1 if up else layer - 1},
+        )
+
+    def spread_each(kind, act):
+        @pl.when((layer >= origin) & (layer < depth - 1))
+        def _():
+            act(spread(kind, True))
+
+        @pl.when((layer <= origin) & (layer > 0))
+        def _():
+            act(spread(kind, False))
+
+    def head_pass(kind):
+        @pl.when(layer == origin)
+        def _():
+            for side in range(1, 8):
+                source = (own + side) % 8
+                remote(
+                    head_refs[kind].at[:, pl.ds(0, BLK)],
+                    qkv_all.at[kind, source],
+                    head_send.at[0, kind],
+                    head_recv.at[source, kind],
+                    {"wide": source},
+                ).wait_recv()
+            head_local(kind).wait()
+
+        @pl.when(layer > origin)
+        def _():
+            spread(kind, True).wait_recv()
+
+        @pl.when(layer < origin)
+        def _():
+            spread(kind, False).wait_recv()
+
+        spread_each(kind, lambda copy: copy.start())
+
     hid = gather_of(0, hidden, hidden_all)
     hid.start()
     line = LineGather(
         depth,
         [
-            (w_query, lambda at: z_qkv.at[at, 0]),
-            (w_key, lambda at: z_qkv.at[at, 1]),
-            (w_value, lambda at: z_qkv.at[at, 2]),
             (w_dense, lambda at: dense_all.at[own, at]),
             (vec_line, lambda at: z_vec.at[at]),
         ],
@@ -957,12 +1056,11 @@
 
         return lax.fori_loop(0, steps, norm_part, carry)
 
-    hid.arrive("p")
-    hid.local.wait()
-    lax.fori_loop(0, 2, norm_block, 0)
+    head_pass(0)
     hid.first()
     line.arrive(1)
     line.start(2)
+    head_pass(1)
     hid.second()
     ups = wide_of(
         3, lambda dev: w_up.at[:, block_rows(dev)], lambda dev: up_t.at[block_rows(dev)]
@@ -978,8 +1076,12 @@
     downs.start()
     for copy in unit_copies:
         copy.start()
+    head_pass(2)
     line.arrive(2)
     line.start(3)
+    hid.arrive("p")
+    hid.local.wait()
+    lax.fori_loop(0, 2, norm_block, 0)
     hid.arrive("px0", "px1", "py0", "py1")
     lax.fori_loop(2, 6, norm_block, 0)
     hid.third()
@@ -987,14 +1089,6 @@
     for copy in own_copies:
         copy.wait()
 
-    def goal_lanes(dev):
-        return pl.ds(pl.multiple_of((dev % per_layer) * BLK, BLK), BLK)
-
-    heads = wide_of(
-        1,
-        lambda dev: z_qkv.at[dev // per_layer, :, :, goal_lanes(dev)],
-        lambda dev: attn_in.at[dev],
-    )
     biases = wide_of(2, lambda dev: z_vec, lambda dev: vec_line_all.at[dev])
     dense = SquareGather(
         (dense_all.at[own, pl.ds(0, 2)], dense_all.at[own, pl.ds(2, 2)], dense_all.at[own]),
@@ -1004,26 +1098,18 @@
         gather_recv.at[3],
     )
     biases.start()
-    heads.start()
     dense.start()
     gd = gather_of(1, down_own, down_all)
-    own_copies = [
-        pltpu.make_async_copy(z_qkv.at[own // per_layer, :, :, goal_lanes(own)], attn_in.at[own], own_sems.at[5]),
-    ]
-    for copy in own_copies:
-        copy.start()
     vec_line_all[own] = z_vec[...]
     hid.arrive("pd0", "pd1")
     lax.fori_loop(6, 8, norm_block, 0)
     biases.arrive()
-    head_layer = own // per_layer
-    piece = own % per_layer
     unit_row = own // 2
     for dev in range(8):
         for head in range(2):
             lanes = slice(head * HEAD + dev * 8, head * HEAD + dev * 8 + 8)
             row = pl.ds(b_up.shape[0] + 2 * piece + head, 1)
-            values = vec_line_all[dev, head_layer, row]
+            values = vec_line_all[dev, origin, row]
             qkv_bias[:, lanes] = values[:, 0:8]
             lanes = slice(4 * HEAD + lanes.start, 4 * HEAD + lanes.stop)
             qkv_bias[:, lanes] = values[:, 8:16]
@@ -1032,15 +1118,13 @@
         for part in range(4):
             values = vec_line_all[4 * (own % 2) + part, up, pl.ds(unit_row, 1)]
             up_bias[:, up * BLK + part * 32 : up * BLK + part * 32 + 32] = values[:, 0:32]
-    heads.arrive()
     hid.sent()
-    for copy in own_copies + unit_copies:
+    for copy in unit_copies:
         copy.wait()
     ups.arrive()
     downs.arrive()
-    for dev in range(8):
-        for kind in range(3):
-            qkv_w[dev * BLK : (dev + 1) * BLK, kind * BLK : (kind + 1) * BLK] = attn_in[dev, kind]
+    for kind in range(3):
+        qkv_w[:, kind * BLK : (kind + 1) * BLK] = qkv_all[kind].reshape(width, BLK)
 
     ffn_line = LineGather(
         depth,
@@ -1059,7 +1143,7 @@
     for copy in unit_copies:
         copy.start()
     slopes = [
-        jnp.exp2(-0.5 * (jnp.full((1, 1), 2 * own + head, jnp.int32).astype(F32) + 1.0)) * LOG2E
+        jnp.exp2(-0.5 * (jnp.full((1, 1), 2 * mine + head, jnp.int32).astype(F32) + 1.0)) * LOG2E
         for head in range(2)
     ]
 
@@ -1067,12 +1151,12 @@
         return wide_of(
             7 + slot,
             lambda dev: attention.at[slot, block_rows(dev)],
-            lambda dev: att_own.at[slot, :, block_rows(dev)],
+            lambda dev: att_own.at[slot, :, block_rows(pair_of(dev))],
         )
 
     def att_local(slot):
         return pltpu.make_async_copy(
-            attention.at[slot, block_rows(own)], att_own.at[slot, :, block_rows(own)], own_sems.at[10 + slot]
+            attention.at[slot, block_rows(own)], att_own.at[slot, :, block_rows(mine)], own_sems.at[10 + slot]
         )
 
     def one_slot(slot, carry):
@@ -1099,13 +1183,13 @@
             ffn_line.arrive(1)
             ffn_line.start(2)
             dense.third()
-            gd.start()
+            gd.start_half()
 
         return carry
 
     lax.fori_loop(0, 2, one_slot, 0)
+    gd.start_rest()
     gd.first()
-    gd.second()
     ffn_line.arrive(2)
     ffn_line.start(3)
     dense.arrive("p", "px0", "px1", "py0", "py1", "pd0", "pd1")
@@ -1175,6 +1259,7 @@
     gather.local.wait()
     lax.fori_loop(0, 2, compute, 0)
     scatter.pairs[3].start()
+    gd.second()
     gather.first()
     gd.third()
     gather.second()
@@ -1264,13 +1349,13 @@
     def att_back(slot):
         return wide_of(
             9 + slot,
-            lambda dev: att_grad_own.at[slot, :, block_rows(dev)],
+            lambda dev: att_grad_own.at[slot, :, block_rows(pair_of(dev))],
             lambda dev: grad_att.at[slot, block_rows(dev)],
         )
 
     def att_back_local(slot):
         return pltpu.make_async_copy(
-            att_grad_own.at[slot, :, block_rows(own)], grad_att.at[slot, block_rows(own)], own_sems.at[12 + slot]
+            att_grad_own.at[slot, :, block_rows(mine)], grad_att.at[slot, block_rows(own)], own_sems.at[12 + slot]
         )
 
     for slot in range(2):
@@ -1378,24 +1463,39 @@
             attn_g[blk, kind] = weight_part[
                 kind * BLK : (kind + 1) * BLK, blk * BLK : (blk + 1) * BLK
             ]
-    exchange = wide_of(11, lambda dev: attn_g.at[dev], lambda dev: attn_in.at[dev])
-
-    def onward(index, source):
+    kinds = (pl.ds(0, 2), pl.ds(2, 1))
+    exchanges = [
+        wide_of(
+            (11, 1)[group],
+            lambda dev, kind=kind: attn_g.at[dev, kind],
+            lambda dev, kind=kind: attn_in.at[dev, kind],
+        )
+        for group, kind in enumerate(kinds)
+    ]
+
+    def onward(group, index, source):
+        pair = pair_of(index)
         return remote(
-            source.at[index],
-            attn_z.at[layer, index % per_layer],
-            onward_send.at[index],
-            onward_recv.at[layer, index % per_layer],
-            {"tp": index // per_layer},
+            source.at[index, kinds[group]],
+            attn_z.at[layer, pair % per_layer, kinds[group]],
+            onward_send.at[group, index],
+            onward_recv.at[group, layer, pair % per_layer],
+            {"tp": pair // per_layer},
         )
 
-    def forward(index, source):
-        @pl.when(index // per_layer != layer)
+    def forward(group, index, source):
+        @pl.when(pair_of(index) // per_layer != layer)
         def _():
-            onward(index, source).start()
-
-    exchange.start()
-    forward(own, attn_g)
+            onward(group, index, source).start()
+
+    def forward_all(group):
+        for number in range(1, 8):
+            exchanges[group].copies[number - 1].wait_recv()
+            forward(group, (own + 8 - number) % 8, attn_in)
+
+    exchanges[0].start()
+    for group in range(2):
+        forward(group, own, attn_g)
     share = second_share
     grad_normed = grad_second
     scatter = scatter_of(2, share, grad_normed, (a_summed, a_x, a_y))
@@ -1412,8 +1512,8 @@
         scatter.pairs[chip].start()
         if chip:
             scatter.near(chip - 1)
+    exchanges[1].start()
     line_sums(1)
-    ffn_exchange(1).start()
     head_sum = jnp.sum(grad_qkv[0].astype(F32), axis=0, keepdims=True)
     head_sum = head_sum + jnp.sum(grad_qkv[1].astype(F32), axis=0, keepdims=True)
     down.finish()
@@ -1426,11 +1526,11 @@
         return carry
 
     lax.fori_loop(0, steps, out_part, 0)
-    for number in range(1, 8):
-        exchange.copies[number - 1].wait_recv()
-        forward((own + 8 - number) % 8, attn_in)
+    forward_all(0)
     scatter.near(3)
     scatter.middle()
+    ffn_exchange(1).start()
+    forward_all(1)
     for blk in range(8):
         lanes = slice(blk * BLK, (blk + 1) * BLK)
         for place in range(4):
@@ -1472,20 +1572,21 @@
     for copy in sum_copies:
         copy.start()
     gathered[own, layer] = parts[own]
-    for up in range(1, depth):
-        source = (layer + up) % depth
-        for number in range(per_layer):
-            remote(
-                attn_in.at[number],
-                attn_z.at[source, number],
-                onward_send.at[number],
-                onward_recv.at[source, number],
-                {"tp": source},
-            ).wait_recv()
+    for group in range(2):
+        for up in range(1, depth):
+            source = (layer + up) % depth
+            for number in range(per_layer):
+                remote(
+                    attn_in.at[number, kinds[group]],
+                    attn_z.at[source, number, kinds[group]],
+                    onward_send.at[group, number],
+                    onward_recv.at[group, source, number],
+                    {"tp": source},
+                ).wait_recv()
     attn_in[own] = attn_g[own]
     for number in range(per_layer):
         for kind in range(3):
-            total = attn_in[layer * per_layer + number, kind].astype(F32)
+            total = attn_in[dev_of(layer * per_layer + number), kind].astype(F32)
             for up in range(1, depth):
                 total = total + attn_z[(layer + up) % depth, number, kind].astype(F32)
             attn_sum[number, kind] = total
@@ -1516,8 +1617,18 @@
         att_exchange(slot).sent()
         att_back(slot).sent()
         ffn_exchange(slot).sent()
-    for sends in (gains, biases, heads, ups, downs, exchange):
+    for sends in (gains, biases, ups, downs) + tuple(exchanges):
         sends.sent()
+    for number in range(per_layer):
+        goal, copies = head_copies(number)
+
+        @pl.when(goal != own)
+        def _(copies=copies):
+            for copy in copies:
+                copy.wait_send()
+
+    for kind in range(3):
+        spread_each(kind, lambda copy: copy.wait_send())
     for number in range(1, depth):
         line.sent(number)
         ffn_line.sent(number)
@@ -1528,11 +1639,12 @@
         copy.wait_send()
     gd.sent()
     dense.sent()
-    for index in range(8):
-
-        @pl.when(index // per_layer != layer)
-        def _(index=index):
-            onward(index, attn_in).wait_send()
+    for group in range(2):
+        for index in range(8):
+
+            @pl.when(pair_of(index) // per_layer != layer)
+            def _(index=index, group=group):
+                onward(group, index, attn_in).wait_send()
 
 
 def layer_pass(depth, lengths, hidden, cotangent, *weights):
@@ -1580,7 +1692,7 @@
             pltpu.VMEM((BLK, width), BF),
             pltpu.VMEM((width, units), BF),
             pltpu.VMEM((units, width), BF),
-            pltpu.VMEM((depth, 3, BLK, per_layer * BLK), BF),
+            pltpu.VMEM((3, 8, BLK, BLK), BF),
             pltpu.VMEM((depth,) + line_vec, F32),
             pltpu.VMEM((8, BLK), F32),
             pltpu.VMEM(line_vec, F32),
@@ -1620,18 +1732,22 @@
             dma((4,)),
             dma((4, SquareScatter.SENDS)),
             dma((4, SquareScatter.SENDS)),
-            dma((2, 5, depth - 1)),
-            dma((2, 5, depth - 1)),
+            dma((2, 2, depth - 1)),
+            dma((2, 2, depth - 1)),
             dma((2, 2, depth - 1)),
             dma((2, 2, depth - 1)),
             dma((12, 7)),
             dma((12, 7)),
             dma((2, depth - 1)),
             dma((2, depth - 1)),
-            dma((8,)),
-            dma((depth, per_layer)),
+            dma((2, 8)),
+            dma((2, depth, per_layer)),
             dma((depth - 1,)),
             dma((depth - 1,)),
+            dma((per_layer, 3)),
+            dma((8, 3)),
+            dma((2, 3)),
+            dma((2, 3)),
             dma((peers,)),
             dma((peers,)),
             dma((14,)),
@@ -1685,7 +1801,7 @@
         up_b[row : row + 1] = moved[:, :32]
         shift = (BLK - ((row % 2) * HEAD + 8 * own)) % BLK
         for place, target in enumerate((query_b, value_b)):
-            unit = unit_sums[per_layer * layer + row // 2, pl.ds(6 + depth + place, 1)]
+            unit = unit_sums[dev_of(per_layer * layer + row // 2), pl.ds(6 + depth + place, 1)]
             target[row : row + 1] = pltpu.roll(unit, shift, 1)[:, :8]
     for place, target in enumerate(vec_rows):
         target[...] = vec_in[pl.ds(place, 1)]

time: 210 us -> 213 us (1.014)
  Pallas kernels: 209 us -> 212 us
    pallas_call x1, Pallas kernels: 206 us -> 209 us  [layer_pass(): pl.pallas_call(functools.partial(layer_body, depth), out_shape=[rows, row...]
where the time goes in v6:
time: 213 us
  Pallas kernels  212 us (100%)
    pallas_call x1, Pallas kernels, layer_pass(): pl.pallas_call(functools.partial(layer_body, depth), out_shape=[rows, row...  209 us

profile of v6, /device:TPU:0, one launch (start us, length us, event | category | flops | bytes accessed | tf_op | source)
XLA Modules:
  0.0 213.1 jit_solution(7982564275314080332)
XLA Ops:
  0.7 209.1 %layer.1 = (bf16[2,128,1024]{2,1,0:T(8,128)(2,1)}, bf16[2,128,1024]{2,1,0:T(8,128)(2,1)}, f32[2,3,128,128]{3,2,1,0:T(8,128)}, f32[128,256]{1,0:T(8,128)}, bf16[8...) custom-call(s32[8]{0:T(128)} %lengths.1, bf16[2,128,1024]{2,1,0:T(8,128)(2,1)} %hidden.1, ...), custom_call_target="tpu_custom_call" | custom-call | tf_op jit(solution)/shard_map/layer/pallas_call | solution.py:1663
  209.7 3.2 %write_out.1 = (bf16[2,128,1024]{2,1,0:T(8,128)(2,1)}, bf16[2,128,1024]{2,1,0:T(8,128)(2,1)}, f32[128,256]{1,0:T(8,128)}, f32[128,256]{1,0:T(8,128)}, f32[128,25...) custom-call(bf16[2,128,1024]{2,1,0:T(8,128)(2,1)} %get-tuple-element, ...), custom_call_target="tpu_custom_call" | custom-call | tf_op jit(solution)/shard_map/write_out/pallas_call | solution.py:1816

commit v7 on v5

--- a/solution.py
+++ b/solution.py
@@ -836,6 +836,7 @@
     dense_out,
     dense_in,
     parts,
+    parts_bf,
     gathered,
     a_summed,
     a_x,
@@ -860,8 +861,6 @@
     onward_recv,
     dense_send,
     dense_recv,
-    sum_send,
-    sum_recv,
     own_sems,
 ):
     own = lax.axis_index("wide")
@@ -1000,8 +999,8 @@
         (dense_all.at[own, pl.ds(0, 2)], dense_all.at[own, pl.ds(2, 2)], dense_all.at[own]),
         lambda half, dev: dense_all.at[dev, pl.ds(2 * half, 2)],
         lambda dev: dense_all.at[dev],
-        gather_send.at[3],
-        gather_recv.at[3],
+        gather_send.at[2],
+        gather_recv.at[2],
     )
     biases.start()
     heads.start()
@@ -1065,7 +1064,7 @@
 
     def att_exchange(slot):
         return wide_of(
-            7 + slot,
+            5 + slot,
             lambda dev: attention.at[slot, block_rows(dev)],
             lambda dev: att_own.at[slot, :, block_rows(dev)],
         )
@@ -1143,7 +1142,7 @@
 
     lax.fori_loop(0, steps, second_part, 0)
     second_all = hidden_all
-    gather = gather_of(2, own_rows, second_all)
+    gather = gather_of(0, own_rows, second_all)
     gather.start()
     scatter = scatter_of(0, second_share, grad_second, (a_summed, a_x, a_y))
     gd.arrive("p")
@@ -1263,7 +1262,7 @@
 
     def att_back(slot):
         return wide_of(
-            9 + slot,
+            5 + slot,
             lambda dev: att_grad_own.at[slot, :, block_rows(dev)],
             lambda dev: grad_att.at[slot, block_rows(dev)],
         )
@@ -1273,6 +1272,9 @@
             att_grad_own.at[slot, :, block_rows(own)], grad_att.at[slot, block_rows(own)], own_sems.at[12 + slot]
         )
 
+    for sends in (gains, biases, heads, ups, downs, att_exchange(0), att_exchange(1)):
+        sends.sent()
+    dense.sent()
     for slot in range(2):
         att_back(slot).start()
         att_back_local(slot).start()
@@ -1296,8 +1298,8 @@
         lambda chip, half: second_all.at[half, pl.ds(chip * BLK, BLK), sum_lanes],
         lambda place: second_all.at[0, pl.ds((4 + place) * BLK, BLK), sum_lanes],
         lambda place: second_all.at[1, pl.ds((4 + place) * BLK, BLK), sum_lanes],
-        scatter_send.at[3],
-        scatter_recv.at[3],
+        scatter_send.at[2],
+        scatter_recv.at[2],
     )
 
     def dense_piece(at):
@@ -1324,7 +1326,7 @@
         dense_back.near(chip)
 
     def ffn_exchange(kind):
-        return wide_of(5 + kind, lambda dev: ffn_sum.at[dev, kind], lambda dev: ffn_x.at[dev, kind])
+        return wide_of(kind, lambda dev: ffn_sum.at[dev, kind], lambda dev: ffn_x.at[dev, kind])
 
     def slot_back(slot, carry):
         def one_head(head):
@@ -1378,27 +1380,42 @@
             attn_g[blk, kind] = weight_part[
                 kind * BLK : (kind + 1) * BLK, blk * BLK : (blk + 1) * BLK
             ]
-    exchange = wide_of(11, lambda dev: attn_g.at[dev], lambda dev: attn_in.at[dev])
-
-    def onward(index, source):
+    kinds = (pl.ds(0, 2), pl.ds(2, 1))
+    exchanges = [
+        wide_of(
+            2 + group,
+            lambda dev, kind=kind: attn_g.at[dev, kind],
+            lambda dev, kind=kind: attn_in.at[dev, kind],
+        )
+        for group, kind in enumerate(kinds)
+    ]
+
+    def onward(group, index, source):
+        pair = index
         return remote(
-            source.at[index],
-            attn_z.at[layer, index % per_layer],
-            onward_send.at[index],
-            onward_recv.at[layer, index % per_layer],
-            {"tp": index // per_layer},
+            source.at[index, kinds[group]],
+            attn_z.at[layer, pair % per_layer, kinds[group]],
+            onward_send.at[group, index],
+            onward_recv.at[group, layer, pair % per_layer],
+            {"tp": pair // per_layer},
         )
 
-    def forward(index, source):
+    def forward(group, index, source):
         @pl.when(index // per_layer != layer)
         def _():
-            onward(index, source).start()
-
-    exchange.start()
-    forward(own, attn_g)
+            onward(group, index, source).start()
+
+    def forward_all(group):
+        for number in range(1, 8):
+            exchanges[group].copies[number - 1].wait_recv()
+            forward(group, (own + 8 - number) % 8, attn_in)
+
+    exchanges[0].start()
+    for group in range(2):
+        forward(group, own, attn_g)
     share = second_share
     grad_normed = grad_second
-    scatter = scatter_of(2, share, grad_normed, (a_summed, a_x, a_y))
+    scatter = scatter_of(0, share, grad_normed, (a_summed, a_x, a_y))
 
     def normed_block(index, carry):
         rows = pl.ds(pl.multiple_of(relation(index) * BLK, BLK), BLK)
@@ -1412,8 +1429,8 @@
         scatter.pairs[chip].start()
         if chip:
             scatter.near(chip - 1)
+    exchanges[1].start()
     line_sums(1)
-    ffn_exchange(1).start()
     head_sum = jnp.sum(grad_qkv[0].astype(F32), axis=0, keepdims=True)
     head_sum = head_sum + jnp.sum(grad_qkv[1].astype(F32), axis=0, keepdims=True)
     down.finish()
@@ -1426,11 +1443,11 @@
         return carry
 
     lax.fori_loop(0, steps, out_part, 0)
-    for number in range(1, 8):
-        exchange.copies[number - 1].wait_recv()
-        forward((own + 8 - number) % 8, attn_in)
+    forward_all(0)
     scatter.near(3)
     scatter.middle()
+    ffn_exchange(1).start()
+    forward_all(1)
     for blk in range(8):
         lanes = slice(blk * BLK, (blk + 1) * BLK)
         for place in range(4):
@@ -1459,29 +1476,38 @@
         lanes = slice(blk * BLK, (blk + 1) * BLK)
         parts[blk, pl.ds(0, 1)] = gain_sum[:, lanes]
         parts[blk, pl.ds(1, 1)] = shift_sum[:, lanes]
+    gd.sent()
+
+    def sum_sems(index):
+        if index < 7:
+            return wide_send.at[4, index], wide_recv.at[4, index]
+        number, place = 2 - (index - 7) // SquareGather.SENDS, (index - 7) % SquareGather.SENDS
+        return gather_send.at[number, place], gather_recv.at[number, place]
+
+    parts_bf[...] = parts[...].astype(BF)
     sum_copies = [
         remote(
-            parts.at[wide],
+            parts_bf.at[wide],
             gathered.at[own, layer],
-            sum_send.at[index],
-            sum_recv.at[index],
+            *sum_sems(index),
             {"wide": wide, "tp": tp},
         )
         for index, (wide, tp) in enumerate(others)
     ]
     for copy in sum_copies:
         copy.start()
-    gathered[own, layer] = parts[own]
-    for up in range(1, depth):
-        source = (layer + up) % depth
-        for number in range(per_layer):
-            remote(
-                attn_in.at[number],
-                attn_z.at[source, number],
-                onward_send.at[number],
-                onward_recv.at[source, number],
-                {"tp": source},
-            ).wait_recv()
+    gathered[own, layer] = parts_bf[own]
+    for group in range(2):
+        for up in range(1, depth):
+            source = (layer + up) % depth
+            for number in range(per_layer):
+                remote(
+                    attn_in.at[number, kinds[group]],
+                    attn_z.at[source, number, kinds[group]],
+                    onward_send.at[group, number],
+                    onward_recv.at[group, source, number],
+                    {"tp": source},
+                ).wait_recv()
     attn_in[own] = attn_g[own]
     for number in range(per_layer):
         for kind in range(3):
@@ -1502,9 +1528,9 @@
         copy.wait_recv()
 
     def unit_part(dev, carry):
-        total = gathered[dev, 0]
+        total = gathered[dev, 0].astype(F32)
         for up in range(1, depth):
-            total = total + gathered[dev, up]
+            total = total + gathered[dev, up].astype(F32)
         unit_sums[dev] = total
         return carry + total
 
@@ -1513,10 +1539,9 @@
     for copy in sum_copies:
         copy.wait_send()
     for slot in range(2):
-        att_exchange(slot).sent()
         att_back(slot).sent()
         ffn_exchange(slot).sent()
-    for sends in (gains, biases, heads, ups, downs, exchange):
+    for sends in exchanges:
         sends.sent()
     for number in range(1, depth):
         line.sent(number)
@@ -1526,13 +1551,12 @@
             copy.wait_send()
     for copy in dense_copies():
         copy.wait_send()
-    gd.sent()
-    dense.sent()
-    for index in range(8):
-
-        @pl.when(index // per_layer != layer)
-        def _(index=index):
-            onward(index, attn_in).wait_send()
+    for group in range(2):
+        for index in range(8):
+
+            @pl.when(index // per_layer != layer)
+            def _(index=index, group=group):
+                onward(group, index, attn_in).wait_send()
 
 
 def layer_pass(depth, lengths, hidden, cotangent, *weights):
@@ -1545,7 +1569,6 @@
     own_f32 = pltpu.VMEM((2, BLK, width), F32)
     own_bf = pltpu.VMEM((2, BLK, width), BF)
     line_vec = (8, BLK)
-    peers = 8 * depth - 1
     vectors = [part.reshape(1, BLK) for part in weights[6:12]]
     operands = (hidden, cotangent) + weights[:6] + tuple(vectors) + weights[12:]
     return pl.pallas_call(
@@ -1606,7 +1629,8 @@
             pltpu.VMEM((2, BLK, width // 2), BF),
             pltpu.VMEM((depth - 1, BLK, per_layer * BLK), BF),
             pltpu.VMEM((8, 16, BLK), F32),
-            pltpu.VMEM((8, depth, 16, BLK), F32),
+            pltpu.VMEM((8, 16, BLK), BF),
+            pltpu.VMEM((8, depth, 16, BLK), BF),
         ]
         + [
             pltpu.VMEM((4, 2, BLK, width), BF),
@@ -1615,25 +1639,23 @@
         ]
         * 2
         + [
-            dma((4, SquareGather.SENDS)),
-            dma((4, SquareGather.SENDS)),
-            dma((4,)),
-            dma((4, SquareScatter.SENDS)),
-            dma((4, SquareScatter.SENDS)),
+            dma((3, SquareGather.SENDS)),
+            dma((3, SquareGather.SENDS)),
+            dma((2,)),
+            dma((3, SquareScatter.SENDS)),
+            dma((3, SquareScatter.SENDS)),
             dma((2, 5, depth - 1)),
             dma((2, 5, depth - 1)),
             dma((2, 2, depth - 1)),
             dma((2, 2, depth - 1)),
-            dma((12, 7)),
-            dma((12, 7)),
+            dma((7, 7)),
+            dma((7, 7)),
             dma((2, depth - 1)),
             dma((2, depth - 1)),
-            dma((8,)),
-            dma((depth, per_layer)),
+            dma((2, 8)),
+            dma((2, depth, per_layer)),
             dma((depth - 1,)),
             dma((depth - 1,)),
-            dma((peers,)),
-            dma((peers,)),
             dma((14,)),
         ],
         compiler_params=pltpu.CompilerParams(

time: 210 us -> 205 us (0.976)
  Pallas kernels: 209 us -> 204 us
    pallas_call x1, Pallas kernels: 206 us -> 201 us  [layer_pass(): pl.pallas_call(functools.partial(layer_body, depth), out_shape=[rows, row...]
where the time goes in v7:
time: 205 us
  Pallas kernels  204 us (100%)
    pallas_call x1, Pallas kernels, layer_pass(): pl.pallas_call(functools.partial(layer_body, depth), out_shape=[rows, row...  201 us

profile of v7, /device:TPU:0, one launch (start us, length us, event | category | flops | bytes accessed | tf_op | source)
XLA Modules:
  0.0 204.8 jit_solution(14498181546139726622)
XLA Ops:
  0.7 200.7 %layer.1 = (bf16[2,128,1024]{2,1,0:T(8,128)(2,1)}, bf16[2,128,1024]{2,1,0:T(8,128)(2,1)}, f32[2,3,128,128]{3,2,1,0:T(8,128)}, f32[128,256]{1,0:T(8,128)}, bf16[8...) custom-call(s32[8]{0:T(128)} %lengths.1, bf16[2,128,1024]{2,1,0:T(8,128)(2,1)} %hidden.1, ...), custom_call_target="tpu_custom_call" | custom-call | tf_op jit(solution)/shard_map/layer/pallas_call | solution.py:1574
  201.4 3.2 %write_out.1 = (bf16[2,128,1024]{2,1,0:T(8,128)(2,1)}, bf16[2,128,1024]{2,1,0:T(8,128)(2,1)}, f32[128,256]{1,0:T(8,128)}, f32[128,256]{1,0:T(8,128)}, f32[128,25...) custom-call(bf16[2,128,1024]{2,1,0:T(8,128)(2,1)} %get-tuple-element, ...), custom_call_target="tpu_custom_call" | custom-call | tf_op jit(solution)/shard_map/write_out/pallas_call | solution.py:1722

commit v8 on v7

--- a/solution.py
+++ b/solution.py
@@ -1006,6 +1006,7 @@
     heads.start()
     dense.start()
     gd = gather_of(1, down_own, down_all)
+    gd.start()
     own_copies = [
         pltpu.make_async_copy(z_qkv.at[own // per_layer, :, :, goal_lanes(own)], attn_in.at[own], own_sems.at[5]),
     ]
@@ -1082,13 +1083,17 @@
 
         lax.fori_loop(0, 8 * BLK // QB, block, 0)
         length = lengths[layer * 2 + slot]
-        attend_head(slot, 0, length, slopes, qkv, attention, totals, bias)
-
         @pl.when(slot == 0)
         def _():
             dense.first()
             dense.second()
 
+        attend_head(slot, 0, length, slopes, qkv, attention, totals, bias)
+
+        @pl.when(slot == 0)
+        def _():
+            dense.third()
+
         attend_head(slot, 1, length, slopes, qkv, attention, totals, bias)
         att_exchange(slot).start()
         att_local(slot).start()
@@ -1097,8 +1102,6 @@
         def _():
             ffn_line.arrive(1)
             ffn_line.start(2)
-            dense.third()
-            gd.start()
 
         return carry
 

time: 205 us -> 206 us (level)
  no operation moved by 1% of the time
where the time goes in v8:
time: 206 us
  Pallas kernels  205 us (100%)
    pallas_call x1, Pallas kernels, layer_pass(): pl.pallas_call(functools.partial(layer_body, depth), out_shape=[rows, row...  202 us

profile of v8, /device:TPU:0, one launch (start us, length us, event | category | flops | bytes accessed | tf_op | source)
XLA Modules:
  0.0 206.2 jit_solution(16649557784428366655)
XLA Ops:
  0.7 202.1 %layer.1 = (bf16[2,128,1024]{2,1,0:T(8,128)(2,1)}, bf16[2,128,1024]{2,1,0:T(8,128)(2,1)}, f32[2,3,128,128]{3,2,1,0:T(8,128)}, f32[128,256]{1,0:T(8,128)}, bf16[8...) custom-call(s32[8]{0:T(128)} %lengths.1, bf16[2,128,1024]{2,1,0:T(8,128)(2,1)} %hidden.1, ...), custom_call_target="tpu_custom_call" | custom-call | tf_op jit(solution)/shard_map/layer/pallas_call | solution.py:1577
  202.8 3.2 %write_out.1 = (bf16[2,128,1024]{2,1,0:T(8,128)(2,1)}, bf16[2,128,1024]{2,1,0:T(8,128)(2,1)}, f32[128,256]{1,0:T(8,128)}, f32[128,256]{1,0:T(8,128)}, f32[128,25...) custom-call(bf16[2,128,1024]{2,1,0:T(8,128)(2,1)} %get-tuple-element, ...), custom_call_target="tpu_custom_call" | custom-call | tf_op jit(solution)/shard_map/write_out/pallas_call | solution.py:1725
